TPU v7x, 256 devices: a whole 4x4x8 slice. The times are simulated.
256 devices in a mesh: dp: 16 (over y, x_hi, core), expert: 16 (over z, x_lo).
Axes of the slice: x: 4 (x_hi: 2, x_lo: 2; x = x_hi * 2 + x_lo), y: 4, z: 8, core: 2. Of those that a mesh axis runs over, the one named last changes fastest.
Arguments:
- tokens: bfloat16 [32768, 2048], P(('dp', 'expert')), may hold values from -6 to 6
- routes: int32 [32768, 2], P(('dp', 'expert')), may hold values from 0 to 15, as said below
- grad_hidden: bfloat16 [32768, 2, 768], P(('dp', 'expert')), may hold values from -1.1953125 to 1.1953125
- w_gate: bfloat16 [16, 2048, 768], P('expert'), may hold values from -0.125 to 0.125
- w_up: bfloat16 [16, 2048, 768], P('expert'), may hold values from -0.125 to 0.125
Outputs:
- grad_tokens: bfloat16 [32768, 2048], P(('dp', 'expert'))
- grad_gate: float32 [16, 2048, 768], P('expert', 'dp')
- grad_up: float32 [16, 2048, 768], P('expert', 'dp')
Inputs may be any that keep to these rules, and one draw needn't show every extreme that they name: `routes`: each row names 2 different experts. In each data group 2 experts are hot, the same for all rows of the group: in the rows of one device each hot expert of its group is named more often than every other expert and at most 46 times, every other expert at most 16 times. In the rows of every device some expert is named exactly 16 times; in the rows of some device a hot expert is named exactly 46 times. Every expert is hot in some data group. The indices of a group's two hot experts never differ by 8.
All inputs are finite; a program needn't handle non-finite values.
Results may differ from a plain program's by a relative error of at most 0.012.
Values may be sent and summed in bfloat16 or wider, within the bound.
No kernel may reach another device: no remote copies, remote signals or barrier semaphores. Data moves between devices by JAX's collectives and lax.ppermute only.
A program may use at most 128 MiB of HBM per device.

v0:
```python
import jax
import jax.numpy as jnp
from jax import lax
from jax.sharding import PartitionSpec as P


def in_one_piece(arrays, axis, dim, along):
    both = jnp.concatenate(arrays, axis=along)
    whole, at, finished = (lax.psum_scatter(both, axis, scatter_dimension=dim, tiled=True), 0, [])
    for a in arrays:
        finished.append(lax.slice_in_dim(whole, at, at + a.shape[along], axis=along))
        at += a.shape[along]
    return tuple(finished)


def expert_grads(rows_x, rows_dh, gate_w, up_w):
    gate_act = jnp.dot(rows_x, gate_w, preferred_element_type=jnp.float32)
    up_act = jnp.dot(rows_x, up_w, preferred_element_type=jnp.float32)
    gate_sig = jax.nn.sigmoid(gate_act)
    grad_wide = rows_dh.astype(jnp.float32)
    gate_delta = (grad_wide * up_act * gate_sig * (1.0 + gate_act * (1.0 - gate_sig))).astype(
        jnp.bfloat16
    )
    up_delta = (grad_wide * gate_act * gate_sig).astype(jnp.bfloat16)
    back_rows = lax.dot_general(
        gate_delta, gate_w, (((1,), (1,)), ((), ())), preferred_element_type=jnp.float32
    )
    back_rows = back_rows + lax.dot_general(
        up_delta, up_w, (((1,), (1,)), ((), ())), preferred_element_type=jnp.float32
    )
    gate_grad = lax.dot_general(
        rows_x, gate_delta, (((0,), (0,)), ((), ())), preferred_element_type=jnp.float32
    )
    up_grad = lax.dot_general(
        rows_x, up_delta, (((0,), (0,)), ((), ())), preferred_element_type=jnp.float32
    )
    return (back_rows.astype(jnp.bfloat16), gate_grad, up_grad)


def tile_grads(got_rows, got_grads, begin, finish, gate_w, up_w):
    groups = got_rows.shape[0]
    width = finish - begin
    rows_x = got_rows[:, begin:finish].reshape(groups * width, got_rows.shape[2])
    rows_dh = got_grads[:, begin:finish].reshape(groups * width, got_grads.shape[2])
    back_rows, gate_grad, up_grad = expert_grads(rows_x, rows_dh, gate_w, up_w)
    return (back_rows.reshape(groups, width, got_rows.shape[2]), gate_grad, up_grad)


def per_device(tokens, routes, grad_hidden, w_gate, w_up):
    tok_rows, features = tokens.shape
    per_token = routes.shape[1]
    hidden = w_gate.shape[2]
    groups = lax.axis_size("expert")
    pair_count = tok_rows * per_token
    cold_most = per_token * tok_rows // groups
    cold_floor = cold_most - 2 - cold_most // 8
    hot_total = pair_count - (groups - 3) * cold_floor - cold_most
    hot_most = (hot_total + 1) // 2 + min((hot_total - 2 * cold_most - 2) // 2, cold_most // 4)
    chosen = routes.reshape(pair_count)
    expert_ids = jnp.arange(groups, dtype=jnp.int32)
    member = (chosen[:, None] == expert_ids[None, :]).astype(jnp.int32)
    ranked = jnp.sum(jnp.cumsum(member, axis=0) * member, axis=1) - 1
    own_gate = w_gate[0]
    own_up = w_up[0]
    second_part = (hot_most - cold_most + 1) // 2
    limit = cold_most + second_part
    position = chosen * hot_most + ranked
    send_rows = (
        jnp.zeros((groups * hot_most, features), jnp.bfloat16)
        .at[position]
        .set(jnp.repeat(tokens, per_token, axis=0))
    )
    send_grads = (
        jnp.zeros((groups * hot_most, hidden), jnp.bfloat16)
        .at[position]
        .set(grad_hidden.reshape(pair_count, hidden))
    )
    got_rows, got_grads = (
        lax.all_to_all(
            send_rows.reshape(groups, hot_most, features),
            "expert",
            split_axis=0,
            concat_axis=0,
            tiled=True,
        ),
        lax.all_to_all(
            send_grads.reshape(groups, hot_most, hidden),
            "expert",
            split_axis=0,
            concat_axis=0,
            tiled=True,
        ),
    )
    head_back, main_gate, main_up = tile_grads(got_rows, got_grads, 0, limit, own_gate, own_up)
    tail_back, extra_gate, extra_up = tile_grads(
        got_rows, got_grads, limit, hot_most, own_gate, own_up
    )
    back_tiles = jnp.concatenate([head_back, tail_back], axis=1)
    returned = lax.all_to_all(back_tiles, "expert", split_axis=0, concat_axis=0, tiled=True)
    pair_back = returned.reshape(groups * hot_most, features)[position]
    grad_tokens = jnp.sum(
        pair_back.reshape(tok_rows, per_token, features).astype(jnp.float32), axis=1
    ).astype(jnp.bfloat16)
    kept_gate, spill_gate, kept_up, spill_up = tuple(
        (
            part.astype(jnp.float32)
            for part in in_one_piece(
                (
                    main_gate.astype(jnp.bfloat16),
                    extra_gate.astype(jnp.bfloat16),
                    main_up.astype(jnp.bfloat16),
                    extra_up.astype(jnp.bfloat16),
                ),
                "dp",
                0,
                1,
            )
        )
    )
    gate_part = kept_gate + spill_gate
    up_part = kept_up + spill_up
    return (grad_tokens, gate_part[None], up_part[None])


def solution(mesh):
    placed = (
        P(("dp", "expert"), None),
        P(("dp", "expert"), None),
        P(("dp", "expert"), None, None),
        P("expert", None, None),
        P("expert", None, None),
    )
    return jax.shard_map(
        per_device,
        mesh=mesh,
        in_specs=placed,
        out_specs=(P(("dp", "expert"), None), P("expert", "dp", None), P("expert", "dp", None)),
        check_vma=False,
    )
```

profile of v0, /device:TPU:14, one launch (start us, length us, event | category | flops | bytes accessed | tf_op | source)
XLA Modules:
  0.0 369.4 jit_solution(1344470280549742219)
XLA Ops:
  11.6 2.7 scatter_custom_fusion
  14.2 2.2 reshape.95
  16.5 9.9 %all-to-all-start = ((bf16[16,46,768]{2,1,0:T(8,128)(2,1)}), bf16[16,46,768]{2,1,0:T(8,128)(2,1)}, u32[]{:S(2)}, u32[]{:S(2)}) async-start(bf16[16,46,768]{2,1,0:T(8,128)(2,1)} %reshape.95), calls=%async_computation | async-start | bytes 2359296 | tf_op jit(solution)/shard_map/all_to_all | solution.py:86
  26.4 2.6 broadcast_in_dim.21
  29.0 2.2 reshape.126
  31.3 4.9 %scatter_custom_fusion.1 = bf16[736,2048]{1,0:T(8,128)(2,1)} fusion(s32[256]{0:T(256)S(1)} %bitcast.77, bf16[256,2048]{1,0:T(8,128)(2,1)} %reshape.126, bf16[]{:T(256)} %constant.6.clone.1), kind=kCustom, calls=%fused_computation.31 | custom fusion | bytes 3015168 | tf_op jit(solution)/shard_map/scatter | solution.py:71
  36.2 4.5 %reshape.97 = bf16[16,46,2048]{2,1,0:T(8,128)(2,1)} reshape(bf16[736,2048]{1,0:T(8,128)(2,1)} %scatter_custom_fusion.1) | data formatting | bytes 6029312 | tf_op jit(solution)/shard_map/reshape | solution.py:80
  40.7 16.0 %all-to-all-done = bf16[16,46,768]{2,1,0:T(8,128)(2,1)} async-done(((bf16[16,46,768]{2,1,0:T(8,128)(2,1)}), bf16[16,46,768]{2,1,0:T(8,128)(2,1)}, u32[]{:S(2)}, u32[]{:S(2)}) %all-to-all-start) | async-done | bytes 1130528 | tf_op jit(solution)/shard_map/all_to_all | solution.py:86
  56.7 5.5 %all-to-all-start.1 = ((bf16[16,46,2048]{2,1,0:T(8,128)(2,1)}), bf16[16,46,2048]{2,1,0:T(8,128)(2,1)}, u32[]{:S(2)}, u32[]{:S(2)}) async-start(bf16[16,46,2048]{2,1,0:T(8,128)(2,1)} %reshape.97), calls=%async_computation.1 | async-start | bytes 6291456 | tf_op jit(solution)/shard_map/all_to_all | solution.py:79
  64.3 2.1 reshape.105
  66.4 2.4 slice_convert_fusion
  68.9 2.8 reshape.104
  71.7 60.9 %all-to-all-done.1 = bf16[16,46,2048]{2,1,0:T(8,128)(2,1)} async-done(((bf16[16,46,2048]{2,1,0:T(8,128)(2,1)}), bf16[16,46,2048]{2,1,0:T(8,128)(2,1)}, u32[]{:S(2)}, u32[]{:S(2)}) %all-to-all-start.1) | async-done | bytes 3014688 | tf_op jit(solution)/shard_map/all_to_all | solution.py:79
  132.6 2.8 slice.46
  135.4 2.5 reshape.100
  137.9 3.2 slice.44
  141.1 2.9 reshape.98
  144.0 2.6 multiply_convert_fusion.2
  158.8 27.3 %pad_maximum_fusion = bf16[2048,3072]{0,1:T(8,128)(2,1)} fusion(bf16[2048,768]{0,1:T(8,128)(2,1)S(1)} %convolution_convert_fusion.2, bf16[2048,768]{0,1:T(8,128)(2,1)S(1)} %convolution_convert_fusion, bf16[2048,768]{0,1:T(8,128)(2,1)S(1)} %convolution_convert_fusion.3, bf16[2048,768]{0,1:T(8,128)(2,1)S(1)} %convolution_convert_fusion.1), kind=kLoop, calls=%fused_computation.3 | loop fusion | flops 50331648 | bytes 25165824 | tf_op jit(solution)/shard_map/concatenate | solution.py:8
  186.1 16.6 %copy.22 = bf16[2048,3072]{1,0:T(8,128)(2,1)} copy(bf16[2048,3072]{0,1:T(8,128)(2,1)} %pad_maximum_fusion) | data formatting | bytes 25165824
  206.7 2.5 reshape.101
  209.2 3.0 fusion.4
  212.3 3.1 add_convert_fusion
  215.4 3.1 reshape.99
  218.5 4.7 %pad_maximum_fusion.1 = bf16[16,46,2048]{2,1,0:T(8,128)(2,1)} fusion(bf16[16,15,2048]{2,1,0:T(8,128)(2,1)} %reshape.101, bf16[16,31,2048]{2,1,0:T(8,128)(2,1)} %reshape.99), kind=kLoop, calls=%fused_computation.9 | loop fusion | flops 6029312 | bytes 6029312 | tf_op jit(solution)/shard_map/concatenate | solution.py:98
  223.2 5.8 %all-to-all-start.2 = ((bf16[16,46,2048]{2,1,0:T(8,128)(2,1)}), bf16[16,46,2048]{2,1,0:T(8,128)(2,1)}, u32[]{:S(2)}, u32[]{:S(2)}) async-start(bf16[16,46,2048]{2,1,0:T(8,128)(2,1)} %pad_maximum_fusion.1), calls=%async_computation.2 | async-start | bytes 6291456 | tf_op jit(solution)/shard_map/all_to_all | solution.py:99
  229.0 71.0 %all-to-all-done.2 = bf16[16,46,2048]{2,1,0:T(8,128)(2,1)} async-done(((bf16[16,46,2048]{2,1,0:T(8,128)(2,1)}), bf16[16,46,2048]{2,1,0:T(8,128)(2,1)}, u32[]{:S(2)}, u32[]{:S(2)}) %all-to-all-start.2) | async-done | bytes 3014688 | tf_op jit(solution)/shard_map/all_to_all | solution.py:99
  300.1 4.5 %reshape.102 = bf16[736,2048]{1,0:T(8,128)(2,1)} reshape(bf16[16,46,2048]{2,1,0:T(8,128)(2,1)} %all-to-all-done.2) | data formatting | bytes 6029312 | tf_op jit(solution)/shard_map/reshape | solution.py:100
  304.6 5.6 %gather_fusion = bf16[256,2048]{1,0:T(8,128)(2,1)} fusion(bf16[736,2048]{1,0:T(8,128)(2,1)} %reshape.102, s32[1024]{0:T(1024)S(1)} %pad_clamp_fusion), kind=kCustom, calls=%fused_computation | custom fusion | bytes 2098176 | tf_op jit(solution)/shard_map/gather | solution.py:100
  310.2 2.6 reshape.103
  312.7 4.6 %reduce_sum.22 = bf16[128,2048]{1,0:T(8,128)(2,1)} reduce(bf16[128,2,2048]{2,1,0:T(2,128)(2,1)} %reshape.103, bf16[]{:T(256)} %constant.6.clone.1), dimensions={1}, to_apply=%region_5.6 | reduce | flops 262144 | bytes 1572866 | tf_op jit(solution)/shard_map/reduce_sum | solution.py:101
  317.3 34.1 %reduce-scatter.4.cloned.1.call-done = bf16[128,3072]{1,0:T(8,128)(2,1)} async-done(((bf16[2048,3072]{1,0:T(8,128)(2,1)}), bf16[128,3072]{1,0:T(8,128)(2,1)}) %reduce-scatter.4.cloned.1.call-update) | async-done | bytes 786448
  (63 shorter events, 33.5 us)
Async XLA Ops:
  7.2 136.9 %copy-start = (bf16[1,2048,768]{2,1,0:T(8,128)(2,1)S(1)}, bf16[1,2048,768]{2,1,0:T(8,128)(2,1)}, u32[]{:S(2)}) copy-start(bf16[1,2048,768]{2,1,0:T(8,128)(2,1)} %param.8) | copy-start | bytes 9437188
  16.5 40.2 %all-to-all-start = ((bf16[16,46,768]{2,1,0:T(8,128)(2,1)}), bf16[16,46,768]{2,1,0:T(8,128)(2,1)}, u32[]{:S(2)}, u32[]{:S(2)}) async-start(bf16[16,46,768]{2,1,0:T(8,128)(2,1)} %reshape.95), calls=%async_computation | async-start | bytes 2359296 | tf_op jit(solution)/shard_map/all_to_all | solution.py:86
  56.7 75.9 %all-to-all-start.1 = ((bf16[16,46,2048]{2,1,0:T(8,128)(2,1)}), bf16[16,46,2048]{2,1,0:T(8,128)(2,1)}, u32[]{:S(2)}, u32[]{:S(2)}) async-start(bf16[16,46,2048]{2,1,0:T(8,128)(2,1)} %reshape.97), calls=%async_computation.1 | async-start | bytes 6291456 | tf_op jit(solution)/shard_map/all_to_all | solution.py:79
  62.2 289.2 %reduce-scatter.4.cloned.1.call-start = ((), (), s32[]{:S(2)}) async-start(), calls=%async_computation.4 | async-start | bytes 13369344
  144.0 2.6 copy-start.1
  144.0 2.7 copy-start.2
  144.0 2.9 copy-start.9
  146.6 6.3 %copy-start.7 = (bf16[240,768]{1,0:T(8,128)(2,1)}, bf16[240,768]{1,0:T(8,128)(2,1)S(1)}, u32[]{:S(2)}) copy-start(bf16[240,768]{1,0:T(8,128)(2,1)S(1)} %get-tuple-element.16) | copy-start | bytes 1105924
  146.9 1.6 copy-start.5
  146.9 2.0 copy-start.6
  150.8 3.1 copy-start.11
  152.9 4.0 %copy-start.10 = (bf16[496,768]{1,0:T(8,128)(2,1)}, bf16[496,768]{1,0:T(8,128)(2,1)S(1)}, u32[]{:S(2)}) copy-start(bf16[496,768]{1,0:T(8,128)(2,1)S(1)} %multiply_convert_fusion.1) | copy-start | bytes 2285572
  202.7 1.9 copy-start.3
  202.7 1.9 copy-start.8
  209.2 3.1 copy-start.4
  209.2 3.1 copy-start.12
  223.2 76.8 %all-to-all-start.2 = ((bf16[16,46,2048]{2,1,0:T(8,128)(2,1)}), bf16[16,46,2048]{2,1,0:T(8,128)(2,1)}, u32[]{:S(2)}, u32[]{:S(2)}) async-start(bf16[16,46,2048]{2,1,0:T(8,128)(2,1)} %pad_maximum_fusion.1), calls=%async_computation.2 | async-start | bytes 6291456 | tf_op jit(solution)/shard_map/all_to_all | solution.py:99
Sparse Core Ops, SparseCore 0:
  202.8 148.5 reduce-scatter.3
where the time goes:
time: 374 us; the launch traced here: 369 us
  waiting for transfers between devices  182 us (49%)
  local copies, waits for them, and re-layouts  84.3 us (23%)
  other arithmetic  44.8 us (12%)
  matrix products  22.6 us (6%)
  starting transfers between devices  21.3 us (6%)
  between operations  14.3 us (4%)
    all_to_all x1, waiting for transfers between devices, per_device(): lax.all_to_all(back_tiles, 'expert', split_axis=0, concat_axis=0, tiled=T...  71 us
    all_to_all x1, waiting for transfers between devices, per_device(): lax.all_to_all(send_rows.reshape(groups, hot_most, features), 'expert', s...  60.9 us
    unnamed x2, waiting for transfers between devices  34.1 us
    concatenate x1, other arithmetic, in_one_piece(): both = jnp.concatenate(arrays, axis=along)  27.3 us
    unnamed x34, local copies, waits for them, and re-layouts  26.6 us
    all_to_all x1, waiting for transfers between devices, per_device(): lax.all_to_all(send_grads.reshape(groups, hot_most, hidden), 'expert', sp...  16 us
    all_to_all x1, starting transfers between devices, per_device(): lax.all_to_all(send_grads.reshape(groups, hot_most, hidden), 'expert', sp...  9.94 us
  transfers between devices with their start and end apart: 4, of which 4 were waited for; matrix products, arithmetic and copies ran while one was open for 16% of the time, Pallas kernels for 0%

commit v1 on v0

v1 whole, which is shorter than its diff:
```python
import functools

import jax
import jax.numpy as jnp
import numpy as np
from jax import lax
from jax.experimental import pallas as pl
from jax.experimental.pallas import tpu as pltpu
from jax.sharding import PartitionSpec as P

D = 2048
FF = 768
EXPERTS = 16
CAP = 48
ROWS = EXPERTS * CAP
BLOCK = 128
FF_BLOCK = 256
MIB = 1 << 20


def pack_kernel(routes_ref, tokens_ref, grads_ref, sel_ref, out_ref):
    pairs = routes_ref.shape[1]
    toks = tokens_ref.shape[0]
    rows = out_ref.shape[0]
    routes = routes_ref[...]
    member = (routes == lax.broadcasted_iota(jnp.int32, (EXPERTS, pairs), 0)).astype(jnp.bfloat16)
    earlier = (
        lax.broadcasted_iota(jnp.int32, (pairs, pairs), 0)
        < lax.broadcasted_iota(jnp.int32, (pairs, pairs), 1)
    ).astype(jnp.bfloat16)
    before = jnp.dot(member, earlier, preferred_element_type=jnp.float32)
    rank = jnp.sum(member.astype(jnp.float32) * before, axis=0, keepdims=True).astype(jnp.int32)
    slot = routes * CAP + rank
    first = pl.program_id(0) * rows
    pick = (slot == first + lax.broadcasted_iota(jnp.int32, (rows, pairs), 0)).astype(jnp.bfloat16)
    to_token = (
        lax.broadcasted_iota(jnp.int32, (pairs, toks), 0) // 2
        == lax.broadcasted_iota(jnp.int32, (pairs, toks), 1)
    ).astype(jnp.bfloat16)
    pick_token = jnp.dot(pick, to_token, preferred_element_type=jnp.float32).astype(jnp.bfloat16)
    sel_ref[...] = pick_token
    out_ref[:, :D] = jnp.dot(
        pick_token, tokens_ref[...], preferred_element_type=jnp.float32
    ).astype(jnp.bfloat16)
    out_ref[:, D:] = jnp.dot(pick, grads_ref[...], preferred_element_type=jnp.float32).astype(
        jnp.bfloat16
    )


def pack(routes, tokens, grads):
    steps = 4
    toks, pairs = tokens.shape[0], grads.shape[0]
    return pl.pallas_call(
        pack_kernel,
        grid=(steps,),
        in_specs=[
            pl.BlockSpec((1, pairs), lambda i: (0, 0)),
            pl.BlockSpec((toks, D), lambda i: (0, 0)),
            pl.BlockSpec((pairs, FF), lambda i: (0, 0)),
        ],
        out_specs=[
            pl.BlockSpec((ROWS // steps, toks), lambda i: (i, 0)),
            pl.BlockSpec((ROWS // steps, D + FF), lambda i: (i, 0)),
        ],
        out_shape=[
            jax.ShapeDtypeStruct((ROWS, toks), jnp.bfloat16),
            jax.ShapeDtypeStruct((ROWS, D + FF), jnp.bfloat16),
        ],
        compiler_params=pltpu.CompilerParams(vmem_limit_bytes=32 * MIB),
        cost_estimate=pl.CostEstimate(flops=10**9, bytes_accessed=6 * MIB, transcendentals=0),
        name="pack",
    )(routes, tokens, grads)


def expert_kernel(x_ref, dh_ref, wg_ref, wu_ref, delta_g_ref, delta_u_ref, back_ref, acc_ref):
    j = pl.program_id(0)
    x = x_ref[...]
    wg = wg_ref[0]
    wu = wu_ref[0]
    gate = jnp.dot(x, wg, preferred_element_type=jnp.float32)
    up = jnp.dot(x, wu, preferred_element_type=jnp.float32)
    sig = jax.nn.sigmoid(gate)
    wide = dh_ref[...].astype(jnp.float32)
    delta_g = (wide * up * sig * (1.0 + gate * (1.0 - sig))).astype(jnp.bfloat16)
    delta_u = (wide * gate * sig).astype(jnp.bfloat16)
    delta_g_ref[...] = delta_g
    delta_u_ref[...] = delta_u
    dims = (((1,), (1,)), ((), ()))
    part = lax.dot_general(
        delta_g, wg, dims, preferred_element_type=jnp.float32
    ) + lax.dot_general(delta_u, wu, dims, preferred_element_type=jnp.float32)
    last = pl.num_programs(0) - 1

    @pl.when(j == 0)
    def _():
        acc_ref[...] = part

    @pl.when(jnp.logical_and(j > 0, j < last))
    def _():
        acc_ref[...] += part

    @pl.when(j == last)
    def _():
        back_ref[...] = (acc_ref[...] + part).astype(jnp.bfloat16)


def expert(got, w_gate, w_up):
    steps = FF // FF_BLOCK
    off = D // FF_BLOCK
    return pl.pallas_call(
        expert_kernel,
        grid=(steps,),
        in_specs=[
            pl.BlockSpec((ROWS, D), lambda j: (0, 0)),
            pl.BlockSpec((ROWS, FF_BLOCK), lambda j: (0, off + j)),
            pl.BlockSpec((1, D, FF_BLOCK), lambda j: (0, 0, j)),
            pl.BlockSpec((1, D, FF_BLOCK), lambda j: (0, 0, j)),
        ],
        out_specs=[
            pl.BlockSpec((ROWS, FF_BLOCK), lambda j: (0, j)),
            pl.BlockSpec((ROWS, FF_BLOCK), lambda j: (0, j)),
            pl.BlockSpec((ROWS, D), lambda j: (0, 0)),
        ],
        out_shape=[
            jax.ShapeDtypeStruct((ROWS, FF), jnp.bfloat16),
            jax.ShapeDtypeStruct((ROWS, FF), jnp.bfloat16),
            jax.ShapeDtypeStruct((ROWS, D), jnp.bfloat16),
        ],
        scratch_shapes=[pltpu.VMEM((ROWS, D), jnp.float32)],
        compiler_params=pltpu.CompilerParams(vmem_limit_bytes=48 * MIB),
        cost_estimate=pl.CostEstimate(
            flops=8 * ROWS * D * FF, bytes_accessed=17 * MIB, transcendentals=ROWS * FF
        ),
        name="expert",
    )(got, got, w_gate, w_up)


def weight_part(x_ref, dg_ref, du_ref):
    dims = (((0,), (0,)), ((), ()))
    x = x_ref[...]
    return (
        lax.dot_general(x, dg_ref[...], dims, preferred_element_type=jnp.float32),
        lax.dot_general(x, du_ref[...], dims, preferred_element_type=jnp.float32),
    )


def weight_send_kernel(block_ref, x_ref, dg_ref, du_ref, out_ref):
    gate, up = weight_part(x_ref, dg_ref, du_ref)
    out_ref[:, :FF] = gate.astype(jnp.bfloat16)
    out_ref[:, FF:] = up.astype(jnp.bfloat16)


def weight_specs():
    return [
        pl.BlockSpec((ROWS, BLOCK), lambda i, b: (0, b[i])),
        pl.BlockSpec((ROWS, FF), lambda i, b: (0, 0)),
        pl.BlockSpec((ROWS, FF), lambda i, b: (0, 0)),
    ]


def weight_send(blocks, got, delta_g, delta_u):
    count = blocks.shape[0]
    return pl.pallas_call(
        weight_send_kernel,
        grid_spec=pltpu.PrefetchScalarGridSpec(
            num_scalar_prefetch=1,
            grid=(count,),
            in_specs=weight_specs(),
            out_specs=pl.BlockSpec((BLOCK, 2 * FF), lambda i, b: (i, 0)),
        ),
        out_shape=jax.ShapeDtypeStruct((count * BLOCK, 2 * FF), jnp.bfloat16),
        compiler_params=pltpu.CompilerParams(vmem_limit_bytes=32 * MIB),
        cost_estimate=pl.CostEstimate(
            flops=4 * ROWS * count * BLOCK * FF, bytes_accessed=8 * MIB, transcendentals=0
        ),
        name="weight_send",
    )(blocks, got, delta_g, delta_u)


def weight_keep_kernel(block_ref, x_ref, dg_ref, du_ref, came_ref, own_ref, *out_refs):
    i = pl.program_id(0)
    gate, up = weight_part(x_ref, dg_ref, du_ref)
    gate = gate + came_ref[:, :FF].astype(jnp.float32)
    up = up + came_ref[:, FF:].astype(jnp.float32)

    @pl.when(i == 0)
    def _():
        own_ref[:, :FF] = gate
        own_ref[:, FF:] = up

    for k, out_ref in enumerate(out_refs):

        @pl.when(i == k + 1)
        def _(out_ref=out_ref):
            out_ref[:, :FF] = gate.astype(jnp.bfloat16)
            out_ref[:, FF:] = up.astype(jnp.bfloat16)


def weight_keep(blocks, got, delta_g, delta_u, came):
    count = blocks.shape[0]
    whole = pl.BlockSpec((BLOCK, 2 * FF), lambda i, b: (0, 0))
    return pl.pallas_call(
        weight_keep_kernel,
        grid_spec=pltpu.PrefetchScalarGridSpec(
            num_scalar_prefetch=1,
            grid=(count,),
            in_specs=weight_specs() + [pl.BlockSpec((BLOCK, 2 * FF), lambda i, b: (i, 0))],
            out_specs=[whole] * count,
        ),
        out_shape=[jax.ShapeDtypeStruct((BLOCK, 2 * FF), jnp.float32)]
        + [jax.ShapeDtypeStruct((BLOCK, 2 * FF), jnp.bfloat16)] * (count - 1),
        compiler_params=pltpu.CompilerParams(vmem_limit_bytes=40 * MIB),
        cost_estimate=pl.CostEstimate(
            flops=4 * ROWS * count * BLOCK * FF, bytes_accessed=11 * MIB, transcendentals=0
        ),
        name="weight_keep",
    )(blocks, got, delta_g, delta_u, came)


def place(index):
    return index // 4, index // 2 % 2, index % 2


def partner(index, step):
    y, x, core = place(index)
    return (y + step // 2) % 4 * 4 + (x + step % 2) % 2 * 2 + core


def per_device(tokens, routes, grad_hidden, w_gate, w_up):
    toks, per_token = routes.shape
    pairs = toks * per_token
    groups = lax.axis_size("dp")
    steps = groups // 2
    sel, send = pack(
        routes.reshape(1, pairs), tokens, grad_hidden.reshape(pairs, grad_hidden.shape[2])
    )
    got = lax.all_to_all(send, "expert", split_axis=0, concat_axis=0, tiled=True)
    delta_g, delta_u, back = expert(got, w_gate, w_up)
    returned = lax.all_to_all(back, "expert", split_axis=0, concat_axis=0, tiled=True)

    keep_table = np.array([[partner(i, s) for s in range(steps)] for i in range(groups)], np.int32)
    me = lax.axis_index("dp")
    keep_blocks = jnp.asarray(keep_table)[me]
    other_half = weight_send(keep_blocks ^ 1, got, delta_g, delta_u)
    came = lax.ppermute(other_half, "dp", [(i, i ^ 1) for i in range(groups)])
    own, *parts = weight_keep(keep_blocks, got, delta_g, delta_u, came)
    total = own
    for s, part in enumerate(parts, 1):
        came = lax.ppermute(part, "dp", [(i, partner(i, s)) for i in range(groups)])
        total = total + came.astype(jnp.float32)
    grad_tokens = lax.dot_general(
        sel, returned, (((0,), (0,)), ((), ())), preferred_element_type=jnp.float32
    ).astype(jnp.bfloat16)
    return grad_tokens, total[None, :, :FF], total[None, :, FF:]


def solution(mesh):
    placed = (
        P(("dp", "expert"), None),
        P(("dp", "expert"), None),
        P(("dp", "expert"), None, None),
        P("expert", None, None),
        P("expert", None, None),
    )
    return jax.shard_map(
        per_device,
        mesh=mesh,
        in_specs=placed,
        out_specs=(P(("dp", "expert"), None), P("expert", "dp", None), P("expert", "dp", None)),
        check_vma=False,
    )
```

time: 374 us -> 231 us (0.62)
  waiting for transfers between devices: 182 us -> 59.1 us
  blocking collectives: 0 us -> 108 us
  local copies, waits for them, and re-layouts: 84.3 us -> 8.7 us
  other arithmetic: 44.8 us -> 1.06 us
  Pallas kernels: 0 us -> 28.8 us
  matrix products: 22.6 us -> 3.29 us
  between operations: 14.3 us -> 0.71 us
    all_to_all x3 -> x1, waiting for transfers between devices: 148 us -> 0.01 us  [per_device(): lax.all_to_all(back, 'expert', split_axis=0, concat_axis=0, tiled=True)]
    all_to_all x0 -> x1, blocking collectives: none -> 108 us  [per_device(): lax.all_to_all(send, 'expert', split_axis=0, concat_axis=0, tiled=True)]
    ppermute x0 -> x8, waiting for transfers between devices: none -> 59.1 us  [the longest x7 54.2 us: per_device(): came = lax.ppermute(part, 'dp', [(i, partner(i, s)) for i in range(groups)])]
    unnamed x2 -> x0, waiting for transfers between devices: 34.1 us -> none
    concatenate x2 -> x0, other arithmetic: 32.1 us -> none  [the longest x1 27.3 us: in_one_piece(): both = jnp.concatenate(arrays, axis=along)]
    pallas_call x0 -> x4, Pallas kernels: none -> 28.8 us  [the longest x1 15.4 us: expert(): pl.pallas_call(expert_kernel, grid=(steps,), in_specs=[pl.BlockSpec((ROWS...]
    reshape x10 -> x2, local copies, waits for them, and re-layouts: 28.2 us -> 1.28 us  [the longest x1 1.15 us: per_device(): grad_hidden.reshape(pairs, grad_hidden.shape[2])]
    unnamed x34 -> x11, local copies, waits for them, and re-layouts: 26.6 us -> 5.79 us
  transfers between devices with their start and end apart: 4 -> 9, of which waited for: 4 -> 5; matrix products, arithmetic and copies ran while one was open for 16% -> 1% of each run, Pallas kernels for 0% -> 5%
where the time goes in v1:
time: 231 us; the launch traced here: 230 us
  blocking collectives  108 us (47%)
  waiting for transfers between devices  59.1 us (26%)
  Pallas kernels  28.8 us (12%)
  starting transfers between devices  20.3 us (9%)
  local copies, waits for them, and re-layouts  8.7 us (4%)
  matrix products  3.29 us (1%)
    all_to_all x1, blocking collectives, per_device(): lax.all_to_all(send, 'expert', split_axis=0, concat_axis=0, tiled=True)  108 us
    ppermute x7, waiting for transfers between devices, per_device(): came = lax.ppermute(part, 'dp', [(i, partner(i, s)) for i in range(groups)])  54.2 us
    pallas_call x1, Pallas kernels, expert(): pl.pallas_call(expert_kernel, grid=(steps,), in_specs=[pl.BlockSpec((ROWS...  15.4 us
    ppermute x7, starting transfers between devices, per_device(): came = lax.ppermute(part, 'dp', [(i, partner(i, s)) for i in range(groups)])  14.3 us
    all_to_all x1, starting transfers between devices, per_device(): lax.all_to_all(back, 'expert', split_axis=0, concat_axis=0, tiled=True)  5.84 us
    unnamed x11, local copies, waits for them, and re-layouts  5.79 us
    pallas_call x1, Pallas kernels, weight_keep(): pl.pallas_call(weight_keep_kernel, grid_spec=pltpu.PrefetchScalarGridSpec...  5.55 us
    pallas_call x1, Pallas kernels, weight_send(): pl.pallas_call(weight_send_kernel, grid_spec=pltpu.PrefetchScalarGridSpec...  4.95 us
  transfers between devices with their start and end apart: 9, of which 5 were waited for; matrix products, arithmetic and copies ran while one was open for 1% of the time, Pallas kernels for 5%

profile of v1, /device:TPU:14, one launch (start us, length us, event | category | flops | bytes accessed | tf_op | source)
XLA Modules:
  0.0 229.9 jit_solution(10369800575317284952)
XLA Ops:
  0.6 0.8 copy.10
  1.4 0.1 reshape.16.routes_ref
  1.6 1.1 reshape.17.grads_ref
  2.7 0.0 copy-start.2
  2.7 1.0 copy-done.2
  3.8 2.9 %pack.1 = (bf16[768,128]{1,0:T(8,128)(2,1)S(1)}, bf16[768,2816]{1,0:T(8,128)(2,1)S(1)}) custom-call(s32[1,256]{1,0:T(1,128)S(1)} %reshape.16.routes_ref, bf16[128,2048]{1,0:T(8,128)(2,1)S(1)} %copy-done.2, bf16[256,768]{1,0:T(8,128)(2,1)S(1)} %reshape.17.grads_ref), custom_call_target="tpu_custom_call" | custom-call | flops 1000000000 | bytes 6291456 | tf_op jit(solution)/shard_map/pack/pallas_call | solution.py:53
  6.7 108.0 %all_to_all.23 = bf16[16,48,2816]{2,1,0:T(8,128)(2,1)} all-to-all(bf16[16,48,2816]{2,1,0:T(8,128)(2,1)S(1)} %bitcast.20), channel_id=1, replica_groups=mesh['dp'=16,'expert'=16] {'expert'}, dimensions={0} | all-to-all | bytes 8650752 | tf_op jit(solution)/shard_map/all_to_all | solution.py:237
  114.6 15.4 %expert.1 = (bf16[768,768]{1,0:T(8,128)(2,1)S(1)}, bf16[768,768]{1,0:T(8,128)(2,1)S(1)}, bf16[768,2048]{1,0:T(8,128)(2,1)S(1)}) custom-call(bf16[768,2816]{1,0:T(8,128)(2,1)} %bitcast.14, bf16[768,2816]{1,0:T(8,128)(2,1)} %bitcast.15, bf16[1,2048,768]{2,1,0:T(8,128)(2,1)} %wg_ref.1, bf16[1,2048,768]{2,1,0:T(8,128)(2,1)} %wu_ref.1), custom_call_target="tpu_custom_call" | custom-call | flops 9663676416 | bytes 17825792 | tf_op jit(solution)/shard_map/expert/pallas_call | solution.py:110
  130.1 1.7 copy-done.1
  131.8 5.8 %all-to-all-start.1 = ((bf16[16,48,2048]{2,1,0:T(8,128)(2,1)}), bf16[16,48,2048]{2,1,0:T(8,128)(2,1)}, u32[]{:S(2)}, u32[]{:S(2)}) async-start(bf16[16,48,2048]{2,1,0:T(8,128)(2,1)} %bitcast.21), calls=%async_computation.1 | async-start | bytes 6291456 | tf_op jit(solution)/shard_map/all_to_all | solution.py:239
  137.6 0.7 broadcast_xor_fusion.block_ref
  138.3 2.2 copy-done
  140.6 4.9 %weight_send.1 = bf16[1024,1536]{1,0:T(8,128)(2,1)S(1)} custom-call(s32[8]{0:T(128)S(1)} %broadcast_xor_fusion.block_ref, bf16[768,2816]{1,0:T(8,128)(2,1)S(1)} %bitcast.16, bf16[768,768]{1,0:T(8,128)(2,1)S(1)} %get-tuple-element.19.dg_ref, bf16[768,768]{1,0:T(8,128)(2,1)S(1)} %get-tuple-element.20.du_ref), custom_call_target="tpu_custom_call" | custom-call | flops 2415919104 | bytes 8388608 | tf_op jit(solution)/shard_map/weight_send/pallas_call | solution.py:163
  145.5 0.1 collective-permute-start
  145.6 0.7 dynamic-slice_bitcast_fusion.block_ref
  146.3 4.9 %collective-permute-done.came_ref = bf16[1024,1536]{1,0:T(8,128)(2,1)S(1)} collective-permute-done((bf16[1024,1536]{1,0:T(8,128)(2,1)S(1)}, bf16[1024,1536]{1,0:T(8,128)(2,1)S(1)}, u32[]{:S(2)}, u32[]{:S(2)}) %collective-permute-start) | collective-permute-done | bytes 3145760 | tf_op jit(solution)/shard_map/ppermute | solution.py:245
  151.3 5.5 %weight_keep.1 = (f32[128,1536]{1,0:T(8,128)S(1)}, bf16[128,1536]{1,0:T(8,128)(2,1)S(1)}, bf16[128,1536]{1,0:T(8,128)(2,1)S(1)}, bf16[128,1536]{1,0:T(8,128)(2,1...) custom-call(s32[8]{0:T(128)S(1)} %dynamic-slice_bitcast_fusion.block, ...), custom_call_target="tpu_custom_call" | custom-call | flops 2415919104 | bytes 11534336 | tf_op jit(solution)/shard_map/weight_keep/pallas_call | solution.py:202
  156.8 1.5 collective-permute-start.1
  158.3 1.6 collective-permute-start.2
  159.9 2.8 %collective-permute-start.3 = (bf16[128,1536]{1,0:T(8,128)(2,1)S(1)}, bf16[128,1536]{1,0:T(8,128)(2,1)S(1)}, u32[]{:S(2)}, u32[]{:S(2)}) collective-permute-start(bf16[128,1536]{1,0:T(8,128)(2,1)S(1)} %get-tuple-element.24), channel_id=1, source_target_pairs={{0,96},{16,112},{32,64},{48,80},{64,160},{80,176},{96,128},{112,14... | collective-permute-start | bytes 1179656 | tf_op jit(solution)/shard_map/ppermute | solution.py:249
  162.7 1.2 collective-permute-start.4
  164.0 3.1 %collective-permute-start.5 = (bf16[128,1536]{1,0:T(8,128)(2,1)S(1)}, bf16[128,1536]{1,0:T(8,128)(2,1)S(1)}, u32[]{:S(2)}, u32[]{:S(2)}) collective-permute-start(bf16[128,1536]{1,0:T(8,128)(2,1)S(1)} %get-tuple-element.26), channel_id=1, source_target_pairs={{0,160},{16,176},{32,128},{48,144},{64,224},{80,240},{96,192},{112... | collective-permute-start | bytes 1179656 | tf_op jit(solution)/shard_map/ppermute | solution.py:249
  167.1 5.3 %collective-permute-done.1 = bf16[128,1536]{1,0:T(8,128)(2,1)S(1)} collective-permute-done((bf16[128,1536]{1,0:T(8,128)(2,1)S(1)}, bf16[128,1536]{1,0:T(8,128)(2,1)S(1)}, u32[]{:S(2)}, u32[]{:S(2)}) %collective-permute-start.1) | collective-permute-done | bytes 393248 | tf_op jit(solution)/shard_map/ppermute | solution.py:249
  172.5 0.4 collective-permute-start.6
  172.9 0.0 collective-permute-done.2
  172.9 3.6 %collective-permute-start.7 = (bf16[128,1536]{1,0:T(8,128)(2,1)S(1)}, bf16[128,1536]{1,0:T(8,128)(2,1)S(1)}, u32[]{:S(2)}, u32[]{:S(2)}) collective-permute-start(bf16[128,1536]{1,0:T(8,128)(2,1)S(1)} %get-tuple-element.28), channel_id=1, source_target_pairs={{0,224},{16,240},{32,192},{48,208},{64,32},{80,48},{96,0},{112,16}... | collective-permute-start | bytes 1179656 | tf_op jit(solution)/shard_map/ppermute | solution.py:249
  176.5 18.3 %collective-permute-done.3 = bf16[128,1536]{1,0:T(8,128)(2,1)S(1)} collective-permute-done((bf16[128,1536]{1,0:T(8,128)(2,1)S(1)}, bf16[128,1536]{1,0:T(8,128)(2,1)S(1)}, u32[]{:S(2)}, u32[]{:S(2)}) %collective-permute-start.3) | collective-permute-done | bytes 393248 | tf_op jit(solution)/shard_map/ppermute | solution.py:249
  194.8 23.6 %collective-permute-done.5 = bf16[128,1536]{1,0:T(8,128)(2,1)S(1)} collective-permute-done((bf16[128,1536]{1,0:T(8,128)(2,1)S(1)}, bf16[128,1536]{1,0:T(8,128)(2,1)S(1)}, u32[]{:S(2)}, u32[]{:S(2)}) %collective-permute-start.5) | collective-permute-done | bytes 393248 | tf_op jit(solution)/shard_map/ppermute | solution.py:249
  218.4 6.9 %collective-permute-done.7 = bf16[128,1536]{1,0:T(8,128)(2,1)S(1)} collective-permute-done((bf16[128,1536]{1,0:T(8,128)(2,1)S(1)}, bf16[128,1536]{1,0:T(8,128)(2,1)S(1)}, u32[]{:S(2)}, u32[]{:S(2)}) %collective-permute-start.7) | collective-permute-done | bytes 393248 | tf_op jit(solution)/shard_map/ppermute | solution.py:249
  225.3 0.4 convert_add_fusion
  225.7 0.9 slice_bitcast_fusion
  226.6 3.3 %convolution_convert_fusion = bf16[128,2048]{1,0:T(8,128)(2,1)} fusion(bf16[768,128]{1,0:T(8,128)(2,1)S(1)} %get-tuple-element.16, bf16[768,2048]{1,0:T(8,128)(2,1)} %bitcast.3), kind=kOutput, calls=%fused_computation | convolution fusion | flops 402915328 | bytes 3866624 | tf_op jit(solution)/shard_map/dot_general | solution.py:251
  (10 shorter events, 0.0 us)
Async XLA Ops:
  2.7 1.0 copy-start.2
  130.1 1.7 copy-start.1
  131.8 19.5 %slice-start = ((s8[4325376]{0:T(1024)(128)(4,1)}), s8[131072]{0:T(1024)(128)(4,1)S(1)}, s32[]{:S(2)}) async-start(s8[4325376]{0:T(1024)(128)(4,1)} %bitcast.17), calls=%async_computation.2 | async-start | bytes 262144
  131.8 94.8 %all-to-all-start.1 = ((bf16[16,48,2048]{2,1,0:T(8,128)(2,1)}), bf16[16,48,2048]{2,1,0:T(8,128)(2,1)}, u32[]{:S(2)}, u32[]{:S(2)}) async-start(bf16[16,48,2048]{2,1,0:T(8,128)(2,1)} %bitcast.21), calls=%async_computation.1 | async-start | bytes 6291456 | tf_op jit(solution)/shard_map/all_to_all | solution.py:239
  138.3 2.2 copy-start
  140.6 10.7 %slice-start.1 = ((s8[4325376]{0:T(1024)(128)(4,1)}), s8[4194304]{0:T(1024)(128)(4,1)S(1)}, s32[]{:S(2)}) async-start(s8[4325376]{0:T(1024)(128)(4,1)} %bitcast.17), calls=%async_computation.3 | async-start | bytes 8388608
  145.5 5.7 %collective-permute-start = (bf16[1024,1536]{1,0:T(8,128)(2,1)S(1)}, bf16[1024,1536]{1,0:T(8,128)(2,1)S(1)}, u32[]{:S(2)}, u32[]{:S(2)}) collective-permute-start(bf16[1024,1536]{1,0:T(8,128)(2,1)S(1)} %weight_send.1), channel_id=1, source_target_pairs={{0,16},{16,0},{32,48},{48,32},{64,80},{80,64},{96,112},{112,96},{1... | collective-permute-start | bytes 9437192 | tf_op jit(solution)/shard_map/ppermute | solution.py:245
  156.8 15.6 %collective-permute-start.1 = (bf16[128,1536]{1,0:T(8,128)(2,1)S(1)}, bf16[128,1536]{1,0:T(8,128)(2,1)S(1)}, u32[]{:S(2)}, u32[]{:S(2)}) collective-permute-start(bf16[128,1536]{1,0:T(8,128)(2,1)S(1)} %get-tuple-element.22), channel_id=1, source_target_pairs={{0,32},{16,48},{32,0},{48,16},{64,96},{80,112},{96,64},{112,80},{1... | collective-permute-start | bytes 1179656 | tf_op jit(solution)/shard_map/ppermute | solution.py:249
  158.3 14.6 %collective-permute-start.2 = (bf16[128,1536]{1,0:T(8,128)(2,1)S(1)}, bf16[128,1536]{1,0:T(8,128)(2,1)S(1)}, u32[]{:S(2)}, u32[]{:S(2)}) collective-permute-start(bf16[128,1536]{1,0:T(8,128)(2,1)S(1)} %get-tuple-element.23), channel_id=1, source_target_pairs={{0,64},{16,80},{32,96},{48,112},{64,128},{80,144},{96,160},{112,17... | collective-permute-start | bytes 1179656 | tf_op jit(solution)/shard_map/ppermute | solution.py:249
  159.9 34.9 %collective-permute-start.3 = (bf16[128,1536]{1,0:T(8,128)(2,1)S(1)}, bf16[128,1536]{1,0:T(8,128)(2,1)S(1)}, u32[]{:S(2)}, u32[]{:S(2)}) collective-permute-start(bf16[128,1536]{1,0:T(8,128)(2,1)S(1)} %get-tuple-element.24), channel_id=1, source_target_pairs={{0,96},{16,112},{32,64},{48,80},{64,160},{80,176},{96,128},{112,14... | collective-permute-start | bytes 1179656 | tf_op jit(solution)/shard_map/ppermute | solution.py:249
  162.7 32.1 %collective-permute-start.4 = (bf16[128,1536]{1,0:T(8,128)(2,1)S(1)}, bf16[128,1536]{1,0:T(8,128)(2,1)S(1)}, u32[]{:S(2)}, u32[]{:S(2)}) collective-permute-start(bf16[128,1536]{1,0:T(8,128)(2,1)S(1)} %get-tuple-element.25), channel_id=1, source_target_pairs={{0,128},{16,144},{32,160},{48,176},{64,192},{80,208},{96,224},{112... | collective-permute-start | bytes 1179656 | tf_op jit(solution)/shard_map/ppermute | solution.py:249
  164.0 54.4 %collective-permute-start.5 = (bf16[128,1536]{1,0:T(8,128)(2,1)S(1)}, bf16[128,1536]{1,0:T(8,128)(2,1)S(1)}, u32[]{:S(2)}, u32[]{:S(2)}) collective-permute-start(bf16[128,1536]{1,0:T(8,128)(2,1)S(1)} %get-tuple-element.26), channel_id=1, source_target_pairs={{0,160},{16,176},{32,128},{48,144},{64,224},{80,240},{96,192},{112... | collective-permute-start | bytes 1179656 | tf_op jit(solution)/shard_map/ppermute | solution.py:249
  172.5 45.9 %collective-permute-start.6 = (bf16[128,1536]{1,0:T(8,128)(2,1)S(1)}, bf16[128,1536]{1,0:T(8,128)(2,1)S(1)}, u32[]{:S(2)}, u32[]{:S(2)}) collective-permute-start(bf16[128,1536]{1,0:T(8,128)(2,1)S(1)} %get-tuple-element.27), channel_id=1, source_target_pairs={{0,192},{16,208},{32,224},{48,240},{64,0},{80,16},{96,32},{112,48}... | collective-permute-start | bytes 1179656 | tf_op jit(solution)/shard_map/ppermute | solution.py:249
  172.9 52.4 %collective-permute-start.7 = (bf16[128,1536]{1,0:T(8,128)(2,1)S(1)}, bf16[128,1536]{1,0:T(8,128)(2,1)S(1)}, u32[]{:S(2)}, u32[]{:S(2)}) collective-permute-start(bf16[128,1536]{1,0:T(8,128)(2,1)S(1)} %get-tuple-element.28), channel_id=1, source_target_pairs={{0,224},{16,240},{32,192},{48,208},{64,32},{80,48},{96,0},{112,16}... | collective-permute-start | bytes 1179656 | tf_op jit(solution)/shard_map/ppermute | solution.py:249

commit v2 on v1

v2 whole, which is shorter than its diff:
```python
import functools

import jax
import jax.numpy as jnp
import numpy as np
from jax import lax
from jax.experimental import pallas as pl
from jax.experimental.pallas import tpu as pltpu
from jax.sharding import PartitionSpec as P

D = 2048
FF = 768
EXPERTS = 16
COLD = 16
SPILL = 32
CAP = COLD + SPILL
ROWS = EXPERTS * CAP
DIRECT = EXPERTS * COLD
OVER = EXPERTS * SPILL
WIDTH = D + FF
OFFSETS = (0, -1, 1, -2, 2, -3, 3, 4)
PIECES = ((0, 3), (3, 5), (5, 7), (7, 8))
BLOCK = 128
FF_BLOCK = 256
MIB = 1 << 20


def pack_kernel(me_ref, routes_ref, tokens_ref, grads_ref, choice_ref, sel_ref, out_ref, over_ref):
    pairs = routes_ref.shape[1]
    toks = tokens_ref.shape[0]
    me = me_ref[0]
    routes = routes_ref[...]
    member = (routes == lax.broadcasted_iota(jnp.int32, (EXPERTS, pairs), 0)).astype(jnp.float32)
    member_low = member.astype(jnp.bfloat16)
    earlier = (
        lax.broadcasted_iota(jnp.int32, (pairs, pairs), 0)
        < lax.broadcasted_iota(jnp.int32, (pairs, pairs), 1)
    ).astype(jnp.bfloat16)
    before = jnp.dot(member_low, earlier, preferred_element_type=jnp.float32)
    rank = jnp.sum(member * before, axis=0, keepdims=True).astype(jnp.int32)

    count_col = jnp.sum(member, axis=1, keepdims=True)
    count_row = lax.dot_general(
        jnp.ones((8, pairs), jnp.bfloat16),
        member_low,
        (((1,), (1,)), ((), ())),
        preferred_element_type=jnp.float32,
    )[:1]
    down = lax.broadcasted_iota(jnp.int32, (EXPERTS, EXPERTS), 0)
    across = lax.broadcasted_iota(jnp.int32, (EXPERTS, EXPERTS), 1)
    above_col = jnp.sum((count_row > count_col).astype(jnp.float32), axis=1, keepdims=True)
    above_row = jnp.sum((count_col > count_row).astype(jnp.float32), axis=0, keepdims=True)
    hot_col = (above_col < 1.5).astype(jnp.float32)
    hot_row = (above_row < 1.5).astype(jnp.float32)
    which_col = jnp.sum(hot_row * (across < down).astype(jnp.float32), axis=1, keepdims=True)
    which_row = jnp.sum(hot_col * (down < across).astype(jnp.float32), axis=0, keepdims=True)
    which = jnp.sum(member * which_col, axis=0, keepdims=True).astype(jnp.int32)

    lane16 = lax.broadcasted_iota(jnp.int32, (1, EXPERTS), 1)
    mine = (lane16 == me).astype(jnp.float32)
    beside = (lane16 == me + 1 - 2 * (me % 2)).astype(jnp.float32)
    hot_me = jnp.sum(mine * hot_row, axis=1, keepdims=True)
    slot_me = jnp.sum(mine * hot_row * which_row, axis=1, keepdims=True)
    slot_beside = jnp.sum(beside * hot_row * which_row, axis=1, keepdims=True)
    lane = lax.broadcasted_iota(jnp.int32, (1, 128), 1)
    choice_ref[...] = jnp.where(
        lane == 0,
        slot_me.astype(jnp.int32),
        jnp.where(
            lane == 1,
            hot_me.astype(jnp.int32),
            jnp.where(lane == 2, slot_beside.astype(jnp.int32), me),
        ),
    )

    to_token = (
        lax.broadcasted_iota(jnp.int32, (pairs, toks), 0) // 2
        == lax.broadcasted_iota(jnp.int32, (pairs, toks), 1)
    ).astype(jnp.bfloat16)

    def picked(slot, rows):
        pick = (slot == lax.broadcasted_iota(jnp.int32, (rows, pairs), 0)).astype(jnp.bfloat16)
        tok = jnp.dot(pick, to_token, preferred_element_type=jnp.float32).astype(jnp.bfloat16)
        return pick, tok

    def fill(ref, slot):
        pick, tok = picked(slot, ref.shape[0])
        ref[:, :D] = jnp.dot(tok, tokens_ref[...], preferred_element_type=jnp.float32).astype(
            jnp.bfloat16
        )
        ref[:, D:] = jnp.dot(pick, grads_ref[...], preferred_element_type=jnp.float32).astype(
            jnp.bfloat16
        )

    fill(over_ref, jnp.where(rank >= COLD, which * SPILL + rank - COLD, -1))
    fill(out_ref, jnp.where(rank < COLD, routes * COLD + rank, -1))
    sel_ref[...] = picked(routes * CAP + rank, ROWS)[1]


def pack(me, routes, tokens, grads):
    toks, pairs = tokens.shape[0], grads.shape[0]
    vmem = pl.BlockSpec(memory_space=pltpu.VMEM)
    return pl.pallas_call(
        pack_kernel,
        in_specs=[pl.BlockSpec(memory_space=pltpu.SMEM), vmem, vmem, vmem],
        out_specs=[vmem] * 4,
        out_shape=[
            jax.ShapeDtypeStruct((1, 128), jnp.int32),
            jax.ShapeDtypeStruct((ROWS, toks), jnp.bfloat16),
            jax.ShapeDtypeStruct((DIRECT, WIDTH), jnp.bfloat16),
            jax.ShapeDtypeStruct((2 * SPILL, WIDTH), jnp.bfloat16),
        ],
        compiler_params=pltpu.CompilerParams(vmem_limit_bytes=12 * MIB),
        cost_estimate=pl.CostEstimate(flops=10**9, bytes_accessed=4 * MIB, transcendentals=0),
        name="pack",
    )(me, routes, tokens, grads)


def choose_kernel(choice_ref, *refs):
    for k, ref in enumerate(refs[:-1]):
        refs[-1][k * SPILL : (k + 1) * SPILL, :] = ref[...]


def choose(choice, blocks):
    count = len(blocks)
    return pl.pallas_call(
        choose_kernel,
        grid_spec=pltpu.PrefetchScalarGridSpec(
            num_scalar_prefetch=1,
            grid=(1,),
            in_specs=[pl.BlockSpec((SPILL, WIDTH), lambda i, c: (c[2], 0))] * count,
            out_specs=pl.BlockSpec((count * SPILL, WIDTH), lambda i, c: (0, 0)),
        ),
        out_shape=jax.ShapeDtypeStruct((count * SPILL, WIDTH), jnp.bfloat16),
        compiler_params=pltpu.CompilerParams(vmem_limit_bytes=4 * MIB),
        cost_estimate=pl.CostEstimate(
            flops=0, bytes_accessed=4 * count * SPILL * WIDTH, transcendentals=0
        ),
        name="choose",
    )(choice, *blocks)


def deltas(x, dh, wg, wu):
    gate = jnp.dot(x, wg, preferred_element_type=jnp.float32)
    up = jnp.dot(x, wu, preferred_element_type=jnp.float32)
    sig = jax.nn.sigmoid(gate)
    wide = dh.astype(jnp.float32)
    delta_g = (wide * up * sig * (1.0 + gate * (1.0 - sig))).astype(jnp.bfloat16)
    delta_u = (wide * gate * sig).astype(jnp.bfloat16)
    dims = (((1,), (1,)), ((), ()))
    part = lax.dot_general(
        delta_g, wg, dims, preferred_element_type=jnp.float32
    ) + lax.dot_general(delta_u, wu, dims, preferred_element_type=jnp.float32)
    return delta_g, delta_u, part


def over_kernel(choice_ref, *refs):
    column = refs[:8]
    pieces = refs[8 : 8 + len(PIECES)]
    wg_ref, wu_ref, x_ref, delta_g_ref, delta_u_ref, back_ref, acc_ref, dh_ref = refs[
        8 + len(PIECES) :
    ]
    j = pl.program_id(0)
    last = pl.num_programs(0) - 1
    hot = choice_ref[1] == 1

    @pl.when(j == 0)
    def _():
        back_ref[...] = jnp.zeros_like(back_ref)
        at = 0
        for ref in (*column, *pieces):
            rows = ref.shape[0]
            x_ref[at : at + rows, :] = ref[:, :D]
            for k in range(FF // FF_BLOCK):
                dh_ref[k, at : at + rows, :] = ref[
                    :, D + k * FF_BLOCK : D + (k + 1) * FF_BLOCK
                ]
            at += rows

    @pl.when(jnp.logical_not(hot))
    def _():
        delta_g_ref[...] = jnp.zeros_like(delta_g_ref)
        delta_u_ref[...] = jnp.zeros_like(delta_u_ref)

    @pl.when(hot)
    def _():
        delta_g, delta_u, part = deltas(x_ref[...], dh_ref[j], wg_ref[0], wu_ref[0])
        delta_g_ref[...] = delta_g
        delta_u_ref[...] = delta_u

        @pl.when(j == 0)
        def _():
            acc_ref[...] = part

        @pl.when(jnp.logical_and(j > 0, j < last))
        def _():
            acc_ref[...] += part

        @pl.when(j == last)
        def _():
            acc_ref[...] += part
            me = choice_ref[3]
            for k in range(2 * len(OFFSETS)):
                source = (me + 2 * OFFSETS[k % 8] + EXPERTS) % EXPERTS
                if k >= 8:
                    source = source + 1 - 2 * (source % 2)
                row = pl.multiple_of(source * CAP + COLD, COLD)
                back_ref[pl.ds(row, SPILL), :] = acc_ref[
                    k * SPILL : (k + 1) * SPILL, :
                ].astype(jnp.bfloat16)


def over(choice, column, pieces, w_gate, w_up):
    steps = FF // FF_BLOCK
    return pl.pallas_call(
        over_kernel,
        grid_spec=pltpu.PrefetchScalarGridSpec(
            num_scalar_prefetch=1,
            grid=(steps,),
            in_specs=[pl.BlockSpec((SPILL, WIDTH), lambda j, c: (c[0], 0))] * len(column)
            + [pl.BlockSpec(p.shape, lambda j, c: (0, 0)) for p in pieces]
            + [pl.BlockSpec((1, D, FF_BLOCK), lambda j, c: (0, 0, j))] * 2,
            out_specs=[
                pl.BlockSpec((OVER, D), lambda j, c: (0, 0)),
                pl.BlockSpec((OVER, FF_BLOCK), lambda j, c: (0, j)),
                pl.BlockSpec((OVER, FF_BLOCK), lambda j, c: (0, j)),
                pl.BlockSpec((ROWS, D), lambda j, c: (0, 0)),
            ],
            scratch_shapes=[
                pltpu.VMEM((OVER, D), jnp.float32),
                pltpu.VMEM((steps, OVER, FF_BLOCK), jnp.bfloat16),
            ],
        ),
        out_shape=[
            jax.ShapeDtypeStruct((OVER, D), jnp.bfloat16),
            jax.ShapeDtypeStruct((OVER, FF), jnp.bfloat16),
            jax.ShapeDtypeStruct((OVER, FF), jnp.bfloat16),
            pltpu.HBM((ROWS, D), jnp.bfloat16),
        ],
        compiler_params=pltpu.CompilerParams(vmem_limit_bytes=34 * MIB),
        cost_estimate=pl.CostEstimate(
            flops=8 * OVER * D * FF, bytes_accessed=17 * MIB, transcendentals=OVER * FF
        ),
        name="over",
    )(choice, *column, *pieces, w_gate, w_up)


def direct_kernel(
    x_ref, dh_ref, wg_ref, wu_ref, old_ref, delta_g_ref, delta_u_ref, back_ref, acc_ref, low_ref, sems
):
    j = pl.program_id(0)
    delta_g, delta_u, part = deltas(x_ref[...], dh_ref[...], wg_ref[0], wu_ref[0])
    delta_g_ref[...] = delta_g
    delta_u_ref[...] = delta_u
    last = pl.num_programs(0) - 1

    @pl.when(j == 0)
    def _():
        acc_ref[...] = part

    @pl.when(jnp.logical_and(j > 0, j < last))
    def _():
        acc_ref[...] += part

    @pl.when(j == last)
    def _():
        low_ref[...] = (acc_ref[...] + part).astype(jnp.bfloat16)
        copies = [
            pltpu.make_async_copy(
                low_ref.at[pl.ds(e * COLD, COLD), :],
                back_ref.at[pl.ds(e * CAP, COLD), :],
                sems.at[e],
            )
            for e in range(EXPERTS)
        ]
        for copy in copies:
            copy.start()
        for copy in copies:
            copy.wait()


def direct(got, w_gate, w_up, back):
    steps = FF // FF_BLOCK
    off = D // FF_BLOCK
    return pl.pallas_call(
        direct_kernel,
        grid=(steps,),
        in_specs=[
            pl.BlockSpec((DIRECT, D), lambda j: (0, 0)),
            pl.BlockSpec((DIRECT, FF_BLOCK), lambda j: (0, off + j)),
            pl.BlockSpec((1, D, FF_BLOCK), lambda j: (0, 0, j)),
            pl.BlockSpec((1, D, FF_BLOCK), lambda j: (0, 0, j)),
            pl.BlockSpec(memory_space=pltpu.HBM),
        ],
        out_specs=[
            pl.BlockSpec((DIRECT, FF_BLOCK), lambda j: (0, j)),
            pl.BlockSpec((DIRECT, FF_BLOCK), lambda j: (0, j)),
            pl.BlockSpec(memory_space=pltpu.HBM),
        ],
        out_shape=[
            jax.ShapeDtypeStruct((DIRECT, FF), jnp.bfloat16),
            jax.ShapeDtypeStruct((DIRECT, FF), jnp.bfloat16),
            pltpu.HBM((ROWS, D), jnp.bfloat16),
        ],
        scratch_shapes=[
            pltpu.VMEM((DIRECT, D), jnp.float32),
            pltpu.VMEM((DIRECT, D), jnp.bfloat16),
            pltpu.SemaphoreType.DMA((EXPERTS,)),
        ],
        input_output_aliases={4: 2},
        compiler_params=pltpu.CompilerParams(vmem_limit_bytes=20 * MIB),
        cost_estimate=pl.CostEstimate(
            flops=8 * DIRECT * D * FF, bytes_accessed=10 * MIB, transcendentals=DIRECT * FF
        ),
        name="direct",
    )(got, got, w_gate, w_up, pltpu.with_memory_space_constraint(back, pltpu.HBM))


def weight_part(x_ref, dg_ref, du_ref, over_x_ref, over_dg_ref, over_du_ref):
    dims = (((0,), (0,)), ((), ()))
    x = x_ref[...]
    over_x = over_x_ref[...]

    def both(d_ref, over_d_ref):
        return lax.dot_general(
            x, d_ref[...], dims, preferred_element_type=jnp.float32
        ) + lax.dot_general(over_x, over_d_ref[...], dims, preferred_element_type=jnp.float32)

    return both(dg_ref, over_dg_ref), both(du_ref, over_du_ref)


def weight_send_kernel(block_ref, *refs):
    gate, up = weight_part(*refs[:6])
    out_ref = refs[6]
    out_ref[:, :FF] = gate.astype(jnp.bfloat16)
    out_ref[:, FF:] = up.astype(jnp.bfloat16)


def weight_specs():
    return [
        pl.BlockSpec((DIRECT, BLOCK), lambda i, b: (0, b[i])),
        pl.BlockSpec((DIRECT, FF), lambda i, b: (0, 0)),
        pl.BlockSpec((DIRECT, FF), lambda i, b: (0, 0)),
        pl.BlockSpec((OVER, BLOCK), lambda i, b: (0, b[i])),
        pl.BlockSpec((OVER, FF), lambda i, b: (0, 0)),
        pl.BlockSpec((OVER, FF), lambda i, b: (0, 0)),
    ]


def weight_send(blocks, rows):
    count = blocks.shape[0]
    return pl.pallas_call(
        weight_send_kernel,
        grid_spec=pltpu.PrefetchScalarGridSpec(
            num_scalar_prefetch=1,
            grid=(count,),
            in_specs=weight_specs(),
            out_specs=pl.BlockSpec((BLOCK, 2 * FF), lambda i, b: (i, 0)),
        ),
        out_shape=jax.ShapeDtypeStruct((count * BLOCK, 2 * FF), jnp.bfloat16),
        compiler_params=pltpu.CompilerParams(vmem_limit_bytes=18 * MIB),
        cost_estimate=pl.CostEstimate(
            flops=4 * ROWS * count * BLOCK * FF, bytes_accessed=8 * MIB, transcendentals=0
        ),
        name="weight_send",
    )(blocks, *rows)


def weight_keep_kernel(block_ref, *refs):
    i = pl.program_id(0)
    came_ref, own_ref, *out_refs = refs[6:]
    gate, up = weight_part(*refs[:6])
    gate = gate + came_ref[:, :FF].astype(jnp.float32)
    up = up + came_ref[:, FF:].astype(jnp.float32)

    @pl.when(i == 0)
    def _():
        own_ref[:, :FF] = gate
        own_ref[:, FF:] = up

    for k, out_ref in enumerate(out_refs):

        @pl.when(i == k + 1)
        def _(out_ref=out_ref):
            out_ref[:, :FF] = gate.astype(jnp.bfloat16)
            out_ref[:, FF:] = up.astype(jnp.bfloat16)


def weight_keep(blocks, rows, came):
    count = blocks.shape[0]
    whole = pl.BlockSpec((BLOCK, 2 * FF), lambda i, b: (0, 0))
    return pl.pallas_call(
        weight_keep_kernel,
        grid_spec=pltpu.PrefetchScalarGridSpec(
            num_scalar_prefetch=1,
            grid=(count,),
            in_specs=weight_specs() + [pl.BlockSpec((BLOCK, 2 * FF), lambda i, b: (i, 0))],
            out_specs=[whole] * count,
        ),
        out_shape=[jax.ShapeDtypeStruct((BLOCK, 2 * FF), jnp.float32)]
        + [jax.ShapeDtypeStruct((BLOCK, 2 * FF), jnp.bfloat16)] * (count - 1),
        compiler_params=pltpu.CompilerParams(vmem_limit_bytes=24 * MIB),
        cost_estimate=pl.CostEstimate(
            flops=4 * ROWS * count * BLOCK * FF, bytes_accessed=11 * MIB, transcendentals=0
        ),
        name="weight_keep",
    )(blocks, *rows, came)


def place(index):
    return index // 4, index // 2 % 2, index % 2


def partner(index, step):
    y, x, core = place(index)
    return (y + step // 2) % 4 * 4 + (x + step % 2) % 2 * 2 + core


def per_device(tokens, routes, grad_hidden, w_gate, w_up):
    toks, per_token = routes.shape
    pairs = toks * per_token
    groups = lax.axis_size("dp")
    steps = groups // 2
    expert_at = lax.axis_index("expert")
    choice, sel, send, spill = pack(
        expert_at.reshape(1).astype(jnp.int32),
        routes.reshape(1, pairs),
        tokens,
        grad_hidden.reshape(pairs, grad_hidden.shape[2]),
    )
    choice = choice.reshape(128)
    w_gate = pltpu.with_memory_space_constraint(w_gate, pltpu.HBM)
    w_up = pltpu.with_memory_space_constraint(w_up, pltpu.HBM)
    ups = [(e, (e + 2) % EXPERTS) for e in range(EXPERTS)]
    downs = [(e, (e - 2) % EXPERTS) for e in range(EXPERTS)]
    beside = [(e, e ^ 1) for e in range(EXPERTS)]
    column = [spill]
    right = left = spill
    for _ in range(3):
        right = lax.ppermute(right, "expert", ups)
        left = lax.ppermute(left, "expert", downs)
        column += [right, left]
    column.append(lax.ppermute(right, "expert", ups))
    pieces = [
        lax.ppermute(choose(choice, column[a:b]), "expert", beside) for a, b in PIECES
    ]
    send, right, left = lax.optimization_barrier((send, right, left))
    got = lax.all_to_all(send, "expert", split_axis=0, concat_axis=0, tiled=True)
    over_x, over_g, over_u, back = over(choice, column, pieces, w_gate, w_up)
    delta_g, delta_u, back = direct(got, w_gate, w_up, back)
    returned = lax.all_to_all(back, "expert", split_axis=0, concat_axis=0, tiled=True)
    rows = (got, delta_g, delta_u, over_x, over_g, over_u)

    keep_table = np.array([[partner(i, s) for s in range(steps)] for i in range(groups)], np.int32)
    me = lax.axis_index("dp")
    keep_blocks = jnp.asarray(keep_table)[me]
    other_half = weight_send(keep_blocks ^ 1, rows)
    came = lax.ppermute(other_half, "dp", [(i, i ^ 1) for i in range(groups)])
    own, *parts = weight_keep(keep_blocks, rows, came)
    total = own
    for s, part in enumerate(parts, 1):
        came = lax.ppermute(part, "dp", [(i, partner(i, s)) for i in range(groups)])
        total = total + came.astype(jnp.float32)
    grad_tokens = lax.dot_general(
        sel, returned, (((0,), (0,)), ((), ())), preferred_element_type=jnp.float32
    ).astype(jnp.bfloat16)
    return grad_tokens, total[None, :, :FF], total[None, :, FF:]


def solution(mesh):
    placed = (
        P(("dp", "expert"), None),
        P(("dp", "expert"), None),
        P(("dp", "expert"), None, None),
        P("expert", None, None),
        P("expert", None, None),
    )
    return jax.shard_map(
        per_device,
        mesh=mesh,
        in_specs=placed,
        out_specs=(P(("dp", "expert"), None), P("expert", "dp", None), P("expert", "dp", None)),
        check_vma=False,
    )
```

time: 231 us -> 228 us (0.987)
  blocking collectives: 108 us -> 0 us
  waiting for transfers between devices: 59.1 us -> 120 us
  starting transfers between devices: 20.3 us -> 42.8 us
  local copies, waits for them, and re-layouts: 8.7 us -> 21.4 us
  Pallas kernels: 28.8 us -> 35.8 us
    all_to_all x1 -> x0, blocking collectives: 108 us -> none  [per_device(): lax.all_to_all(send, 'expert', split_axis=0, concat_axis=0, tiled=True)]
    ppermute x0 -> x11, waiting for transfers between devices: none -> 58.6 us  [the longest x1 30.7 us: per_device(): column.append(lax.ppermute(right, 'expert', ups))]
    ppermute x0 -> x11, starting transfers between devices: none -> 18.4 us  [the longest x3 13.2 us: per_device(): left = lax.ppermute(left, 'expert', downs)]
    unnamed x11 -> x61, local copies, waits for them, and re-layouts: 5.79 us -> 18.5 us
    pallas_call x2 -> x7, Pallas kernels: 18.3 us -> 25 us  [the longest x1 12.9 us: over(): pl.pallas_call(over_kernel, grid_spec=pltpu.PrefetchScalarGridSpec(num_sc...]
    all_to_all x0 -> x1, starting transfers between devices: none -> 4.75 us  [per_device(): lax.all_to_all(send, 'expert', split_axis=0, concat_axis=0, tiled=True)]
    ppermute x7, waiting for transfers between devices: 54.2 us -> 56.9 us  [per_device(): came = lax.ppermute(part, 'dp', [(i, partner(i, s)) for i in range(groups)])]
  transfers between devices with their start and end apart: 9 -> 21, of which waited for: 5 -> 13; matrix products, arithmetic and copies ran while one was open for 1% -> 1% of each run, Pallas kernels for 5% -> 11%
where the time goes in v2:
time: 228 us; the launch traced here: 226 us
  waiting for transfers between devices  120 us (53%)
  starting transfers between devices  42.8 us (19%)
  Pallas kernels  35.8 us (16%)
  local copies, waits for them, and re-layouts  21.4 us (9%)
  matrix products  3.29 us (1%)
    ppermute x7, waiting for transfers between devices, per_device(): came = lax.ppermute(part, 'dp', [(i, partner(i, s)) for i in range(groups)])  56.9 us
    ppermute x1, waiting for transfers between devices, per_device(): column.append(lax.ppermute(right, 'expert', ups))  30.7 us
    ppermute x3, waiting for transfers between devices, per_device(): left = lax.ppermute(left, 'expert', downs)  20.3 us
    unnamed x61, local copies, waits for them, and re-layouts  18.5 us
    ppermute x7, starting transfers between devices, per_device(): came = lax.ppermute(part, 'dp', [(i, partner(i, s)) for i in range(groups)])  14.3 us
    ppermute x3, starting transfers between devices, per_device(): left = lax.ppermute(left, 'expert', downs)  13.2 us
    pallas_call x1, Pallas kernels, over(): pl.pallas_call(over_kernel, grid_spec=pltpu.PrefetchScalarGridSpec(num_sc...  12.9 us
    pallas_call x1, Pallas kernels, direct(): pl.pallas_call(direct_kernel, grid=(steps,), in_specs=[pl.BlockSpec((DIRE...  7.58 us
  transfers between devices with their start and end apart: 21, of which 13 were waited for; matrix products, arithmetic and copies ran while one was open for 1% of the time, Pallas kernels for 11%

profile of v2, /device:TPU:14, one launch (start us, length us, event | category | flops | bytes accessed | tf_op | source)
XLA Modules:
  0.0 225.8 jit_solution(14561924585907579479)
XLA Ops:
  1.6 1.1 reshape.24.grads_ref
  3.8 2.3 %pack.1 = (s32[1,128]{1,0:T(1,128)S(1)}, bf16[768,128]{1,0:T(8,128)(2,1)S(1)}, bf16[256,2816]{1,0:T(8,128)(2,1)}, bf16[64,2816]{1,0:T(8,128)(2,1)S(1)}) custom-call(s32[1]{0:T(128)} %bitcast.me_ref, s32[1,256]{1,0:T(1,128)S(1)} %reshape.23.routes_ref, bf16[128,2048]{1,0:T(8,128)(2,1)S(1)} %copy-done.29, bf16[256,768]{1,0:T(8,128)(2,1)S(1)} %reshape.24.grads_ref), custom_call_target="tpu_custom_call" | custom-call | flops 1000000000 | bytes 4194304 | tf_op jit(solution)/shard_map/pack/pallas_call | solution.py:103
  6.7 5.9 %collective-permute-start.3 = (bf16[64,2816]{1,0:T(8,128)(2,1)S(1)}, bf16[64,2816]{1,0:T(8,128)(2,1)S(1)}, u32[]{:S(2)}, u32[]{:S(2)}) collective-permute-start(bf16[64,2816]{1,0:T(8,128)(2,1)S(1)} %get-tuple-element.25.refs_0_), channel_id=1, source_target_pairs={{0,14},{1,15},{2,0},{3,1},{4,2},{5,3},{6,4},{7,5},{8,6},{9,7},{10,... | collective-permute-start | bytes 1081352 | tf_op jit(solution)/shard_map/ppermute | solution.py:441
  12.6 7.7 %collective-permute-done.3.refs_2_ = bf16[64,2816]{1,0:T(8,128)(2,1)S(1)} collective-permute-done((bf16[64,2816]{1,0:T(8,128)(2,1)S(1)}, bf16[64,2816]{1,0:T(8,128)(2,1)S(1)}, u32[]{:S(2)}, u32[]{:S(2)}) %collective-permute-start.3) | collective-permute-done | bytes 360480 | tf_op jit(solution)/shard_map/ppermute | solution.py:441
  20.3 3.7 %collective-permute-start.4 = (bf16[64,2816]{1,0:T(8,128)(2,1)S(1)}, bf16[64,2816]{1,0:T(8,128)(2,1)S(1)}, u32[]{:S(2)}, u32[]{:S(2)}) collective-permute-start(bf16[64,2816]{1,0:T(8,128)(2,1)S(1)} %collective-permute-done.3.refs_2_), channel_id=1, source_target_pairs={{0,14},{1,15},{2,0},{3,1},{4,2},{5,3},{6,4},{7,5},{8,6},{9,7},{10,... | collective-permute-start | bytes 1081352 | tf_op jit(solution)/shard_map/ppermute | solution.py:441
  24.0 6.8 %collective-permute-done.4.refs_1_.refs_4_ = bf16[64,2816]{1,0:T(8,128)(2,1)S(1)} collective-permute-done((bf16[64,2816]{1,0:T(8,128)(2,1)S(1)}, bf16[64,2816]{1,0:T(8,128)(2,1)S(1)}, u32[]{:S(2)}, u32[]{:S(2)}) %collective-permute-start.4) | collective-permute-done | bytes 360480 | tf_op jit(solution)/shard_map/ppermute | solution.py:441
  30.7 3.7 %collective-permute-start.5 = (bf16[64,2816]{1,0:T(8,128)(2,1)S(1)}, bf16[64,2816]{1,0:T(8,128)(2,1)S(1)}, u32[]{:S(2)}, u32[]{:S(2)}) collective-permute-start(bf16[64,2816]{1,0:T(8,128)(2,1)S(1)} %collective-permute-done.4.refs_1_.refs_4_), channel_id=1, source_target_pairs={{0,14},{1,15},{2,0},{3,1},{4,2},{5,3},{6,4},{7,5},{8,6},{9,7},{10,... | collective-permute-start | bytes 1081352 | tf_op jit(solution)/shard_map/ppermute | solution.py:441
  34.5 5.9 %collective-permute-done.5.refs_1_.refs_6_ = bf16[64,2816]{1,0:T(8,128)(2,1)S(1)} collective-permute-done((bf16[64,2816]{1,0:T(8,128)(2,1)S(1)}, bf16[64,2816]{1,0:T(8,128)(2,1)S(1)}, u32[]{:S(2)}, u32[]{:S(2)}) %collective-permute-start.5) | collective-permute-done | bytes 360480 | tf_op jit(solution)/shard_map/ppermute | solution.py:441
  41.1 2.7 %collective-permute-done.2.refs_0_.refs_5_ = bf16[64,2816]{1,0:T(8,128)(2,1)S(1)} collective-permute-done((bf16[64,2816]{1,0:T(8,128)(2,1)S(1)}, bf16[64,2816]{1,0:T(8,128)(2,1)S(1)}, u32[]{:S(2)}, u32[]{:S(2)}) %collective-permute-start.2) | collective-permute-done | bytes 360480 | tf_op jit(solution)/shard_map/ppermute | solution.py:440
  44.5 4.8 %all-to-all-start = ((bf16[16,16,2816]{2,1,0:T(8,128)(2,1)}), bf16[16,16,2816]{2,1,0:T(8,128)(2,1)S(1)}, u32[]{:S(2)}, u32[]{:S(2)}) async-start(bf16[16,16,2816]{2,1,0:T(8,128)(2,1)} %bitcast.1), calls=%async_computation | async-start | bytes 2883584 | tf_op jit(solution)/shard_map/all_to_all | solution.py:448
  50.0 1.9 collective-permute-start.6
  52.5 1.6 collective-permute-start.8
  57.3 30.7 %collective-permute-done.6.refs_0_.refs_7_ = bf16[64,2816]{1,0:T(8,128)(2,1)S(1)} collective-permute-done((bf16[64,2816]{1,0:T(8,128)(2,1)}, bf16[64,2816]{1,0:T(8,128)(2,1)S(1)}, u32[]{:S(2)}, u32[]{:S(2)}) %collective-permute-start.6) | collective-permute-done | bytes 360480 | tf_op jit(solution)/shard_map/ppermute | solution.py:443
  89.4 1.9 collective-permute-done.9.refs_10_
  91.4 3.0 %collective-permute-done.10.refs_11_ = bf16[32,2816]{1,0:T(8,128)(2,1)S(1)} collective-permute-done((bf16[32,2816]{1,0:T(8,128)(2,1)S(1)}, bf16[32,2816]{1,0:T(8,128)(2,1)S(1)}, u32[]{:S(2)}, u32[]{:S(2)}) %collective-permute-start.10) | collective-permute-done | bytes 180256 | tf_op jit(solution)/shard_map/ppermute | solution.py:445
  99.3 12.9 %over.1 = (bf16[512,2048]{1,0:T(8,128)(2,1)S(1)}, bf16[512,768]{1,0:T(8,128)(2,1)S(1)}, bf16[512,768]{1,0:T(8,128)(2,1)S(1)}, bf16[768,2048]{1,0:T(8,128)(2,1)}) custom-call(s32[128]{0:T(128)S(1)} %bitcast.24, bf16[64,2816]{1,0:T(8,128)(2,1)S(1)} %copy-done.12, bf16[64,2816]{1,0:T(8,128)(2,1)S(1)} %copy-done.16, bf16[64,2816]{1,0:T(8,128)(2,1)S(1)} %copy-done.14, ...), custom_call_target="tpu_custom_call" | custom-call | flops 6442450944 | bytes 17825792 | tf_op jit(solution)/shard_map/over/pallas_call | solution.py:215
  114.1 7.6 %direct.1 = (bf16[256,768]{1,0:T(8,128)(2,1)S(1)}, bf16[256,768]{1,0:T(8,128)(2,1)S(1)}, bf16[768,2048]{1,0:T(8,128)(2,1)}) custom-call(bf16[256,2816]{1,0:T(8,128)(2,1)S(1)} %bitcast.16, bf16[256,2816]{1,0:T(8,128)(2,1)S(1)} %bitcast.17, bf16[1,2048,768]{2,1,0:T(8,128)(2,1)} %wg_ref.1, ...), custom_call_target="tpu_custom_call", output_to_operand_aliasing={{2}: (4, {})} | custom-call | flops 3221225472 | bytes 10485760 | tf_op jit(solution)/shard_map/direct/pallas_call | solution.py:285
  123.1 5.3 %all-to-all-start.1 = ((bf16[16,48,2048]{2,1,0:T(8,128)(2,1)}), bf16[16,48,2048]{2,1,0:T(8,128)(2,1)}, u32[]{:S(2)}, u32[]{:S(2)}) async-start(bf16[16,48,2048]{2,1,0:T(8,128)(2,1)} %bitcast.25), calls=%async_computation.1 | async-start | bytes 6291456 | tf_op jit(solution)/shard_map/all_to_all | solution.py:451
  133.4 5.1 %weight_send.1 = bf16[1024,1536]{1,0:T(8,128)(2,1)S(1)} custom-call(s32[8]{0:T(128)S(1)} %broadcast_xor_fusion.block_ref, bf16[256,2816]{1,0:T(8,128)(2,1)S(1)} %bitcast.18, bf16[256,768]{1,0:T(8,128)(2,1)S(1)} %copy-done.6, bf16[256,768]{1,0:T(8,128)(2,1)S(1)} %copy-done.9, bf16[512,2048]{1,0:T(8,128)(2,1)S(1)} %get-tuple-element.32.refs_3_, ...), custom_call_target="tpu_custom_call" | custom-call | flops 2415919104 | bytes 8388608 | tf_op jit(solution)/shard_map/weight_send/pallas_call | solution.py:352
  139.3 4.9 %collective-permute-done.11.refs_6_ = bf16[1024,1536]{1,0:T(8,128)(2,1)S(1)} collective-permute-done((bf16[1024,1536]{1,0:T(8,128)(2,1)S(1)}, bf16[1024,1536]{1,0:T(8,128)(2,1)S(1)}, u32[]{:S(2)}, u32[]{:S(2)}) %collective-permute-start.11) | collective-permute-done | bytes 3145760 | tf_op jit(solution)/shard_map/ppermute | solution.py:458
  144.3 5.7 %weight_keep.1 = (f32[128,1536]{1,0:T(8,128)S(1)}, bf16[128,1536]{1,0:T(8,128)(2,1)S(1)}, bf16[128,1536]{1,0:T(8,128)(2,1)S(1)}, bf16[128,1536]{1,0:T(8,128)(2,1...) custom-call(s32[8]{0:T(128)S(1)} %dynamic-slice_bitcast_fusion.block, ...), custom_call_target="tpu_custom_call" | custom-call | flops 2415919104 | bytes 11534336 | tf_op jit(solution)/shard_map/weight_keep/pallas_call | solution.py:392
  150.0 1.6 collective-permute-start.12
  151.6 3.6 %collective-permute-start.13 = (bf16[128,1536]{1,0:T(8,128)(2,1)S(1)}, bf16[128,1536]{1,0:T(8,128)(2,1)S(1)}, u32[]{:S(2)}, u32[]{:S(2)}) collective-permute-start(bf16[128,1536]{1,0:T(8,128)(2,1)S(1)} %get-tuple-element.37), channel_id=1, source_target_pairs={{0,64},{16,80},{32,96},{48,112},{64,128},{80,144},{96,160},{112,17... | collective-permute-start | bytes 1179656 | tf_op jit(solution)/shard_map/ppermute | solution.py:462
  155.2 3.5 %collective-permute-start.14 = (bf16[128,1536]{1,0:T(8,128)(2,1)S(1)}, bf16[128,1536]{1,0:T(8,128)(2,1)S(1)}, u32[]{:S(2)}, u32[]{:S(2)}) collective-permute-start(bf16[128,1536]{1,0:T(8,128)(2,1)S(1)} %get-tuple-element.38), channel_id=1, source_target_pairs={{0,96},{16,112},{32,64},{48,80},{64,160},{80,176},{96,128},{112,14... | collective-permute-start | bytes 1179656 | tf_op jit(solution)/shard_map/ppermute | solution.py:462
  158.7 3.1 %collective-permute-start.16 = (bf16[128,1536]{1,0:T(8,128)(2,1)S(1)}, bf16[128,1536]{1,0:T(8,128)(2,1)S(1)}, u32[]{:S(2)}, u32[]{:S(2)}) collective-permute-start(bf16[128,1536]{1,0:T(8,128)(2,1)S(1)} %get-tuple-element.40), channel_id=1, source_target_pairs={{0,160},{16,176},{32,128},{48,144},{64,224},{80,240},{96,192},{112... | collective-permute-start | bytes 1179656 | tf_op jit(solution)/shard_map/ppermute | solution.py:462
  161.8 6.9 %collective-permute-done.12 = bf16[128,1536]{1,0:T(8,128)(2,1)S(1)} collective-permute-done((bf16[128,1536]{1,0:T(8,128)(2,1)S(1)}, bf16[128,1536]{1,0:T(8,128)(2,1)S(1)}, u32[]{:S(2)}, u32[]{:S(2)}) %collective-permute-start.12) | collective-permute-done | bytes 393248 | tf_op jit(solution)/shard_map/ppermute | solution.py:462
  168.7 2.5 %collective-permute-start.17 = (bf16[128,1536]{1,0:T(8,128)(2,1)S(1)}, bf16[128,1536]{1,0:T(8,128)(2,1)S(1)}, u32[]{:S(2)}, u32[]{:S(2)}) collective-permute-start(bf16[128,1536]{1,0:T(8,128)(2,1)S(1)} %get-tuple-element.41), channel_id=1, source_target_pairs={{0,192},{16,208},{32,224},{48,240},{64,0},{80,16},{96,32},{112,48}... | collective-permute-start | bytes 1179656 | tf_op jit(solution)/shard_map/ppermute | solution.py:462
  171.2 5.0 %collective-permute-done.13 = bf16[128,1536]{1,0:T(8,128)(2,1)S(1)} collective-permute-done((bf16[128,1536]{1,0:T(8,128)(2,1)S(1)}, bf16[128,1536]{1,0:T(8,128)(2,1)S(1)}, u32[]{:S(2)}, u32[]{:S(2)}) %collective-permute-start.13) | collective-permute-done | bytes 393248 | tf_op jit(solution)/shard_map/ppermute | solution.py:462
  176.2 24.3 %collective-permute-done.14 = bf16[128,1536]{1,0:T(8,128)(2,1)S(1)} collective-permute-done((bf16[128,1536]{1,0:T(8,128)(2,1)S(1)}, bf16[128,1536]{1,0:T(8,128)(2,1)S(1)}, u32[]{:S(2)}, u32[]{:S(2)}) %collective-permute-start.14) | collective-permute-done | bytes 393248 | tf_op jit(solution)/shard_map/ppermute | solution.py:462
  200.6 15.6 %collective-permute-done.16 = bf16[128,1536]{1,0:T(8,128)(2,1)S(1)} collective-permute-done((bf16[128,1536]{1,0:T(8,128)(2,1)S(1)}, bf16[128,1536]{1,0:T(8,128)(2,1)S(1)}, u32[]{:S(2)}, u32[]{:S(2)}) %collective-permute-start.16) | collective-permute-done | bytes 393248 | tf_op jit(solution)/shard_map/ppermute | solution.py:462
  216.2 5.0 %collective-permute-done.18 = bf16[128,1536]{1,0:T(8,128)(2,1)S(1)} collective-permute-done((bf16[128,1536]{1,0:T(8,128)(2,1)S(1)}, bf16[128,1536]{1,0:T(8,128)(2,1)S(1)}, u32[]{:S(2)}, u32[]{:S(2)}) %collective-permute-start.18) | collective-permute-done | bytes 393248 | tf_op jit(solution)/shard_map/ppermute | solution.py:462
  222.5 3.3 %convolution_convert_fusion = bf16[128,2048]{1,0:T(8,128)(2,1)} fusion(bf16[768,128]{1,0:T(8,128)(2,1)S(1)} %copy-done.28, bf16[768,2048]{1,0:T(8,128)(2,1)} %bitcast.5), kind=kOutput, calls=%fused_computation | convolution fusion | flops 402915328 | bytes 3866624 | tf_op jit(solution)/shard_map/dot_general | solution.py:464
  (87 shorter events, 25.5 us)
Async XLA Ops:
  6.7 49.9 %copy-start.11 = (bf16[64,2816]{1,0:T(8,128)(2,1)}, bf16[64,2816]{1,0:T(8,128)(2,1)S(1)}, u32[]{:S(2)}) copy-start(bf16[64,2816]{1,0:T(8,128)(2,1)S(1)} %get-tuple-element.25.refs_0_) | copy-start | bytes 1081348
  6.7 13.5 %collective-permute-start.3 = (bf16[64,2816]{1,0:T(8,128)(2,1)S(1)}, bf16[64,2816]{1,0:T(8,128)(2,1)S(1)}, u32[]{:S(2)}, u32[]{:S(2)}) collective-permute-start(bf16[64,2816]{1,0:T(8,128)(2,1)S(1)} %get-tuple-element.25.refs_0_), channel_id=1, source_target_pairs={{0,14},{1,15},{2,0},{3,1},{4,2},{5,3},{6,4},{7,5},{8,6},{9,7},{10,... | collective-permute-start | bytes 1081352 | tf_op jit(solution)/shard_map/ppermute | solution.py:441
  12.6 11.4 %collective-permute-start = (bf16[64,2816]{1,0:T(8,128)(2,1)S(1)}, bf16[64,2816]{1,0:T(8,128)(2,1)S(1)}, u32[]{:S(2)}, u32[]{:S(2)}) collective-permute-start(bf16[64,2816]{1,0:T(8,128)(2,1)S(1)} %get-tuple-element.25.refs_0_), channel_id=1, source_target_pairs={{0,2},{1,3},{2,4},{3,5},{4,6},{5,7},{6,8},{7,9},{8,10},{9,11},{10,... | collective-permute-start | bytes 1081352 | tf_op jit(solution)/shard_map/ppermute | solution.py:440
  20.3 36.4 %copy-start.13 = (bf16[64,2816]{1,0:T(8,128)(2,1)}, bf16[64,2816]{1,0:T(8,128)(2,1)S(1)}, u32[]{:S(2)}) copy-start(bf16[64,2816]{1,0:T(8,128)(2,1)S(1)} %collective-permute-done.3.refs_2_) | copy-start | bytes 1081348
  20.3 10.5 %collective-permute-start.4 = (bf16[64,2816]{1,0:T(8,128)(2,1)S(1)}, bf16[64,2816]{1,0:T(8,128)(2,1)S(1)}, u32[]{:S(2)}, u32[]{:S(2)}) collective-permute-start(bf16[64,2816]{1,0:T(8,128)(2,1)S(1)} %collective-permute-done.3.refs_2_), channel_id=1, source_target_pairs={{0,14},{1,15},{2,0},{3,1},{4,2},{5,3},{6,4},{7,5},{8,6},{9,7},{10,... | collective-permute-start | bytes 1081352 | tf_op jit(solution)/shard_map/ppermute | solution.py:441
  24.0 32.7 %copy-start.15 = (bf16[64,2816]{1,0:T(8,128)(2,1)}, bf16[64,2816]{1,0:T(8,128)(2,1)S(1)}, u32[]{:S(2)}) copy-start(bf16[64,2816]{1,0:T(8,128)(2,1)S(1)} %collective-permute-done.refs_1_) | copy-start | bytes 1081348
  24.0 10.5 %collective-permute-start.1 = (bf16[64,2816]{1,0:T(8,128)(2,1)S(1)}, bf16[64,2816]{1,0:T(8,128)(2,1)S(1)}, u32[]{:S(2)}, u32[]{:S(2)}) collective-permute-start(bf16[64,2816]{1,0:T(8,128)(2,1)S(1)} %collective-permute-done.refs_1_), channel_id=1, source_target_pairs={{0,2},{1,3},{2,4},{3,5},{4,6},{5,7},{6,8},{7,9},{8,10},{9,11},{10,... | collective-permute-start | bytes 1081352 | tf_op jit(solution)/shard_map/ppermute | solution.py:440
  30.7 25.9 %copy-start.17 = (bf16[64,2816]{1,0:T(8,128)(2,1)}, bf16[64,2816]{1,0:T(8,128)(2,1)S(1)}, u32[]{:S(2)}) copy-start(bf16[64,2816]{1,0:T(8,128)(2,1)S(1)} %collective-permute-done.4.refs_1_.refs_4_) | copy-start | bytes 1081348
  30.7 9.6 %collective-permute-start.5 = (bf16[64,2816]{1,0:T(8,128)(2,1)S(1)}, bf16[64,2816]{1,0:T(8,128)(2,1)S(1)}, u32[]{:S(2)}, u32[]{:S(2)}) collective-permute-start(bf16[64,2816]{1,0:T(8,128)(2,1)S(1)} %collective-permute-done.4.refs_1_.refs_4_), channel_id=1, source_target_pairs={{0,14},{1,15},{2,0},{3,1},{4,2},{5,3},{6,4},{7,5},{8,6},{9,7},{10,... | collective-permute-start | bytes 1081352 | tf_op jit(solution)/shard_map/ppermute | solution.py:441
  34.4 22.2 %copy-start.19 = (bf16[64,2816]{1,0:T(8,128)(2,1)}, bf16[64,2816]{1,0:T(8,128)(2,1)S(1)}, u32[]{:S(2)}) copy-start(bf16[64,2816]{1,0:T(8,128)(2,1)S(1)} %collective-permute-done.1.refs_0_.refs_3_) | copy-start | bytes 1081348
  34.4 9.3 %collective-permute-start.2 = (bf16[64,2816]{1,0:T(8,128)(2,1)S(1)}, bf16[64,2816]{1,0:T(8,128)(2,1)S(1)}, u32[]{:S(2)}, u32[]{:S(2)}) collective-permute-start(bf16[64,2816]{1,0:T(8,128)(2,1)S(1)} %collective-permute-done.1.refs_0_.refs_3_), channel_id=1, source_target_pairs={{0,2},{1,3},{2,4},{3,5},{4,6},{5,7},{6,8},{7,9},{8,10},{9,11},{10,... | collective-permute-start | bytes 1081352 | tf_op jit(solution)/shard_map/ppermute | solution.py:440
  44.5 69.6 %all-to-all-start = ((bf16[16,16,2816]{2,1,0:T(8,128)(2,1)}), bf16[16,16,2816]{2,1,0:T(8,128)(2,1)S(1)}, u32[]{:S(2)}, u32[]{:S(2)}) async-start(bf16[16,16,2816]{2,1,0:T(8,128)(2,1)} %bitcast.1), calls=%async_computation | async-start | bytes 2883584 | tf_op jit(solution)/shard_map/all_to_all | solution.py:448
  49.2 45.1 %copy-start.23 = (bf16[64,2816]{1,0:T(8,128)(2,1)S(1)}, bf16[64,2816]{1,0:T(8,128)(2,1)}, u32[]{:S(2)}) copy-start(bf16[64,2816]{1,0:T(8,128)(2,1)} %copy-done.21) | copy-start | bytes 1081348
  49.2 45.1 %copy-start.26 = (bf16[64,2816]{1,0:T(8,128)(2,1)S(1)}, bf16[64,2816]{1,0:T(8,128)(2,1)}, u32[]{:S(2)}) copy-start(bf16[64,2816]{1,0:T(8,128)(2,1)} %copy-done.24) | copy-start | bytes 1081348
  49.8 39.6 %collective-permute-start.7 = (bf16[96,2816]{1,0:T(8,128)(2,1)S(1)}, bf16[96,2816]{1,0:T(8,128)(2,1)S(1)}, u32[]{:S(2)}, u32[]{:S(2)}) collective-permute-start(bf16[96,2816]{1,0:T(8,128)(2,1)S(1)} %choose.4), channel_id=1, source_target_pairs={{0,1},{1,0},{2,3},{3,2},{4,5},{5,4},{6,7},{7,6},{8,9},{9,8},{10,11... | collective-permute-start | bytes 1622024 | tf_op jit(solution)/shard_map/ppermute | solution.py:445
  50.0 38.0 %collective-permute-start.6 = (bf16[64,2816]{1,0:T(8,128)(2,1)}, bf16[64,2816]{1,0:T(8,128)(2,1)S(1)}, u32[]{:S(2)}, u32[]{:S(2)}) collective-permute-start(bf16[64,2816]{1,0:T(8,128)(2,1)} %copy-done.24), channel_id=1, source_target_pairs={{0,2},{1,3},{2,4},{3,5},{4,6},{5,7},{6,8},{7,9},{8,10},{9,11},{10,... | collective-permute-start | bytes 1081352 | tf_op jit(solution)/shard_map/ppermute | solution.py:443
  52.5 36.9 %collective-permute-start.8 = (bf16[64,2816]{1,0:T(8,128)(2,1)S(1)}, bf16[64,2816]{1,0:T(8,128)(2,1)S(1)}, u32[]{:S(2)}, u32[]{:S(2)}) collective-permute-start(bf16[64,2816]{1,0:T(8,128)(2,1)S(1)} %choose.5), channel_id=1, source_target_pairs={{0,1},{1,0},{2,3},{3,2},{4,5},{5,4},{6,7},{7,6},{8,9},{9,8},{10,11... | collective-permute-start | bytes 1081352 | tf_op jit(solution)/shard_map/ppermute | solution.py:445
  56.7 34.7 %collective-permute-start.9 = (bf16[64,2816]{1,0:T(8,128)(2,1)S(1)}, bf16[64,2816]{1,0:T(8,128)(2,1)S(1)}, u32[]{:S(2)}, u32[]{:S(2)}) collective-permute-start(bf16[64,2816]{1,0:T(8,128)(2,1)S(1)} %choose.6), channel_id=1, source_target_pairs={{0,1},{1,0},{2,3},{3,2},{4,5},{5,4},{6,7},{7,6},{8,9},{9,8},{10,11... | collective-permute-start | bytes 1081352 | tf_op jit(solution)/shard_map/ppermute | solution.py:445
  88.6 5.8 %collective-permute-start.10 = (bf16[32,2816]{1,0:T(8,128)(2,1)S(1)}, bf16[32,2816]{1,0:T(8,128)(2,1)S(1)}, u32[]{:S(2)}, u32[]{:S(2)}) collective-permute-start(bf16[32,2816]{1,0:T(8,128)(2,1)S(1)} %choose.7), channel_id=1, source_target_pairs={{0,1},{1,0},{2,3},{3,2},{4,5},{5,4},{6,7},{7,6},{8,9},{9,8},{10,11... | collective-permute-start | bytes 540680 | tf_op jit(solution)/shard_map/ppermute | solution.py:445
  123.1 99.4 %all-to-all-start.1 = ((bf16[16,48,2048]{2,1,0:T(8,128)(2,1)}), bf16[16,48,2048]{2,1,0:T(8,128)(2,1)}, u32[]{:S(2)}, u32[]{:S(2)}) async-start(bf16[16,48,2048]{2,1,0:T(8,128)(2,1)} %bitcast.25), calls=%async_computation.1 | async-start | bytes 6291456 | tf_op jit(solution)/shard_map/all_to_all | solution.py:451
  133.4 10.8 %copy-start.2 = (bf16[512,768]{1,0:T(8,128)(2,1)S(1)}, bf16[512,768]{1,0:T(8,128)(2,1)}, u32[]{:S(2)}) copy-start(bf16[512,768]{1,0:T(8,128)(2,1)} %copy-done) | copy-start | bytes 2359300
  133.4 10.8 %copy-start.7 = (bf16[256,768]{1,0:T(8,128)(2,1)S(1)}, bf16[256,768]{1,0:T(8,128)(2,1)}, u32[]{:S(2)}) copy-start(bf16[256,768]{1,0:T(8,128)(2,1)} %copy-done.5) | copy-start | bytes 1179652
  133.4 10.8 %copy-start.10 = (bf16[256,768]{1,0:T(8,128)(2,1)S(1)}, bf16[256,768]{1,0:T(8,128)(2,1)}, u32[]{:S(2)}) copy-start(bf16[256,768]{1,0:T(8,128)(2,1)} %copy-done.8) | copy-start | bytes 1179652
  138.5 5.7 %collective-permute-start.11 = (bf16[1024,1536]{1,0:T(8,128)(2,1)S(1)}, bf16[1024,1536]{1,0:T(8,128)(2,1)S(1)}, u32[]{:S(2)}, u32[]{:S(2)}) collective-permute-start(bf16[1024,1536]{1,0:T(8,128)(2,1)S(1)} %weight_send.1), channel_id=1, source_target_pairs={{0,16},{16,0},{32,48},{48,32},{64,80},{80,64},{96,112},{112,96},{1... | collective-permute-start | bytes 9437192 | tf_op jit(solution)/shard_map/ppermute | solution.py:458
  150.0 72.5 %copy-start.28 = (bf16[768,128]{1,0:T(8,128)(2,1)S(1)}, bf16[768,128]{1,0:T(8,128)(2,1)}, u32[]{:S(2)}) copy-start(bf16[768,128]{1,0:T(8,128)(2,1)} %copy-done.27) | copy-start | bytes 589828
  150.0 18.7 %collective-permute-start.12 = (bf16[128,1536]{1,0:T(8,128)(2,1)S(1)}, bf16[128,1536]{1,0:T(8,128)(2,1)S(1)}, u32[]{:S(2)}, u32[]{:S(2)}) collective-permute-start(bf16[128,1536]{1,0:T(8,128)(2,1)S(1)} %get-tuple-element.36), channel_id=1, source_target_pairs={{0,32},{16,48},{32,0},{48,16},{64,96},{80,112},{96,64},{112,80},{1... | collective-permute-start | bytes 1179656 | tf_op jit(solution)/shard_map/ppermute | solution.py:462
  151.6 24.6 %collective-permute-start.13 = (bf16[128,1536]{1,0:T(8,128)(2,1)S(1)}, bf16[128,1536]{1,0:T(8,128)(2,1)S(1)}, u32[]{:S(2)}, u32[]{:S(2)}) collective-permute-start(bf16[128,1536]{1,0:T(8,128)(2,1)S(1)} %get-tuple-element.37), channel_id=1, source_target_pairs={{0,64},{16,80},{32,96},{48,112},{64,128},{80,144},{96,160},{112,17... | collective-permute-start | bytes 1179656 | tf_op jit(solution)/shard_map/ppermute | solution.py:462
  155.2 45.4 %collective-permute-start.14 = (bf16[128,1536]{1,0:T(8,128)(2,1)S(1)}, bf16[128,1536]{1,0:T(8,128)(2,1)S(1)}, u32[]{:S(2)}, u32[]{:S(2)}) collective-permute-start(bf16[128,1536]{1,0:T(8,128)(2,1)S(1)} %get-tuple-element.38), channel_id=1, source_target_pairs={{0,96},{16,112},{32,64},{48,80},{64,160},{80,176},{96,128},{112,14... | collective-permute-start | bytes 1179656 | tf_op jit(solution)/shard_map/ppermute | solution.py:462
  158.7 41.9 %collective-permute-start.15 = (bf16[128,1536]{1,0:T(8,128)(2,1)S(1)}, bf16[128,1536]{1,0:T(8,128)(2,1)S(1)}, u32[]{:S(2)}, u32[]{:S(2)}) collective-permute-start(bf16[128,1536]{1,0:T(8,128)(2,1)S(1)} %get-tuple-element.39), channel_id=1, source_target_pairs={{0,128},{16,144},{32,160},{48,176},{64,192},{80,208},{96,224},{112... | collective-permute-start | bytes 1179656 | tf_op jit(solution)/shard_map/ppermute | solution.py:462
  158.7 57.5 %collective-permute-start.16 = (bf16[128,1536]{1,0:T(8,128)(2,1)S(1)}, bf16[128,1536]{1,0:T(8,128)(2,1)S(1)}, u32[]{:S(2)}, u32[]{:S(2)}) collective-permute-start(bf16[128,1536]{1,0:T(8,128)(2,1)S(1)} %get-tuple-element.40), channel_id=1, source_target_pairs={{0,160},{16,176},{32,128},{48,144},{64,224},{80,240},{96,192},{112... | collective-permute-start | bytes 1179656 | tf_op jit(solution)/shard_map/ppermute | solution.py:462
  168.7 47.5 %collective-permute-start.17 = (bf16[128,1536]{1,0:T(8,128)(2,1)S(1)}, bf16[128,1536]{1,0:T(8,128)(2,1)S(1)}, u32[]{:S(2)}, u32[]{:S(2)}) collective-permute-start(bf16[128,1536]{1,0:T(8,128)(2,1)S(1)} %get-tuple-element.41), channel_id=1, source_target_pairs={{0,192},{16,208},{32,224},{48,240},{64,0},{80,16},{96,32},{112,48}... | collective-permute-start | bytes 1179656 | tf_op jit(solution)/shard_map/ppermute | solution.py:462
  176.2 44.9 %collective-permute-start.18 = (bf16[128,1536]{1,0:T(8,128)(2,1)S(1)}, bf16[128,1536]{1,0:T(8,128)(2,1)S(1)}, u32[]{:S(2)}, u32[]{:S(2)}) collective-permute-start(bf16[128,1536]{1,0:T(8,128)(2,1)S(1)} %get-tuple-element.42), channel_id=1, source_target_pairs={{0,224},{16,240},{32,192},{48,208},{64,32},{80,48},{96,0},{112,16}... | collective-permute-start | bytes 1179656 | tf_op jit(solution)/shard_map/ppermute | solution.py:462
  (19 other events, 17.7 us)

commit v3 on v2

--- a/solution.py
+++ b/solution.py
@@ -19,13 +19,23 @@
 OVER = EXPERTS * SPILL
 WIDTH = D + FF
 OFFSETS = (0, -1, 1, -2, 2, -3, 3, 4)
-PIECES = ((0, 3), (3, 5), (5, 7), (7, 8))
+PIECES = ((0, 3), (3, 5))
+SLOT_ME, HOT_ME, SLOT_BESIDE, ME = range(4)
+HOPS = ((0, 1, False), (1, -1, False), (0, 2, False), (0, 1, True), (1, -1, True), (1, -2, True))
+SLOT_HOP = 4
 BLOCK = 128
 FF_BLOCK = 256
 MIB = 1 << 20
 
 
-def pack_kernel(me_ref, routes_ref, tokens_ref, grads_ref, choice_ref, sel_ref, out_ref, over_ref):
+def target(expert, step, crosses):
+    there = (expert + 2 * step + EXPERTS) % EXPERTS
+    return there + 1 - 2 * (there % 2) if crosses else there
+
+
+def pack_kernel(
+    me_ref, routes_ref, tokens_ref, grads_ref, choice_ref, sel_ref, out_ref, over_ref
+):
     pairs = routes_ref.shape[1]
     toks = tokens_ref.shape[0]
     me = me_ref[0]
@@ -57,21 +67,26 @@
     which = jnp.sum(member * which_col, axis=0, keepdims=True).astype(jnp.int32)
 
     lane16 = lax.broadcasted_iota(jnp.int32, (1, EXPERTS), 1)
-    mine = (lane16 == me).astype(jnp.float32)
-    beside = (lane16 == me + 1 - 2 * (me % 2)).astype(jnp.float32)
-    hot_me = jnp.sum(mine * hot_row, axis=1, keepdims=True)
-    slot_me = jnp.sum(mine * hot_row * which_row, axis=1, keepdims=True)
-    slot_beside = jnp.sum(beside * hot_row * which_row, axis=1, keepdims=True)
+
+    def at_expert(expert, row):
+        return jnp.sum(
+            jnp.where(lane16 == expert, row, 0.0), axis=1, keepdims=True
+        ).astype(jnp.int32)
+
+    slots = hot_row * which_row
+    values = {
+        SLOT_ME: at_expert(me, slots),
+        HOT_ME: at_expert(me, hot_row),
+        SLOT_BESIDE: at_expert(target(me, 0, True), slots),
+        ME: me,
+    }
+    for k, (_, step, crosses) in enumerate(HOPS):
+        values[SLOT_HOP + k] = at_expert(target(me, step, crosses), slots)
     lane = lax.broadcasted_iota(jnp.int32, (1, 128), 1)
-    choice_ref[...] = jnp.where(
-        lane == 0,
-        slot_me.astype(jnp.int32),
-        jnp.where(
-            lane == 1,
-            hot_me.astype(jnp.int32),
-            jnp.where(lane == 2, slot_beside.astype(jnp.int32), me),
-        ),
-    )
+    choice = jnp.zeros((1, 128), jnp.int32)
+    for at, value in values.items():
+        choice = jnp.where(lane == at, value, choice)
+    choice_ref[...] = choice
 
     to_token = (
         lax.broadcasted_iota(jnp.int32, (pairs, toks), 0) // 2
@@ -128,7 +143,7 @@
         grid_spec=pltpu.PrefetchScalarGridSpec(
             num_scalar_prefetch=1,
             grid=(1,),
-            in_specs=[pl.BlockSpec((SPILL, WIDTH), lambda i, c: (c[2], 0))] * count,
+            in_specs=[pl.BlockSpec((SPILL, WIDTH), lambda i, c: (c[SLOT_BESIDE], 0))] * count,
             out_specs=pl.BlockSpec((count * SPILL, WIDTH), lambda i, c: (0, 0)),
         ),
         out_shape=jax.ShapeDtypeStruct((count * SPILL, WIDTH), jnp.bfloat16),
@@ -138,6 +153,32 @@
         ),
         name="choose",
     )(choice, *blocks)
+
+
+def hop_kernel(choice_ref, *refs):
+    for k in range(len(HOPS)):
+        refs[len(HOPS) + k][...] = refs[k][...]
+
+
+def hop_rows(choice, blocks):
+    return pl.pallas_call(
+        hop_kernel,
+        grid_spec=pltpu.PrefetchScalarGridSpec(
+            num_scalar_prefetch=1,
+            grid=(1,),
+            in_specs=[
+                pl.BlockSpec((SPILL, WIDTH), lambda i, c, k=k: (c[SLOT_HOP + k], 0))
+                for k in range(len(HOPS))
+            ],
+            out_specs=[pl.BlockSpec((SPILL, WIDTH), lambda i, c: (0, 0))] * len(HOPS),
+        ),
+        out_shape=[jax.ShapeDtypeStruct((SPILL, WIDTH), jnp.bfloat16)] * len(HOPS),
+        compiler_params=pltpu.CompilerParams(vmem_limit_bytes=6 * MIB),
+        cost_estimate=pl.CostEstimate(
+            flops=0, bytes_accessed=4 * len(HOPS) * SPILL * WIDTH, transcendentals=0
+        ),
+        name="hop_rows",
+    )(choice, *[blocks[from_above] for from_above, _, _ in HOPS])
 
 
 def deltas(x, dh, wg, wu):
@@ -147,28 +188,28 @@
     wide = dh.astype(jnp.float32)
     delta_g = (wide * up * sig * (1.0 + gate * (1.0 - sig))).astype(jnp.bfloat16)
     delta_u = (wide * gate * sig).astype(jnp.bfloat16)
+    return delta_g, delta_u
+
+
+def back_rows(delta_g, delta_u, wg, wu):
     dims = (((1,), (1,)), ((), ()))
-    part = lax.dot_general(
+    return lax.dot_general(
         delta_g, wg, dims, preferred_element_type=jnp.float32
     ) + lax.dot_general(delta_u, wu, dims, preferred_element_type=jnp.float32)
-    return delta_g, delta_u, part
 
 
 def over_kernel(choice_ref, *refs):
-    column = refs[:8]
-    pieces = refs[8 : 8 + len(PIECES)]
-    wg_ref, wu_ref, x_ref, delta_g_ref, delta_u_ref, back_ref, acc_ref, dh_ref = refs[
-        8 + len(PIECES) :
-    ]
+    inputs = 5 + len(PIECES) + len(HOPS)
+    wg_ref, wu_ref, x_ref, delta_g_ref, delta_u_ref, back_ref, acc_ref, dh_ref = refs[inputs:]
     j = pl.program_id(0)
     last = pl.num_programs(0) - 1
-    hot = choice_ref[1] == 1
+    hot = choice_ref[HOT_ME] == 1
 
     @pl.when(j == 0)
     def _():
         back_ref[...] = jnp.zeros_like(back_ref)
         at = 0
-        for ref in (*column, *pieces):
+        for ref in refs[:inputs]:
             rows = ref.shape[0]
             x_ref[at : at + rows, :] = ref[:, :D]
             for k in range(FF // FF_BLOCK):
@@ -184,9 +225,10 @@
 
     @pl.when(hot)
     def _():
-        delta_g, delta_u, part = deltas(x_ref[...], dh_ref[j], wg_ref[0], wu_ref[0])
+        delta_g, delta_u = deltas(x_ref[...], dh_ref[j], wg_ref[0], wu_ref[0])
         delta_g_ref[...] = delta_g
         delta_u_ref[...] = delta_u
+        part = back_rows(delta_g, delta_u, wg_ref[0], wu_ref[0])
 
         @pl.when(j == 0)
         def _():
@@ -199,7 +241,7 @@
         @pl.when(j == last)
         def _():
             acc_ref[...] += part
-            me = choice_ref[3]
+            me = choice_ref[ME]
             for k in range(2 * len(OFFSETS)):
                 source = (me + 2 * OFFSETS[k % 8] + EXPERTS) % EXPERTS
                 if k >= 8:
@@ -210,15 +252,19 @@
                 ].astype(jnp.bfloat16)
 
 
-def over(choice, column, pieces, w_gate, w_up):
+def over(choice, column, rest, w_gate, w_up):
     steps = FF // FF_BLOCK
+
+    def whole(a):
+        return pl.BlockSpec(a.shape, lambda j, c: (0, 0))
+
     return pl.pallas_call(
         over_kernel,
         grid_spec=pltpu.PrefetchScalarGridSpec(
             num_scalar_prefetch=1,
             grid=(steps,),
-            in_specs=[pl.BlockSpec((SPILL, WIDTH), lambda j, c: (c[0], 0))] * len(column)
-            + [pl.BlockSpec(p.shape, lambda j, c: (0, 0)) for p in pieces]
+            in_specs=[pl.BlockSpec((SPILL, WIDTH), lambda j, c: (c[SLOT_ME], 0))] * len(column)
+            + [whole(a) for a in rest]
             + [pl.BlockSpec((1, D, FF_BLOCK), lambda j, c: (0, 0, j))] * 2,
             out_specs=[
                 pl.BlockSpec((OVER, D), lambda j, c: (0, 0)),
@@ -242,14 +288,15 @@
             flops=8 * OVER * D * FF, bytes_accessed=17 * MIB, transcendentals=OVER * FF
         ),
         name="over",
-    )(choice, *column, *pieces, w_gate, w_up)
+    )(choice, *column, *rest, w_gate, w_up)
 
 
 def direct_kernel(
     x_ref, dh_ref, wg_ref, wu_ref, old_ref, delta_g_ref, delta_u_ref, back_ref, acc_ref, low_ref, sems
 ):
     j = pl.program_id(0)
-    delta_g, delta_u, part = deltas(x_ref[...], dh_ref[...], wg_ref[0], wu_ref[0])
+    delta_g, delta_u = deltas(x_ref[...], dh_ref[...], wg_ref[0], wu_ref[0])
+    part = back_rows(delta_g, delta_u, wg_ref[0], wu_ref[0])
     delta_g_ref[...] = delta_g
     delta_u_ref[...] = delta_u
     last = pl.num_programs(0) - 1
@@ -434,19 +481,24 @@
     ups = [(e, (e + 2) % EXPERTS) for e in range(EXPERTS)]
     downs = [(e, (e - 2) % EXPERTS) for e in range(EXPERTS)]
     beside = [(e, e ^ 1) for e in range(EXPERTS)]
+
     column = [spill]
     right = left = spill
-    for _ in range(3):
+    for _ in range(2):
         right = lax.ppermute(right, "expert", ups)
         left = lax.ppermute(left, "expert", downs)
         column += [right, left]
-    column.append(lax.ppermute(right, "expert", ups))
-    pieces = [
-        lax.ppermute(choose(choice, column[a:b]), "expert", beside) for a, b in PIECES
+    hops = [
+        lax.ppermute(
+            block, "expert", [(e, target(e, step, crosses)) for e in range(EXPERTS)]
+        )
+        for block, (_, step, crosses) in zip(hop_rows(choice, (right, left)), HOPS)
     ]
-    send, right, left = lax.optimization_barrier((send, right, left))
+    pieces = [lax.ppermute(choose(choice, column[a:b]), "expert", beside) for a, b in PIECES]
+    rest = [*hops[:3], *pieces, *hops[3:]]
+    send, *rest = lax.optimization_barrier((send, *rest))
     got = lax.all_to_all(send, "expert", split_axis=0, concat_axis=0, tiled=True)
-    over_x, over_g, over_u, back = over(choice, column, pieces, w_gate, w_up)
+    over_x, over_g, over_u, back = over(choice, column, rest, w_gate, w_up)
     delta_g, delta_u, back = direct(got, w_gate, w_up, back)
     returned = lax.all_to_all(back, "expert", split_axis=0, concat_axis=0, tiled=True)
     rows = (got, delta_g, delta_u, over_x, over_g, over_u)

time: 228 us -> 209 us (0.917)
  waiting for transfers between devices: 120 us -> 103 us
  local copies, waits for them, and re-layouts: 21.4 us -> 30.4 us
  Pallas kernels: 35.8 us -> 28.5 us
    ppermute x1 -> x6, waiting for transfers between devices: 30.7 us -> 11.2 us  [per_device(): lax.ppermute(block, 'expert', [(e, target(e, step, crosses)) for e in ran...]
    all_to_all x1, waiting for transfers between devices: 0.01 us -> 12.1 us  [per_device(): lax.all_to_all(send, 'expert', split_axis=0, concat_axis=0, tiled=True)]
    unnamed x61 -> x81, local copies, waits for them, and re-layouts: 18.5 us -> 27.5 us
    ppermute x3 -> x2, starting transfers between devices: 13.2 us -> 6.15 us  [per_device(): left = lax.ppermute(left, 'expert', downs)]
    pallas_call x1, Pallas kernels: 12.9 us -> 5.96 us  [over(): pl.pallas_call(over_kernel, grid_spec=pltpu.PrefetchScalarGridSpec(num_sc...]
    ppermute x3 -> x2, waiting for transfers between devices: 20.3 us -> 14.3 us  [per_device(): left = lax.ppermute(left, 'expert', downs)]
    ppermute x4 -> x2, waiting for transfers between devices: 4.93 us -> 0.01 us  [per_device(): lax.ppermute(choose(choice, column[a:b]), 'expert', beside)]
    ppermute x1 -> x6, starting transfers between devices: 1.92 us -> 6.09 us  [per_device(): lax.ppermute(block, 'expert', [(e, target(e, step, crosses)) for e in ran...]
  transfers between devices with their start and end apart: 21 -> 22, of which waited for: 13 -> 14; matrix products, arithmetic and copies ran while one was open for 1% -> 1% of each run, Pallas kernels for 11% -> 9%
where the time goes in v3:
time: 209 us; the launch traced here: 208 us
  waiting for transfers between devices  103 us (49%)
  starting transfers between devices  40.9 us (20%)
  local copies, waits for them, and re-layouts  30.4 us (15%)
  Pallas kernels  28.5 us (14%)
  matrix products  3.29 us (2%)
    ppermute x7, waiting for transfers between devices, per_device(): came = lax.ppermute(part, 'dp', [(i, partner(i, s)) for i in range(groups)])  55.2 us
    unnamed x81, local copies, waits for them, and re-layouts  27.5 us
    ppermute x2, waiting for transfers between devices, per_device(): left = lax.ppermute(left, 'expert', downs)  14.3 us
    ppermute x7, starting transfers between devices, per_device(): came = lax.ppermute(part, 'dp', [(i, partner(i, s)) for i in range(groups)])  12.6 us
    all_to_all x1, waiting for transfers between devices, per_device(): lax.all_to_all(send, 'expert', split_axis=0, concat_axis=0, tiled=True)  12.1 us
    ppermute x6, waiting for transfers between devices, per_device(): lax.ppermute(block, 'expert', [(e, target(e, step, crosses)) for e in ran...  11.2 us
    pallas_call x1, Pallas kernels, direct(): pl.pallas_call(direct_kernel, grid=(steps,), in_specs=[pl.BlockSpec((DIRE...  7.58 us
    all_to_all x1, starting transfers between devices, per_device(): lax.all_to_all(send, 'expert', split_axis=0, concat_axis=0, tiled=True)  6.61 us
  transfers between devices with their start and end apart: 22, of which 14 were waited for; matrix products, arithmetic and copies ran while one was open for 1% of the time, Pallas kernels for 9%

profile of v3, /device:TPU:14, one launch (start us, length us, event | category | flops | bytes accessed | tf_op | source)
XLA Modules:
  0.0 207.7 jit_solution(1124714829738777159)
XLA Ops:
  1.6 1.1 reshape.24.grads_ref
  3.8 2.3 %pack.1 = (s32[1,128]{1,0:T(1,128)S(1)}, bf16[768,128]{1,0:T(8,128)(2,1)S(1)}, bf16[256,2816]{1,0:T(8,128)(2,1)}, bf16[64,2816]{1,0:T(8,128)(2,1)S(1)}) custom-call(s32[1]{0:T(128)} %bitcast.me_ref, s32[1,256]{1,0:T(1,128)S(1)} %reshape.23.routes_ref, bf16[128,2048]{1,0:T(8,128)(2,1)S(1)} %copy-done.25, bf16[256,768]{1,0:T(8,128)(2,1)S(1)} %reshape.24.grads_ref), custom_call_target="tpu_custom_call" | custom-call | flops 1000000000 | bytes 4194304 | tf_op jit(solution)/shard_map/pack/pallas_call | solution.py:118
  6.0 5.9 %collective-permute-start.2 = (bf16[64,2816]{1,0:T(8,128)(2,1)S(1)}, bf16[64,2816]{1,0:T(8,128)(2,1)S(1)}, u32[]{:S(2)}, u32[]{:S(2)}) collective-permute-start(bf16[64,2816]{1,0:T(8,128)(2,1)S(1)} %get-tuple-element.40.refs_0_), channel_id=1, source_target_pairs={{0,14},{1,15},{2,0},{3,1},{4,2},{5,3},{6,4},{7,5},{8,6},{9,7},{10,... | collective-permute-start | bytes 1081352 | tf_op jit(solution)/shard_map/ppermute | solution.py:489
  11.9 7.7 %collective-permute-done.2.refs_2_ = bf16[64,2816]{1,0:T(8,128)(2,1)S(1)} collective-permute-done((bf16[64,2816]{1,0:T(8,128)(2,1)S(1)}, bf16[64,2816]{1,0:T(8,128)(2,1)S(1)}, u32[]{:S(2)}, u32[]{:S(2)}) %collective-permute-start.2) | collective-permute-done | bytes 360480 | tf_op jit(solution)/shard_map/ppermute | solution.py:489
  19.6 3.4 %collective-permute-done.refs_1_ = bf16[64,2816]{1,0:T(8,128)(2,1)S(1)} collective-permute-done((bf16[64,2816]{1,0:T(8,128)(2,1)S(1)}, bf16[64,2816]{1,0:T(8,128)(2,1)S(1)}, u32[]{:S(2)}, u32[]{:S(2)}) %collective-permute-start) | collective-permute-done | bytes 360480 | tf_op jit(solution)/shard_map/ppermute | solution.py:488
  24.8 1.7 collective-permute-start.1
  26.5 6.6 %collective-permute-done.3.refs_1_.refs_4_.refs_5_ = bf16[64,2816]{1,0:T(8,128)(2,1)S(1)} collective-permute-done((bf16[64,2816]{1,0:T(8,128)(2,1)S(1)}, bf16[64,2816]{1,0:T(8,128)(2,1)S(1)}, u32[]{:S(2)}, u32[]{:S(2)}) %collective-permute-start.3) | collective-permute-done | bytes 360480 | tf_op jit(solution)/shard_map/ppermute | solution.py:489
  33.2 1.5 collective-permute-done.1.refs_0_.refs_2_.refs_3_
  35.6 3.0 %collective-permute-start.5 = (bf16[32,2816]{1,0:T(8,128)(2,1)S(1)}, bf16[32,2816]{1,0:T(8,128)(2,1)S(1)}, u32[]{:S(2)}, u32[]{:S(2)}) collective-permute-start(bf16[32,2816]{1,0:T(8,128)(2,1)S(1)} %get-tuple-element.42), channel_id=1, source_target_pairs={{0,14},{1,15},{2,0},{3,1},{4,2},{5,3},{6,4},{7,5},{8,6},{9,7},{10,... | collective-permute-start | bytes 540680 | tf_op jit(solution)/shard_map/ppermute | solution.py:492
  39.2 1.3 collective-permute-start.8
  41.4 4.6 %collective-permute-done.4.refs_5_ = bf16[32,2816]{1,0:T(8,128)(2,1)S(1)} collective-permute-done((bf16[32,2816]{1,0:T(8,128)(2,1)S(1)}, bf16[32,2816]{1,0:T(8,128)(2,1)S(1)}, u32[]{:S(2)}, u32[]{:S(2)}) %collective-permute-start.4) | collective-permute-done | bytes 180256 | tf_op jit(solution)/shard_map/ppermute | solution.py:492
  47.3 2.8 %collective-permute-start.11 = (bf16[32,2816]{1,0:T(8,128)(2,1)S(1)}, bf16[32,2816]{1,0:T(8,128)(2,1)S(1)}, u32[]{:S(2)}, u32[]{:S(2)}) collective-permute-start(bf16[32,2816]{1,0:T(8,128)(2,1)S(1)} %get-tuple-element.46), channel_id=1, source_target_pairs={{0,13},{1,12},{2,15},{3,14},{4,1},{5,0},{6,3},{7,2},{8,5},{9,4},{1... | collective-permute-start | bytes 540680 | tf_op jit(solution)/shard_map/ppermute | solution.py:492
  51.1 3.7 %collective-permute-done.9.refs_10_ = bf16[32,2816]{1,0:T(8,128)(2,1)S(1)} collective-permute-done((bf16[32,2816]{1,0:T(8,128)(2,1)S(1)}, bf16[32,2816]{1,0:T(8,128)(2,1)S(1)}, u32[]{:S(2)}, u32[]{:S(2)}) %collective-permute-start.9) | collective-permute-done | bytes 180256 | tf_op jit(solution)/shard_map/ppermute | solution.py:492
  55.5 2.5 %collective-permute-done.10.refs_11_ = bf16[32,2816]{1,0:T(8,128)(2,1)S(1)} collective-permute-done((bf16[32,2816]{1,0:T(8,128)(2,1)S(1)}, bf16[32,2816]{1,0:T(8,128)(2,1)S(1)}, u32[]{:S(2)}, u32[]{:S(2)}) %collective-permute-start.10) | collective-permute-done | bytes 180256 | tf_op jit(solution)/shard_map/ppermute | solution.py:492
  60.1 6.6 %all-to-all-start = ((bf16[16,16,2816]{2,1,0:T(8,128)(2,1)}), bf16[16,16,2816]{2,1,0:T(8,128)(2,1)S(1)}, u32[]{:S(2)}, u32[]{:S(2)}) async-start(bf16[16,16,2816]{2,1,0:T(8,128)(2,1)} %bitcast.2), calls=%async_computation | async-start | bytes 2883584 | tf_op jit(solution)/shard_map/all_to_all | solution.py:500
  79.2 6.0 %over.1 = (bf16[512,2048]{1,0:T(8,128)(2,1)S(1)}, bf16[512,768]{1,0:T(8,128)(2,1)S(1)}, bf16[512,768]{1,0:T(8,128)(2,1)S(1)}, bf16[768,2048]{1,0:T(8,128)(2,1)}) custom-call(s32[128]{0:T(128)S(1)} %bitcast.23, bf16[64,2816]{1,0:T(8,128)(2,1)S(1)} %copy-done.16, bf16[64,2816]{1,0:T(8,128)(2,1)S(1)} %copy-done.20, bf16[64,2816]{1,0:T(8,128)(2,1)S(1)} %copy-done.18, ...), custom_call_target="tpu_custom_call" | custom-call | flops 6442450944 | bytes 17825792 | tf_op jit(solution)/shard_map/over/pallas_call | solution.py:261
  87.0 12.1 %all-to-all-done = bf16[16,16,2816]{2,1,0:T(8,128)(2,1)S(1)} async-done(((bf16[16,16,2816]{2,1,0:T(8,128)(2,1)}), bf16[16,16,2816]{2,1,0:T(8,128)(2,1)S(1)}, u32[]{:S(2)}, u32[]{:S(2)}) %all-to-all-start) | async-done | bytes 1441824 | tf_op jit(solution)/shard_map/all_to_all | solution.py:500
  99.1 7.6 %direct.1 = (bf16[256,768]{1,0:T(8,128)(2,1)S(1)}, bf16[256,768]{1,0:T(8,128)(2,1)S(1)}, bf16[768,2048]{1,0:T(8,128)(2,1)}) custom-call(bf16[256,2816]{1,0:T(8,128)(2,1)S(1)} %bitcast.16, bf16[256,2816]{1,0:T(8,128)(2,1)S(1)} %bitcast.17, bf16[1,2048,768]{2,1,0:T(8,128)(2,1)} %wg_ref.1, ...), custom_call_target="tpu_custom_call", output_to_operand_aliasing={{2}: (4, {})} | custom-call | flops 3221225472 | bytes 10485760 | tf_op jit(solution)/shard_map/direct/pallas_call | solution.py:332
  108.2 5.5 %all-to-all-start.1 = ((bf16[16,48,2048]{2,1,0:T(8,128)(2,1)}), bf16[16,48,2048]{2,1,0:T(8,128)(2,1)}, u32[]{:S(2)}, u32[]{:S(2)}) async-start(bf16[16,48,2048]{2,1,0:T(8,128)(2,1)} %bitcast.24), calls=%async_computation.1 | async-start | bytes 6291456 | tf_op jit(solution)/shard_map/all_to_all | solution.py:503
  118.6 5.2 %weight_send.1 = bf16[1024,1536]{1,0:T(8,128)(2,1)S(1)} custom-call(s32[8]{0:T(128)S(1)} %broadcast_xor_fusion.block_ref, bf16[256,2816]{1,0:T(8,128)(2,1)S(1)} %bitcast.18, bf16[256,768]{1,0:T(8,128)(2,1)S(1)} %copy-done.10, bf16[256,768]{1,0:T(8,128)(2,1)S(1)} %copy-done.13, bf16[512,2048]{1,0:T(8,128)(2,1)S(1)} %get-tuple-element.60.refs_3_, ...), custom_call_target="tpu_custom_call" | custom-call | flops 2415919104 | bytes 8388608 | tf_op jit(solution)/shard_map/weight_send/pallas_call | solution.py:399
  124.6 4.9 %collective-permute-done.12.refs_6_ = bf16[1024,1536]{1,0:T(8,128)(2,1)S(1)} collective-permute-done((bf16[1024,1536]{1,0:T(8,128)(2,1)S(1)}, bf16[1024,1536]{1,0:T(8,128)(2,1)S(1)}, u32[]{:S(2)}, u32[]{:S(2)}) %collective-permute-start.12) | collective-permute-done | bytes 3145760 | tf_op jit(solution)/shard_map/ppermute | solution.py:510
  129.6 5.7 %weight_keep.1 = (f32[128,1536]{1,0:T(8,128)S(1)}, bf16[128,1536]{1,0:T(8,128)(2,1)S(1)}, bf16[128,1536]{1,0:T(8,128)(2,1)S(1)}, bf16[128,1536]{1,0:T(8,128)(2,1...) custom-call(s32[8]{0:T(128)S(1)} %dynamic-slice_bitcast_fusion.block, ...), custom_call_target="tpu_custom_call" | custom-call | flops 2415919104 | bytes 11534336 | tf_op jit(solution)/shard_map/weight_keep/pallas_call | solution.py:439
  136.1 1.6 collective-permute-start.14
  137.7 3.5 %collective-permute-start.15 = (bf16[128,1536]{1,0:T(8,128)(2,1)S(1)}, bf16[128,1536]{1,0:T(8,128)(2,1)S(1)}, u32[]{:S(2)}, u32[]{:S(2)}) collective-permute-start(bf16[128,1536]{1,0:T(8,128)(2,1)S(1)} %get-tuple-element.66), channel_id=1, source_target_pairs={{0,96},{16,112},{32,64},{48,80},{64,160},{80,176},{96,128},{112,14... | collective-permute-start | bytes 1179656 | tf_op jit(solution)/shard_map/ppermute | solution.py:514
  141.2 1.2 collective-permute-start.16
  142.4 2.5 %collective-permute-start.17 = (bf16[128,1536]{1,0:T(8,128)(2,1)S(1)}, bf16[128,1536]{1,0:T(8,128)(2,1)S(1)}, u32[]{:S(2)}, u32[]{:S(2)}) collective-permute-start(bf16[128,1536]{1,0:T(8,128)(2,1)S(1)} %get-tuple-element.68), channel_id=1, source_target_pairs={{0,160},{16,176},{32,128},{48,144},{64,224},{80,240},{96,192},{112... | collective-permute-start | bytes 1179656 | tf_op jit(solution)/shard_map/ppermute | solution.py:514
  144.9 9.3 %collective-permute-done.13 = bf16[128,1536]{1,0:T(8,128)(2,1)S(1)} collective-permute-done((bf16[128,1536]{1,0:T(8,128)(2,1)S(1)}, bf16[128,1536]{1,0:T(8,128)(2,1)S(1)}, u32[]{:S(2)}, u32[]{:S(2)}) %collective-permute-start.13) | collective-permute-done | bytes 393248 | tf_op jit(solution)/shard_map/ppermute | solution.py:514
  154.6 2.5 %collective-permute-start.19 = (bf16[128,1536]{1,0:T(8,128)(2,1)S(1)}, bf16[128,1536]{1,0:T(8,128)(2,1)S(1)}, u32[]{:S(2)}, u32[]{:S(2)}) collective-permute-start(bf16[128,1536]{1,0:T(8,128)(2,1)S(1)} %get-tuple-element.70), channel_id=1, source_target_pairs={{0,224},{16,240},{32,192},{48,208},{64,32},{80,48},{96,0},{112,16}... | collective-permute-start | bytes 1179656 | tf_op jit(solution)/shard_map/ppermute | solution.py:514
  157.1 27.8 %collective-permute-done.15 = bf16[128,1536]{1,0:T(8,128)(2,1)S(1)} collective-permute-done((bf16[128,1536]{1,0:T(8,128)(2,1)S(1)}, bf16[128,1536]{1,0:T(8,128)(2,1)S(1)}, u32[]{:S(2)}, u32[]{:S(2)}) %collective-permute-start.15) | collective-permute-done | bytes 393248 | tf_op jit(solution)/shard_map/ppermute | solution.py:514
  184.9 11.0 %collective-permute-done.17 = bf16[128,1536]{1,0:T(8,128)(2,1)S(1)} collective-permute-done((bf16[128,1536]{1,0:T(8,128)(2,1)S(1)}, bf16[128,1536]{1,0:T(8,128)(2,1)S(1)}, u32[]{:S(2)}, u32[]{:S(2)}) %collective-permute-start.17) | collective-permute-done | bytes 393248 | tf_op jit(solution)/shard_map/ppermute | solution.py:514
  195.9 7.1 %collective-permute-done.19 = bf16[128,1536]{1,0:T(8,128)(2,1)S(1)} collective-permute-done((bf16[128,1536]{1,0:T(8,128)(2,1)S(1)}, bf16[128,1536]{1,0:T(8,128)(2,1)S(1)}, u32[]{:S(2)}, u32[]{:S(2)}) %collective-permute-start.19) | collective-permute-done | bytes 393248 | tf_op jit(solution)/shard_map/ppermute | solution.py:514
  204.4 3.3 %convolution_convert_fusion = bf16[128,2048]{1,0:T(8,128)(2,1)} fusion(bf16[768,128]{1,0:T(8,128)(2,1)S(1)} %copy-done.22, bf16[768,2048]{1,0:T(8,128)(2,1)} %bitcast.5), kind=kOutput, calls=%fused_computation | convolution fusion | flops 402915328 | bytes 3866624 | tf_op jit(solution)/shard_map/dot_general | solution.py:516
  (108 shorter events, 35.5 us)
Async XLA Ops:
  6.0 34.5 %copy-start.15 = (bf16[64,2816]{1,0:T(8,128)(2,1)}, bf16[64,2816]{1,0:T(8,128)(2,1)S(1)}, u32[]{:S(2)}) copy-start(bf16[64,2816]{1,0:T(8,128)(2,1)S(1)} %get-tuple-element.40.refs_0_) | copy-start | bytes 1081348
  6.0 53.3 %copy-start.21 = (bf16[768,128]{1,0:T(8,128)(2,1)}, bf16[768,128]{1,0:T(8,128)(2,1)S(1)}, u32[]{:S(2)}) copy-start(bf16[768,128]{1,0:T(8,128)(2,1)S(1)} %get-tuple-element.37) | copy-start | bytes 589828
  6.0 13.5 %collective-permute-start.2 = (bf16[64,2816]{1,0:T(8,128)(2,1)S(1)}, bf16[64,2816]{1,0:T(8,128)(2,1)S(1)}, u32[]{:S(2)}, u32[]{:S(2)}) collective-permute-start(bf16[64,2816]{1,0:T(8,128)(2,1)S(1)} %get-tuple-element.40.refs_0_), channel_id=1, source_target_pairs={{0,14},{1,15},{2,0},{3,1},{4,2},{5,3},{6,4},{7,5},{8,6},{9,7},{10,... | collective-permute-start | bytes 1081352 | tf_op jit(solution)/shard_map/ppermute | solution.py:489
  11.9 11.1 %collective-permute-start = (bf16[64,2816]{1,0:T(8,128)(2,1)S(1)}, bf16[64,2816]{1,0:T(8,128)(2,1)S(1)}, u32[]{:S(2)}, u32[]{:S(2)}) collective-permute-start(bf16[64,2816]{1,0:T(8,128)(2,1)S(1)} %get-tuple-element.40.refs_0_), channel_id=1, source_target_pairs={{0,2},{1,3},{2,4},{3,5},{4,6},{5,7},{6,8},{7,9},{8,10},{9,11},{10,... | collective-permute-start | bytes 1081352 | tf_op jit(solution)/shard_map/ppermute | solution.py:488
  19.6 13.6 %copy-start.17 = (bf16[64,2816]{1,0:T(8,128)(2,1)}, bf16[64,2816]{1,0:T(8,128)(2,1)S(1)}, u32[]{:S(2)}) copy-start(bf16[64,2816]{1,0:T(8,128)(2,1)S(1)} %collective-permute-done.2.refs_2_) | copy-start | bytes 1081348
  23.0 10.2 %copy-start.19 = (bf16[64,2816]{1,0:T(8,128)(2,1)}, bf16[64,2816]{1,0:T(8,128)(2,1)S(1)}, u32[]{:S(2)}) copy-start(bf16[64,2816]{1,0:T(8,128)(2,1)S(1)} %collective-permute-done.refs_1_) | copy-start | bytes 1081348
  23.6 16.9 %collective-permute-start.7 = (bf16[96,2816]{1,0:T(8,128)(2,1)S(1)}, bf16[96,2816]{1,0:T(8,128)(2,1)S(1)}, u32[]{:S(2)}, u32[]{:S(2)}) collective-permute-start(bf16[96,2816]{1,0:T(8,128)(2,1)S(1)} %choose.2), channel_id=1, source_target_pairs={{0,1},{1,0},{2,3},{3,2},{4,5},{5,4},{6,7},{7,6},{8,9},{9,8},{10,11... | collective-permute-start | bytes 1622024 | tf_op jit(solution)/shard_map/ppermute | solution.py:497
  24.5 8.7 %collective-permute-start.3 = (bf16[64,2816]{1,0:T(8,128)(2,1)S(1)}, bf16[64,2816]{1,0:T(8,128)(2,1)S(1)}, u32[]{:S(2)}, u32[]{:S(2)}) collective-permute-start(bf16[64,2816]{1,0:T(8,128)(2,1)S(1)} %collective-permute-done.2.refs_2_), channel_id=1, source_target_pairs={{0,14},{1,15},{2,0},{3,1},{4,2},{5,3},{6,4},{7,5},{8,6},{9,7},{10,... | collective-permute-start | bytes 1081352 | tf_op jit(solution)/shard_map/ppermute | solution.py:489
  24.8 9.9 %collective-permute-start.1 = (bf16[64,2816]{1,0:T(8,128)(2,1)S(1)}, bf16[64,2816]{1,0:T(8,128)(2,1)S(1)}, u32[]{:S(2)}, u32[]{:S(2)}) collective-permute-start(bf16[64,2816]{1,0:T(8,128)(2,1)S(1)} %collective-permute-done.refs_1_), channel_id=1, source_target_pairs={{0,2},{1,3},{2,4},{3,5},{4,6},{5,7},{6,8},{7,9},{8,10},{9,11},{10,... | collective-permute-start | bytes 1081352 | tf_op jit(solution)/shard_map/ppermute | solution.py:488
  33.2 5.5 %copy-start = (bf16[64,2816]{1,0:T(8,128)(2,1)}, bf16[64,2816]{1,0:T(8,128)(2,1)S(1)}, u32[]{:S(2)}) copy-start(bf16[64,2816]{1,0:T(8,128)(2,1)S(1)} %collective-permute-done.3.refs_1_.refs_4_.refs_5_) | copy-start | bytes 1081348
  34.7 4.5 %copy-start.2 = (bf16[64,2816]{1,0:T(8,128)(2,1)}, bf16[64,2816]{1,0:T(8,128)(2,1)S(1)}, u32[]{:S(2)}) copy-start(bf16[64,2816]{1,0:T(8,128)(2,1)S(1)} %collective-permute-done.1.refs_0_.refs_2_.refs_3_) | copy-start | bytes 1081348
  35.3 10.6 %collective-permute-start.4 = (bf16[32,2816]{1,0:T(8,128)(2,1)S(1)}, bf16[32,2816]{1,0:T(8,128)(2,1)S(1)}, u32[]{:S(2)}, u32[]{:S(2)}) collective-permute-start(bf16[32,2816]{1,0:T(8,128)(2,1)S(1)} %get-tuple-element.41), channel_id=1, source_target_pairs={{0,2},{1,3},{2,4},{3,5},{4,6},{5,7},{6,8},{7,9},{8,10},{9,11},{10,... | collective-permute-start | bytes 540680 | tf_op jit(solution)/shard_map/ppermute | solution.py:492
  35.6 11.0 %collective-permute-start.5 = (bf16[32,2816]{1,0:T(8,128)(2,1)S(1)}, bf16[32,2816]{1,0:T(8,128)(2,1)S(1)}, u32[]{:S(2)}, u32[]{:S(2)}) collective-permute-start(bf16[32,2816]{1,0:T(8,128)(2,1)S(1)} %get-tuple-element.42), channel_id=1, source_target_pairs={{0,14},{1,15},{2,0},{3,1},{4,2},{5,3},{6,4},{7,5},{8,6},{9,7},{10,... | collective-permute-start | bytes 540680 | tf_op jit(solution)/shard_map/ppermute | solution.py:492
  39.2 20.1 %collective-permute-start.8 = (bf16[64,2816]{1,0:T(8,128)(2,1)S(1)}, bf16[64,2816]{1,0:T(8,128)(2,1)S(1)}, u32[]{:S(2)}, u32[]{:S(2)}) collective-permute-start(bf16[64,2816]{1,0:T(8,128)(2,1)S(1)} %choose.3), channel_id=1, source_target_pairs={{0,1},{1,0},{2,3},{3,2},{4,5},{5,4},{6,7},{7,6},{8,9},{9,8},{10,11... | collective-permute-start | bytes 1081352 | tf_op jit(solution)/shard_map/ppermute | solution.py:497
  40.5 9.9 %collective-permute-start.6 = (bf16[32,2816]{1,0:T(8,128)(2,1)S(1)}, bf16[32,2816]{1,0:T(8,128)(2,1)S(1)}, u32[]{:S(2)}, u32[]{:S(2)}) collective-permute-start(bf16[32,2816]{1,0:T(8,128)(2,1)S(1)} %get-tuple-element.43), channel_id=1, source_target_pairs={{0,4},{1,5},{2,6},{3,7},{4,8},{5,9},{6,10},{7,11},{8,12},{9,13},{1... | collective-permute-start | bytes 540680 | tf_op jit(solution)/shard_map/ppermute | solution.py:492
  41.4 13.5 %collective-permute-start.9 = (bf16[32,2816]{1,0:T(8,128)(2,1)S(1)}, bf16[32,2816]{1,0:T(8,128)(2,1)S(1)}, u32[]{:S(2)}, u32[]{:S(2)}) collective-permute-start(bf16[32,2816]{1,0:T(8,128)(2,1)S(1)} %get-tuple-element.44), channel_id=1, source_target_pairs={{0,3},{1,2},{2,5},{3,4},{4,7},{5,6},{6,9},{7,8},{8,11},{9,10},{10,... | collective-permute-start | bytes 540680 | tf_op jit(solution)/shard_map/ppermute | solution.py:492
  46.6 11.4 %collective-permute-start.10 = (bf16[32,2816]{1,0:T(8,128)(2,1)S(1)}, bf16[32,2816]{1,0:T(8,128)(2,1)S(1)}, u32[]{:S(2)}, u32[]{:S(2)}) collective-permute-start(bf16[32,2816]{1,0:T(8,128)(2,1)S(1)} %get-tuple-element.45), channel_id=1, source_target_pairs={{0,15},{1,14},{2,1},{3,0},{4,3},{5,2},{6,5},{7,4},{8,7},{9,6},{10,... | collective-permute-start | bytes 540680 | tf_op jit(solution)/shard_map/ppermute | solution.py:492
  47.3 11.4 %collective-permute-start.11 = (bf16[32,2816]{1,0:T(8,128)(2,1)S(1)}, bf16[32,2816]{1,0:T(8,128)(2,1)S(1)}, u32[]{:S(2)}, u32[]{:S(2)}) collective-permute-start(bf16[32,2816]{1,0:T(8,128)(2,1)S(1)} %get-tuple-element.46), channel_id=1, source_target_pairs={{0,13},{1,12},{2,15},{3,14},{4,1},{5,0},{6,3},{7,2},{8,5},{9,4},{1... | collective-permute-start | bytes 540680 | tf_op jit(solution)/shard_map/ppermute | solution.py:492
  60.1 39.0 %all-to-all-start = ((bf16[16,16,2816]{2,1,0:T(8,128)(2,1)}), bf16[16,16,2816]{2,1,0:T(8,128)(2,1)S(1)}, u32[]{:S(2)}, u32[]{:S(2)}) async-start(bf16[16,16,2816]{2,1,0:T(8,128)(2,1)} %bitcast.2), calls=%async_computation | async-start | bytes 2883584 | tf_op jit(solution)/shard_map/all_to_all | solution.py:500
  108.2 96.2 %all-to-all-start.1 = ((bf16[16,48,2048]{2,1,0:T(8,128)(2,1)}), bf16[16,48,2048]{2,1,0:T(8,128)(2,1)}, u32[]{:S(2)}, u32[]{:S(2)}) async-start(bf16[16,48,2048]{2,1,0:T(8,128)(2,1)} %bitcast.24), calls=%async_computation.1 | async-start | bytes 6291456 | tf_op jit(solution)/shard_map/all_to_all | solution.py:503
  118.6 11.0 %copy-start.6 = (bf16[512,768]{1,0:T(8,128)(2,1)S(1)}, bf16[512,768]{1,0:T(8,128)(2,1)}, u32[]{:S(2)}) copy-start(bf16[512,768]{1,0:T(8,128)(2,1)} %copy-done.4) | copy-start | bytes 2359300
  118.6 11.0 %copy-start.11 = (bf16[256,768]{1,0:T(8,128)(2,1)S(1)}, bf16[256,768]{1,0:T(8,128)(2,1)}, u32[]{:S(2)}) copy-start(bf16[256,768]{1,0:T(8,128)(2,1)} %copy-done.9) | copy-start | bytes 1179652
  118.6 11.0 %copy-start.14 = (bf16[256,768]{1,0:T(8,128)(2,1)S(1)}, bf16[256,768]{1,0:T(8,128)(2,1)}, u32[]{:S(2)}) copy-start(bf16[256,768]{1,0:T(8,128)(2,1)} %copy-done.12) | copy-start | bytes 1179652
  123.8 5.7 %collective-permute-start.12 = (bf16[1024,1536]{1,0:T(8,128)(2,1)S(1)}, bf16[1024,1536]{1,0:T(8,128)(2,1)S(1)}, u32[]{:S(2)}, u32[]{:S(2)}) collective-permute-start(bf16[1024,1536]{1,0:T(8,128)(2,1)S(1)} %weight_send.1), channel_id=1, source_target_pairs={{0,16},{16,0},{32,48},{48,32},{64,80},{80,64},{96,112},{112,96},{1... | collective-permute-start | bytes 9437192 | tf_op jit(solution)/shard_map/ppermute | solution.py:510
  135.3 69.1 %copy-start.22 = (bf16[768,128]{1,0:T(8,128)(2,1)S(1)}, bf16[768,128]{1,0:T(8,128)(2,1)}, u32[]{:S(2)}) copy-start(bf16[768,128]{1,0:T(8,128)(2,1)} %copy-done.21) | copy-start | bytes 589828
  135.3 18.9 %collective-permute-start.13 = (bf16[128,1536]{1,0:T(8,128)(2,1)S(1)}, bf16[128,1536]{1,0:T(8,128)(2,1)S(1)}, u32[]{:S(2)}, u32[]{:S(2)}) collective-permute-start(bf16[128,1536]{1,0:T(8,128)(2,1)S(1)} %get-tuple-element.64), channel_id=1, source_target_pairs={{0,32},{16,48},{32,0},{48,16},{64,96},{80,112},{96,64},{112,80},{1... | collective-permute-start | bytes 1179656 | tf_op jit(solution)/shard_map/ppermute | solution.py:514
  136.1 18.5 %collective-permute-start.14 = (bf16[128,1536]{1,0:T(8,128)(2,1)S(1)}, bf16[128,1536]{1,0:T(8,128)(2,1)S(1)}, u32[]{:S(2)}, u32[]{:S(2)}) collective-permute-start(bf16[128,1536]{1,0:T(8,128)(2,1)S(1)} %get-tuple-element.65), channel_id=1, source_target_pairs={{0,64},{16,80},{32,96},{48,112},{64,128},{80,144},{96,160},{112,17... | collective-permute-start | bytes 1179656 | tf_op jit(solution)/shard_map/ppermute | solution.py:514
  137.7 47.2 %collective-permute-start.15 = (bf16[128,1536]{1,0:T(8,128)(2,1)S(1)}, bf16[128,1536]{1,0:T(8,128)(2,1)S(1)}, u32[]{:S(2)}, u32[]{:S(2)}) collective-permute-start(bf16[128,1536]{1,0:T(8,128)(2,1)S(1)} %get-tuple-element.66), channel_id=1, source_target_pairs={{0,96},{16,112},{32,64},{48,80},{64,160},{80,176},{96,128},{112,14... | collective-permute-start | bytes 1179656 | tf_op jit(solution)/shard_map/ppermute | solution.py:514
  141.2 43.7 %collective-permute-start.16 = (bf16[128,1536]{1,0:T(8,128)(2,1)S(1)}, bf16[128,1536]{1,0:T(8,128)(2,1)S(1)}, u32[]{:S(2)}, u32[]{:S(2)}) collective-permute-start(bf16[128,1536]{1,0:T(8,128)(2,1)S(1)} %get-tuple-element.67), channel_id=1, source_target_pairs={{0,128},{16,144},{32,160},{48,176},{64,192},{80,208},{96,224},{112... | collective-permute-start | bytes 1179656 | tf_op jit(solution)/shard_map/ppermute | solution.py:514
  142.4 53.5 %collective-permute-start.17 = (bf16[128,1536]{1,0:T(8,128)(2,1)S(1)}, bf16[128,1536]{1,0:T(8,128)(2,1)S(1)}, u32[]{:S(2)}, u32[]{:S(2)}) collective-permute-start(bf16[128,1536]{1,0:T(8,128)(2,1)S(1)} %get-tuple-element.68), channel_id=1, source_target_pairs={{0,160},{16,176},{32,128},{48,144},{64,224},{80,240},{96,192},{112... | collective-permute-start | bytes 1179656 | tf_op jit(solution)/shard_map/ppermute | solution.py:514
  154.1 41.8 %collective-permute-start.18 = (bf16[128,1536]{1,0:T(8,128)(2,1)S(1)}, bf16[128,1536]{1,0:T(8,128)(2,1)S(1)}, u32[]{:S(2)}, u32[]{:S(2)}) collective-permute-start(bf16[128,1536]{1,0:T(8,128)(2,1)S(1)} %get-tuple-element.69), channel_id=1, source_target_pairs={{0,192},{16,208},{32,224},{48,240},{64,0},{80,16},{96,32},{112,48}... | collective-permute-start | bytes 1179656 | tf_op jit(solution)/shard_map/ppermute | solution.py:514
  154.6 48.4 %collective-permute-start.19 = (bf16[128,1536]{1,0:T(8,128)(2,1)S(1)}, bf16[128,1536]{1,0:T(8,128)(2,1)S(1)}, u32[]{:S(2)}, u32[]{:S(2)}) collective-permute-start(bf16[128,1536]{1,0:T(8,128)(2,1)S(1)} %get-tuple-element.70), channel_id=1, source_target_pairs={{0,224},{16,240},{32,192},{48,208},{64,32},{80,48},{96,0},{112,16}... | collective-permute-start | bytes 1179656 | tf_op jit(solution)/shard_map/ppermute | solution.py:514
  (30 other events, 26.7 us)

commit v4 on v3

--- a/solution.py
+++ b/solution.py
@@ -33,6 +33,10 @@
     return there + 1 - 2 * (there % 2) if crosses else there
 
 
+def in_hbm(a):
+    return pltpu.with_memory_space_constraint(a, pltpu.HBM)
+
+
 def pack_kernel(
     me_ref, routes_ref, tokens_ref, grads_ref, choice_ref, sel_ref, out_ref, over_ref
 ):
@@ -109,7 +113,17 @@
 
     fill(over_ref, jnp.where(rank >= COLD, which * SPILL + rank - COLD, -1))
     fill(out_ref, jnp.where(rank < COLD, routes * COLD + rank, -1))
-    sel_ref[...] = picked(routes * CAP + rank, ROWS)[1]
+    back = routes * CAP + rank == lax.broadcasted_iota(jnp.int32, (ROWS, pairs), 0)
+    of_token = (
+        lax.broadcasted_iota(jnp.int32, (toks, pairs), 1) // 2
+        == lax.broadcasted_iota(jnp.int32, (toks, pairs), 0)
+    ).astype(jnp.bfloat16)
+    sel_ref[...] = lax.dot_general(
+        of_token,
+        back.astype(jnp.bfloat16),
+        (((1,), (1,)), ((), ())),
+        preferred_element_type=jnp.float32,
+    ).astype(jnp.bfloat16)
 
 
 def pack(me, routes, tokens, grads):
@@ -121,7 +135,7 @@
         out_specs=[vmem] * 4,
         out_shape=[
             jax.ShapeDtypeStruct((1, 128), jnp.int32),
-            jax.ShapeDtypeStruct((ROWS, toks), jnp.bfloat16),
+            pltpu.HBM((toks, ROWS), jnp.bfloat16),
             jax.ShapeDtypeStruct((DIRECT, WIDTH), jnp.bfloat16),
             jax.ShapeDtypeStruct((2 * SPILL, WIDTH), jnp.bfloat16),
         ],
@@ -191,6 +205,11 @@
     return delta_g, delta_u
 
 
+def put_deltas(ref, j, delta_g, delta_u):
+    for first, delta in ((0, delta_g), (FF, delta_u)):
+        ref[:, pl.ds(pl.multiple_of(first + j * FF_BLOCK, FF_BLOCK), FF_BLOCK)] = delta
+
+
 def back_rows(delta_g, delta_u, wg, wu):
     dims = (((1,), (1,)), ((), ()))
     return lax.dot_general(
@@ -200,7 +219,7 @@
 
 def over_kernel(choice_ref, *refs):
     inputs = 5 + len(PIECES) + len(HOPS)
-    wg_ref, wu_ref, x_ref, delta_g_ref, delta_u_ref, back_ref, acc_ref, dh_ref = refs[inputs:]
+    wg_ref, wu_ref, x_ref, delta_ref, back_ref, acc_ref, dh_ref = refs[inputs:]
     j = pl.program_id(0)
     last = pl.num_programs(0) - 1
     hot = choice_ref[HOT_ME] == 1
@@ -220,14 +239,12 @@
 
     @pl.when(jnp.logical_not(hot))
     def _():
-        delta_g_ref[...] = jnp.zeros_like(delta_g_ref)
-        delta_u_ref[...] = jnp.zeros_like(delta_u_ref)
+        delta_ref[...] = jnp.zeros_like(delta_ref)
 
     @pl.when(hot)
     def _():
         delta_g, delta_u = deltas(x_ref[...], dh_ref[j], wg_ref[0], wu_ref[0])
-        delta_g_ref[...] = delta_g
-        delta_u_ref[...] = delta_u
+        put_deltas(delta_ref, j, delta_g, delta_u)
         part = back_rows(delta_g, delta_u, wg_ref[0], wu_ref[0])
 
         @pl.when(j == 0)
@@ -268,8 +285,7 @@
             + [pl.BlockSpec((1, D, FF_BLOCK), lambda j, c: (0, 0, j))] * 2,
             out_specs=[
                 pl.BlockSpec((OVER, D), lambda j, c: (0, 0)),
-                pl.BlockSpec((OVER, FF_BLOCK), lambda j, c: (0, j)),
-                pl.BlockSpec((OVER, FF_BLOCK), lambda j, c: (0, j)),
+                pl.BlockSpec((OVER, 2 * FF), lambda j, c: (0, 0)),
                 pl.BlockSpec((ROWS, D), lambda j, c: (0, 0)),
             ],
             scratch_shapes=[
@@ -278,9 +294,8 @@
             ],
         ),
         out_shape=[
-            jax.ShapeDtypeStruct((OVER, D), jnp.bfloat16),
-            jax.ShapeDtypeStruct((OVER, FF), jnp.bfloat16),
-            jax.ShapeDtypeStruct((OVER, FF), jnp.bfloat16),
+            pltpu.HBM((OVER, D), jnp.bfloat16),
+            pltpu.HBM((OVER, 2 * FF), jnp.bfloat16),
             pltpu.HBM((ROWS, D), jnp.bfloat16),
         ],
         compiler_params=pltpu.CompilerParams(vmem_limit_bytes=34 * MIB),
@@ -292,13 +307,12 @@
 
 
 def direct_kernel(
-    x_ref, dh_ref, wg_ref, wu_ref, old_ref, delta_g_ref, delta_u_ref, back_ref, acc_ref, low_ref, sems
+    x_ref, dh_ref, wg_ref, wu_ref, old_ref, delta_ref, back_ref, acc_ref, low_ref, sems
 ):
     j = pl.program_id(0)
     delta_g, delta_u = deltas(x_ref[...], dh_ref[...], wg_ref[0], wu_ref[0])
     part = back_rows(delta_g, delta_u, wg_ref[0], wu_ref[0])
-    delta_g_ref[...] = delta_g
-    delta_u_ref[...] = delta_u
+    put_deltas(delta_ref, j, delta_g, delta_u)
     last = pl.num_programs(0) - 1
 
     @pl.when(j == 0)
@@ -340,13 +354,11 @@
             pl.BlockSpec(memory_space=pltpu.HBM),
         ],
         out_specs=[
-            pl.BlockSpec((DIRECT, FF_BLOCK), lambda j: (0, j)),
-            pl.BlockSpec((DIRECT, FF_BLOCK), lambda j: (0, j)),
+            pl.BlockSpec((DIRECT, 2 * FF), lambda j: (0, 0)),
             pl.BlockSpec(memory_space=pltpu.HBM),
         ],
         out_shape=[
-            jax.ShapeDtypeStruct((DIRECT, FF), jnp.bfloat16),
-            jax.ShapeDtypeStruct((DIRECT, FF), jnp.bfloat16),
+            pltpu.HBM((DIRECT, 2 * FF), jnp.bfloat16),
             pltpu.HBM((ROWS, D), jnp.bfloat16),
         ],
         scratch_shapes=[
@@ -354,7 +366,7 @@
             pltpu.VMEM((DIRECT, D), jnp.bfloat16),
             pltpu.SemaphoreType.DMA((EXPERTS,)),
         ],
-        input_output_aliases={4: 2},
+        input_output_aliases={4: 1},
         compiler_params=pltpu.CompilerParams(vmem_limit_bytes=20 * MIB),
         cost_estimate=pl.CostEstimate(
             flops=8 * DIRECT * D * FF, bytes_accessed=10 * MIB, transcendentals=DIRECT * FF
@@ -363,95 +375,126 @@
     )(got, got, w_gate, w_up, pltpu.with_memory_space_constraint(back, pltpu.HBM))
 
 
-def weight_part(x_ref, dg_ref, du_ref, over_x_ref, over_dg_ref, over_du_ref):
-    dims = (((0,), (0,)), ((), ()))
-    x = x_ref[...]
-    over_x = over_x_ref[...]
-
-    def both(d_ref, over_d_ref):
-        return lax.dot_general(
-            x, d_ref[...], dims, preferred_element_type=jnp.float32
-        ) + lax.dot_general(over_x, over_d_ref[...], dims, preferred_element_type=jnp.float32)
-
-    return both(dg_ref, over_dg_ref), both(du_ref, over_du_ref)
-
-
-def weight_send_kernel(block_ref, *refs):
-    gate, up = weight_part(*refs[:6])
-    out_ref = refs[6]
-    out_ref[:, :FF] = gate.astype(jnp.bfloat16)
-    out_ref[:, FF:] = up.astype(jnp.bfloat16)
-
-
-def weight_specs():
+def turned(x_ref, turned_ref, block_ref, first):
+    for q in range(turned_ref.shape[0] // BLOCK):
+        column = pl.multiple_of(block_ref[first + q] * BLOCK, BLOCK)
+        turned_ref[q * BLOCK : (q + 1) * BLOCK, :] = x_ref[:, pl.ds(column, BLOCK)].T
+
+
+def weight_over_kernel(block_ref, choice_ref, x_ref, delta_ref, out_ref, turned_ref):
+    hot = choice_ref[HOT_ME] == 1
+
+    @pl.when(hot)
+    def _():
+        @pl.when(pl.program_id(0) == 0)
+        def _():
+            turned(x_ref, turned_ref, block_ref, 0)
+
+        out_ref[...] = jnp.dot(
+            turned_ref[...], delta_ref[...], preferred_element_type=jnp.float32
+        )
+
+    @pl.when(jnp.logical_not(hot))
+    def _():
+        out_ref[...] = jnp.zeros_like(out_ref)
+
+
+def weight_over(blocks, choice, x, delta):
+    rows = blocks.shape[0] * BLOCK
+    return pl.pallas_call(
+        weight_over_kernel,
+        grid_spec=pltpu.PrefetchScalarGridSpec(
+            num_scalar_prefetch=2,
+            grid=(2 * FF // FF_BLOCK,),
+            in_specs=[
+                pl.BlockSpec((OVER, D), lambda j, b, c: (0, 0)),
+                pl.BlockSpec((OVER, FF_BLOCK), lambda j, b, c: (0, j)),
+            ],
+            out_specs=pl.BlockSpec((rows, FF_BLOCK), lambda j, b, c: (0, j)),
+            scratch_shapes=[pltpu.VMEM((rows, OVER), jnp.bfloat16)],
+        ),
+        out_shape=pltpu.HBM((rows, 2 * FF), jnp.float32),
+        compiler_params=pltpu.CompilerParams(vmem_limit_bytes=20 * MIB),
+        cost_estimate=pl.CostEstimate(
+            flops=4 * OVER * rows * FF, bytes_accessed=17 * MIB, transcendentals=0
+        ),
+        name="weight_over",
+    )(blocks, choice, x, delta)
+
+
+def weight_send_kernel(block_ref, x_ref, delta_ref, part_ref, out_ref, turned_ref):
+    @pl.when(pl.program_id(0) == 0)
+    def _():
+        turned(x_ref, turned_ref, block_ref, 0)
+
+    total = part_ref[...] + jnp.dot(
+        turned_ref[...], delta_ref[...], preferred_element_type=jnp.float32
+    )
+    out_ref[...] = total.astype(jnp.bfloat16)
+
+
+def weight_specs(rows, half):
     return [
-        pl.BlockSpec((DIRECT, BLOCK), lambda i, b: (0, b[i])),
-        pl.BlockSpec((DIRECT, FF), lambda i, b: (0, 0)),
-        pl.BlockSpec((DIRECT, FF), lambda i, b: (0, 0)),
-        pl.BlockSpec((OVER, BLOCK), lambda i, b: (0, b[i])),
-        pl.BlockSpec((OVER, FF), lambda i, b: (0, 0)),
-        pl.BlockSpec((OVER, FF), lambda i, b: (0, 0)),
+        pl.BlockSpec((DIRECT, D), lambda j, b: (0, 0)),
+        pl.BlockSpec((DIRECT, FF_BLOCK), lambda j, b: (0, j)),
+        pl.BlockSpec((rows, FF_BLOCK), lambda j, b: (half, j)),
     ]
 
 
-def weight_send(blocks, rows):
-    count = blocks.shape[0]
+def weight_send(blocks, arrays):
+    rows = blocks.shape[0] // 2 * BLOCK
     return pl.pallas_call(
         weight_send_kernel,
         grid_spec=pltpu.PrefetchScalarGridSpec(
             num_scalar_prefetch=1,
-            grid=(count,),
-            in_specs=weight_specs(),
-            out_specs=pl.BlockSpec((BLOCK, 2 * FF), lambda i, b: (i, 0)),
-        ),
-        out_shape=jax.ShapeDtypeStruct((count * BLOCK, 2 * FF), jnp.bfloat16),
-        compiler_params=pltpu.CompilerParams(vmem_limit_bytes=18 * MIB),
-        cost_estimate=pl.CostEstimate(
-            flops=4 * ROWS * count * BLOCK * FF, bytes_accessed=8 * MIB, transcendentals=0
+            grid=(2 * FF // FF_BLOCK,),
+            in_specs=weight_specs(rows, 0),
+            out_specs=pl.BlockSpec((rows, FF_BLOCK), lambda j, b: (0, j)),
+            scratch_shapes=[pltpu.VMEM((rows, DIRECT), jnp.bfloat16)],
+        ),
+        out_shape=jax.ShapeDtypeStruct((rows, 2 * FF), jnp.bfloat16),
+        compiler_params=pltpu.CompilerParams(vmem_limit_bytes=14 * MIB),
+        cost_estimate=pl.CostEstimate(
+            flops=4 * DIRECT * rows * FF, bytes_accessed=11 * MIB, transcendentals=0
         ),
         name="weight_send",
-    )(blocks, *rows)
-
-
-def weight_keep_kernel(block_ref, *refs):
-    i = pl.program_id(0)
-    came_ref, own_ref, *out_refs = refs[6:]
-    gate, up = weight_part(*refs[:6])
-    gate = gate + came_ref[:, :FF].astype(jnp.float32)
-    up = up + came_ref[:, FF:].astype(jnp.float32)
-
-    @pl.when(i == 0)
-    def _():
-        own_ref[:, :FF] = gate
-        own_ref[:, FF:] = up
-
+    )(blocks, *arrays)
+
+
+def weight_keep_kernel(block_ref, x_ref, delta_ref, part_ref, came_ref, *refs):
+    *out_refs, turned_ref = refs
+
+    @pl.when(pl.program_id(0) == 0)
+    def _():
+        turned(x_ref, turned_ref, block_ref, block_ref.shape[0] // 2)
+
+    total = jnp.dot(turned_ref[...], delta_ref[...], preferred_element_type=jnp.float32)
+    total = total + part_ref[...] + came_ref[...].astype(jnp.float32)
     for k, out_ref in enumerate(out_refs):
-
-        @pl.when(i == k + 1)
-        def _(out_ref=out_ref):
-            out_ref[:, :FF] = gate.astype(jnp.bfloat16)
-            out_ref[:, FF:] = up.astype(jnp.bfloat16)
-
-
-def weight_keep(blocks, rows, came):
-    count = blocks.shape[0]
-    whole = pl.BlockSpec((BLOCK, 2 * FF), lambda i, b: (0, 0))
+        rows = out_ref.shape[0]
+        out_ref[...] = total[k * rows : (k + 1) * rows, :].astype(out_ref.dtype)
+
+
+def weight_keep(blocks, arrays, came):
+    rows = blocks.shape[0] // 2 * BLOCK
+    count = rows // BLOCK
     return pl.pallas_call(
         weight_keep_kernel,
         grid_spec=pltpu.PrefetchScalarGridSpec(
             num_scalar_prefetch=1,
-            grid=(count,),
-            in_specs=weight_specs() + [pl.BlockSpec((BLOCK, 2 * FF), lambda i, b: (i, 0))],
-            out_specs=[whole] * count,
-        ),
-        out_shape=[jax.ShapeDtypeStruct((BLOCK, 2 * FF), jnp.float32)]
-        + [jax.ShapeDtypeStruct((BLOCK, 2 * FF), jnp.bfloat16)] * (count - 1),
-        compiler_params=pltpu.CompilerParams(vmem_limit_bytes=24 * MIB),
-        cost_estimate=pl.CostEstimate(
-            flops=4 * ROWS * count * BLOCK * FF, bytes_accessed=11 * MIB, transcendentals=0
+            grid=(2 * FF // FF_BLOCK,),
+            in_specs=weight_specs(rows, 1) + [pl.BlockSpec((rows, FF_BLOCK), lambda j, b: (0, j))],
+            out_specs=[pl.BlockSpec((BLOCK, FF_BLOCK), lambda j, b: (0, j))] * count,
+            scratch_shapes=[pltpu.VMEM((rows, DIRECT), jnp.bfloat16)],
+        ),
+        out_shape=[jax.ShapeDtypeStruct((BLOCK, 2 * FF), jnp.float32)] * 2
+        + [jax.ShapeDtypeStruct((BLOCK, 2 * FF), jnp.bfloat16)] * (count - 2),
+        compiler_params=pltpu.CompilerParams(vmem_limit_bytes=16 * MIB),
+        cost_estimate=pl.CostEstimate(
+            flops=4 * DIRECT * rows * FF, bytes_accessed=14 * MIB, transcendentals=0
         ),
         name="weight_keep",
-    )(blocks, *rows, came)
+    )(blocks, *arrays, came)
 
 
 def place(index):
@@ -476,8 +519,7 @@
         grad_hidden.reshape(pairs, grad_hidden.shape[2]),
     )
     choice = choice.reshape(128)
-    w_gate = pltpu.with_memory_space_constraint(w_gate, pltpu.HBM)
-    w_up = pltpu.with_memory_space_constraint(w_up, pltpu.HBM)
+    w_gate, w_up = in_hbm(w_gate), in_hbm(w_up)
     ups = [(e, (e + 2) % EXPERTS) for e in range(EXPERTS)]
     downs = [(e, (e - 2) % EXPERTS) for e in range(EXPERTS)]
     beside = [(e, e ^ 1) for e in range(EXPERTS)]
@@ -498,24 +540,33 @@
     rest = [*hops[:3], *pieces, *hops[3:]]
     send, *rest = lax.optimization_barrier((send, *rest))
     got = lax.all_to_all(send, "expert", split_axis=0, concat_axis=0, tiled=True)
-    over_x, over_g, over_u, back = over(choice, column, rest, w_gate, w_up)
-    delta_g, delta_u, back = direct(got, w_gate, w_up, back)
+    rest = [in_hbm(a) for a in rest]
+    over_x, over_delta, back = over(choice, column, rest, w_gate, w_up)
+    keep = [[partner(i, s) for s in range(steps)] for i in range(groups)]
+    table = np.array([[b ^ 1 for b in row] + row for row in keep], np.int32)
+    blocks = jnp.asarray(table)[lax.axis_index("dp")]
+    part = weight_over(blocks, choice, in_hbm(over_x), in_hbm(over_delta))
+    got, part = lax.optimization_barrier((got, part))
+    delta, back = direct(got, w_gate, w_up, back)
     returned = lax.all_to_all(back, "expert", split_axis=0, concat_axis=0, tiled=True)
-    rows = (got, delta_g, delta_u, over_x, over_g, over_u)
-
-    keep_table = np.array([[partner(i, s) for s in range(steps)] for i in range(groups)], np.int32)
-    me = lax.axis_index("dp")
-    keep_blocks = jnp.asarray(keep_table)[me]
-    other_half = weight_send(keep_blocks ^ 1, rows)
+    rows = (got, in_hbm(delta), in_hbm(part))
+    other_half = weight_send(blocks, rows)
     came = lax.ppermute(other_half, "dp", [(i, i ^ 1) for i in range(groups)])
-    own, *parts = weight_keep(keep_blocks, rows, came)
-    total = own
-    for s, part in enumerate(parts, 1):
-        came = lax.ppermute(part, "dp", [(i, partner(i, s)) for i in range(groups)])
-        total = total + came.astype(jnp.float32)
-    grad_tokens = lax.dot_general(
-        sel, returned, (((0,), (0,)), ((), ())), preferred_element_type=jnp.float32
-    ).astype(jnp.bfloat16)
+    halves = weight_keep(blocks, rows, came)
+    sums = list(halves[:2])
+    for half in (1, 0):
+        for s in (4, 2, 6):
+            came = lax.ppermute(
+                halves[s + half], "dp", [(i, partner(i, s)) for i in range(groups)]
+            )
+            sums[half] = sums[half] + came.astype(jnp.float32)
+        if half == 1:
+            across = lax.ppermute(
+                sums[1].astype(jnp.bfloat16), "dp", [(i, partner(i, 1)) for i in range(groups)]
+            )
+    grad_tokens = jnp.dot(sel, returned, preferred_element_type=jnp.float32).astype(jnp.bfloat16)
+    across, grad_tokens = lax.optimization_barrier((across, grad_tokens))
+    total = sums[0] + across.astype(jnp.float32)
     return grad_tokens, total[None, :, :FF], total[None, :, FF:]
 
 

time: 209 us -> 187 us (0.89)
  local copies, waits for them, and re-layouts: 30.4 us -> 5.45 us
  Pallas kernels: 28.5 us -> 41.2 us
  waiting for transfers between devices: 103 us -> 97.1 us
  starting transfers between devices: 40.9 us -> 37.7 us
    ppermute x7, waiting for transfers between devices: 55.2 us -> 17.4 us  [the longest x6 16.9 us: per_device(): lax.ppermute(halves[s + half], 'dp', [(i, partner(i, s)) for i in range(g...]
    unnamed x81 -> x23, local copies, waits for them, and re-layouts: 27.5 us -> 2.55 us
    all_to_all x1, waiting for transfers between devices: 0.01 us -> 24.2 us  [per_device(): lax.all_to_all(back, 'expert', split_axis=0, concat_axis=0, tiled=True)]
    pallas_call x0 -> x1, Pallas kernels: none -> 8.24 us  [weight_over(): pl.pallas_call(weight_over_kernel, grid_spec=pltpu.PrefetchScalarGridSpec...]
    all_to_all x1, waiting for transfers between devices: 12.1 us -> 15.1 us  [per_device(): lax.all_to_all(send, 'expert', split_axis=0, concat_axis=0, tiled=True)]
    ppermute x6, waiting for transfers between devices: 11.2 us -> 13.7 us  [per_device(): lax.ppermute(block, 'expert', [(e, target(e, step, crosses)) for e in ran...]
    ppermute x7, starting transfers between devices: 12.6 us -> 10.2 us  [the longest x6 8.5 us: per_device(): lax.ppermute(halves[s + half], 'dp', [(i, partner(i, s)) for i in range(g...]
  transfers between devices with their start and end apart: 22 -> 22, of which waited for: 14 -> 15; matrix products, arithmetic and copies ran while one was open for 1% -> 2% of each run, Pallas kernels for 9% -> 16%
where the time goes in v4:
time: 187 us; the launch traced here: 186 us
  waiting for transfers between devices  97.1 us (52%)
  Pallas kernels  41.2 us (22%)
  starting transfers between devices  37.7 us (20%)
  local copies, waits for them, and re-layouts  5.45 us (3%)
  matrix products  3.3 us (2%)
    all_to_all x1, waiting for transfers between devices, per_device(): lax.all_to_all(back, 'expert', split_axis=0, concat_axis=0, tiled=True)  24.2 us
    ppermute x6, waiting for transfers between devices, per_device(): lax.ppermute(halves[s + half], 'dp', [(i, partner(i, s)) for i in range(g...  16.9 us
    all_to_all x1, waiting for transfers between devices, per_device(): lax.all_to_all(send, 'expert', split_axis=0, concat_axis=0, tiled=True)  15.1 us
    ppermute x2, waiting for transfers between devices, per_device(): left = lax.ppermute(left, 'expert', downs)  14.3 us
    ppermute x6, waiting for transfers between devices, per_device(): lax.ppermute(block, 'expert', [(e, target(e, step, crosses)) for e in ran...  13.7 us
    ppermute x6, starting transfers between devices, per_device(): lax.ppermute(halves[s + half], 'dp', [(i, partner(i, s)) for i in range(g...  8.5 us
    pallas_call x1, Pallas kernels, direct(): pl.pallas_call(direct_kernel, grid=(steps,), in_specs=[pl.BlockSpec((DIRE...  8.35 us
    pallas_call x1, Pallas kernels, weight_over(): pl.pallas_call(weight_over_kernel, grid_spec=pltpu.PrefetchScalarGridSpec...  8.24 us
  transfers between devices with their start and end apart: 22, of which 15 were waited for; matrix products, arithmetic and copies ran while one was open for 2% of the time, Pallas kernels for 16%

profile of v4, /device:TPU:14, one launch (start us, length us, event | category | flops | bytes accessed | tf_op | source)
XLA Modules:
  0.0 185.9 jit_solution(14132150190347613095)
XLA Ops:
  3.8 1.9 %pack.1 = (s32[1,128]{1,0:T(1,128)S(1)}, bf16[128,768]{1,0:T(8,128)(2,1)}, bf16[256,2816]{1,0:T(8,128)(2,1)S(1)}, bf16[64,2816]{1,0:T(8,128)(2,1)S(1)}) custom-call(s32[1]{0:T(128)} %bitcast.1.me_ref, s32[1,256]{1,0:T(1,128)S(1)} %reshape.23.routes_ref, bf16[128,2048]{1,0:T(8,128)(2,1)S(1)} %copy-done.1, bf16[256,768]{1,0:T(8,128)(2,1)S(1)} %reshape.24.grads_ref), custom_call_target="tpu_custom_call" | custom-call | flops 1000000000 | bytes 4194304 | tf_op jit(solution)/shard_map/pack/pallas_call | solution.py:132
  5.6 5.9 %collective-permute-start.2 = (bf16[64,2816]{1,0:T(8,128)(2,1)S(1)}, bf16[64,2816]{1,0:T(8,128)(2,1)S(1)}, u32[]{:S(2)}, u32[]{:S(2)}) collective-permute-start(bf16[64,2816]{1,0:T(8,128)(2,1)S(1)} %get-tuple-element.41.refs_0_), channel_id=1, source_target_pairs={{0,14},{1,15},{2,0},{3,1},{4,2},{5,3},{6,4},{7,5},{8,6},{9,7},{10,... | collective-permute-start | bytes 1081352 | tf_op jit(solution)/shard_map/ppermute | solution.py:531
  11.5 7.7 %collective-permute-done.2.refs_2_ = bf16[64,2816]{1,0:T(8,128)(2,1)S(1)} collective-permute-done((bf16[64,2816]{1,0:T(8,128)(2,1)S(1)}, bf16[64,2816]{1,0:T(8,128)(2,1)S(1)}, u32[]{:S(2)}, u32[]{:S(2)}) %collective-permute-start.2) | collective-permute-done | bytes 360480 | tf_op jit(solution)/shard_map/ppermute | solution.py:531
  19.1 3.4 %collective-permute-done.refs_1_ = bf16[64,2816]{1,0:T(8,128)(2,1)S(1)} collective-permute-done((bf16[64,2816]{1,0:T(8,128)(2,1)S(1)}, bf16[64,2816]{1,0:T(8,128)(2,1)S(1)}, u32[]{:S(2)}, u32[]{:S(2)}) %collective-permute-start) | collective-permute-done | bytes 360480 | tf_op jit(solution)/shard_map/ppermute | solution.py:530
  24.3 1.7 collective-permute-start.1
  26.1 6.7 %collective-permute-done.3.refs_1_.refs_4_.refs_5_ = bf16[64,2816]{1,0:T(8,128)(2,1)S(1)} collective-permute-done((bf16[64,2816]{1,0:T(8,128)(2,1)S(1)}, bf16[64,2816]{1,0:T(8,128)(2,1)S(1)}, u32[]{:S(2)}, u32[]{:S(2)}) %collective-permute-start.3) | collective-permute-done | bytes 360480 | tf_op jit(solution)/shard_map/ppermute | solution.py:531
  32.7 1.5 collective-permute-done.1.refs_0_.refs_2_.refs_3_
  35.2 3.0 %collective-permute-start.5 = (bf16[32,2816]{1,0:T(8,128)(2,1)S(1)}, bf16[32,2816]{1,0:T(8,128)(2,1)S(1)}, u32[]{:S(2)}, u32[]{:S(2)}) collective-permute-start(bf16[32,2816]{1,0:T(8,128)(2,1)S(1)} %get-tuple-element.43), channel_id=1, source_target_pairs={{0,14},{1,15},{2,0},{3,1},{4,2},{5,3},{6,4},{7,5},{8,6},{9,7},{10,... | collective-permute-start | bytes 540680 | tf_op jit(solution)/shard_map/ppermute | solution.py:534
  38.8 1.3 collective-permute-start.8
  40.2 5.3 %collective-permute-done.4.refs_5_ = bf16[32,2816]{1,0:T(8,128)(2,1)S(1)} collective-permute-done((bf16[32,2816]{1,0:T(8,128)(2,1)S(1)}, bf16[32,2816]{1,0:T(8,128)(2,1)S(1)}, u32[]{:S(2)}, u32[]{:S(2)}) %collective-permute-start.4) | collective-permute-done | bytes 180256 | tf_op jit(solution)/shard_map/ppermute | solution.py:534
  45.6 1.8 collective-permute-start.11
  47.4 2.6 %collective-permute-done.6.refs_7_ = bf16[32,2816]{1,0:T(8,128)(2,1)S(1)} collective-permute-done((bf16[32,2816]{1,0:T(8,128)(2,1)S(1)}, bf16[32,2816]{1,0:T(8,128)(2,1)S(1)}, u32[]{:S(2)}, u32[]{:S(2)}) %collective-permute-start.6) | collective-permute-done | bytes 180256 | tf_op jit(solution)/shard_map/ppermute | solution.py:534
  50.0 4.6 %collective-permute-done.9.refs_10_ = bf16[32,2816]{1,0:T(8,128)(2,1)S(1)} collective-permute-done((bf16[32,2816]{1,0:T(8,128)(2,1)S(1)}, bf16[32,2816]{1,0:T(8,128)(2,1)S(1)}, u32[]{:S(2)}, u32[]{:S(2)}) %collective-permute-start.9) | collective-permute-done | bytes 180256 | tf_op jit(solution)/shard_map/ppermute | solution.py:534
  55.8 1.9 %collective-permute-done.8.refs_9_ = bf16[64,2816]{1,0:T(8,128)(2,1)S(1)} collective-permute-done((bf16[64,2816]{1,0:T(8,128)(2,1)S(1)}, bf16[64,2816]{1,0:T(8,128)(2,1)S(1)}, u32[]{:S(2)}, u32[]{:S(2)}) %collective-permute-start.8) | collective-permute-done | bytes 360480 | tf_op jit(solution)/shard_map/ppermute | solution.py:539
  58.4 5.7 %all-to-all-start = ((bf16[16,16,2816]{2,1,0:T(8,128)(2,1)}), bf16[16,16,2816]{2,1,0:T(8,128)(2,1)S(1)}, u32[]{:S(2)}, u32[]{:S(2)}) async-start(bf16[16,16,2816]{2,1,0:T(8,128)(2,1)} %bitcast.18), calls=%async_computation | async-start | bytes 2883584 | tf_op jit(solution)/shard_map/all_to_all | solution.py:542
  64.8 7.7 %over.1 = (bf16[512,2048]{1,0:T(8,128)(2,1)}, bf16[512,1536]{1,0:T(8,128)(2,1)}, bf16[768,2048]{1,0:T(8,128)(2,1)}) custom-call(s32[128]{0:T(128)S(1)} %bitcast.22, bf16[64,2816]{1,0:T(8,128)(2,1)S(1)} %get-tuple-element.41.refs_0_, bf16[64,2816]{1,0:T(8,128)(2,1)S(1)} %collective-permute-done.refs_1_, bf16[64,2816]{1,0:T(8,128)(2,1)S(1)} %collective-permute-done.2.refs_2_, ...), custom_call_target="tpu_custom_call" | custom-call | flops 6442450944 | bytes 17825792 | tf_op jit(solution)/shard_map/over/pallas_call | solution.py:278
  72.5 8.2 %weight_over.1.part_ref = f32[2048,1536]{1,0:T(8,128)} custom-call(s32[16]{0:T(128)S(1)} %dynamic-slice_bitcast_fusion.block_ref, s32[128]{0:T(128)S(1)} %bitcast.23, bf16[512,2048]{1,0:T(8,128)(2,1)} %get-tuple-element.57.x_ref, bf16[512,1536]{1,0:T(8,128)(2,1)} %get-tuple-element.58.delta_ref), custom_call_target="tpu_custom_call" | custom-call | flops 3221225472 | bytes 17825792 | tf_op jit(solution)/shard_map/weight_over/pallas_call | solution.py:404
  80.8 15.1 %all-to-all-done = bf16[16,16,2816]{2,1,0:T(8,128)(2,1)S(1)} async-done(((bf16[16,16,2816]{2,1,0:T(8,128)(2,1)}), bf16[16,16,2816]{2,1,0:T(8,128)(2,1)S(1)}, u32[]{:S(2)}, u32[]{:S(2)}) %all-to-all-start) | async-done | bytes 1441824 | tf_op jit(solution)/shard_map/all_to_all | solution.py:542
  95.8 8.3 %direct.1 = (bf16[256,1536]{1,0:T(8,128)(2,1)}, bf16[768,2048]{1,0:T(8,128)(2,1)}) custom-call(bf16[256,2816]{1,0:T(8,128)(2,1)S(1)} %bitcast.14, bf16[256,2816]{1,0:T(8,128)(2,1)S(1)} %bitcast.15, bf16[1,2048,768]{2,1,0:T(8,128)(2,1)} %wg_ref.1, bf16[1,2048,768]{2,1,0:T(8,128)(2,1)} %wu_ref.1, ...), custom_call_target="tpu_custom_call", output_to_operand_aliasing={{1}: (4, {})} | custom-call | flops 3221225472 | bytes 10485760 | tf_op jit(solution)/shard_map/direct/pallas_call | solution.py:346
  104.2 6.3 %all-to-all-start.1 = ((bf16[16,48,2048]{2,1,0:T(8,128)(2,1)}), bf16[16,48,2048]{2,1,0:T(8,128)(2,1)}, u32[]{:S(2)}, u32[]{:S(2)}) async-start(bf16[16,48,2048]{2,1,0:T(8,128)(2,1)} %bitcast.24), calls=%async_computation.1 | async-start | bytes 6291456 | tf_op jit(solution)/shard_map/all_to_all | solution.py:551
  110.5 6.2 %weight_send.1 = bf16[1024,1536]{1,0:T(8,128)(2,1)S(1)} custom-call(s32[16]{0:T(128)S(1)} %dynamic-slice_bitcast_fusion.block_ref, bf16[256,2816]{1,0:T(8,128)(2,1)S(1)} %bitcast.16, bf16[256,1536]{1,0:T(8,128)(2,1)} %get-tuple-element.61.delta_ref, f32[2048,1536]{1,0:T(8,128)} %weight_over.1.part_ref), custom_call_target="tpu_custom_call" | custom-call | flops 805306368 | bytes 11534336 | tf_op jit(solution)/shard_map/weight_send/pallas_call | solution.py:446
  116.8 5.6 %collective-permute-done.12.came_ref = bf16[1024,1536]{1,0:T(8,128)(2,1)S(1)} collective-permute-done((bf16[1024,1536]{1,0:T(8,128)(2,1)S(1)}, bf16[1024,1536]{1,0:T(8,128)(2,1)S(1)}, u32[]{:S(2)}, u32[]{:S(2)}) %collective-permute-start.12) | collective-permute-done | bytes 3145760 | tf_op jit(solution)/shard_map/ppermute | solution.py:554
  122.5 7.1 %weight_keep.1 = (f32[128,1536]{1,0:T(8,128)S(1)}, f32[128,1536]{1,0:T(8,128)S(1)}, bf16[128,1536]{1,0:T(8,128)(2,1)}, bf16[128,1536]{1,0:T(8,128)(2,1)S(1)}, bf...) custom-call(s32[16]{0:T(128)S(1)} %dynamic-slice_bitcast_fusion.bloc, ...), custom_call_target="tpu_custom_call" | custom-call | flops 805306368 | bytes 14680064 | tf_op jit(solution)/shard_map/weight_keep/pallas_call | solution.py:481
  129.5 2.3 %collective-permute-start.13 = (bf16[128,1536]{1,0:T(8,128)(2,1)S(1)}, bf16[128,1536]{1,0:T(8,128)(2,1)S(1)}, u32[]{:S(2)}, u32[]{:S(2)}) collective-permute-start(bf16[128,1536]{1,0:T(8,128)(2,1)S(1)} %get-tuple-element.64), channel_id=1, source_target_pairs={{0,128},{16,144},{32,160},{48,176},{64,192},{80,208},{96,224},{112... | collective-permute-start | bytes 1179656 | tf_op jit(solution)/shard_map/ppermute | solution.py:559
  131.9 2.0 %collective-permute-start.15 = (bf16[128,1536]{1,0:T(8,128)(2,1)S(1)}, bf16[128,1536]{1,0:T(8,128)(2,1)S(1)}, u32[]{:S(2)}, u32[]{:S(2)}) collective-permute-start(bf16[128,1536]{1,0:T(8,128)(2,1)S(1)} %get-tuple-element.66), channel_id=1, source_target_pairs={{0,192},{16,208},{32,224},{48,240},{64,0},{80,16},{96,32},{112,48}... | collective-permute-start | bytes 1179656 | tf_op jit(solution)/shard_map/ppermute | solution.py:559
  133.9 9.2 %collective-permute-done.13 = bf16[128,1536]{1,0:T(8,128)(2,1)S(1)} collective-permute-done((bf16[128,1536]{1,0:T(8,128)(2,1)S(1)}, bf16[128,1536]{1,0:T(8,128)(2,1)S(1)}, u32[]{:S(2)}, u32[]{:S(2)}) %collective-permute-start.13) | collective-permute-done | bytes 393248 | tf_op jit(solution)/shard_map/ppermute | solution.py:559
  143.1 7.8 %collective-permute-done.14 = bf16[128,1536]{1,0:T(8,128)(2,1)S(1)} collective-permute-done((bf16[128,1536]{1,0:T(8,128)(2,1)S(1)}, bf16[128,1536]{1,0:T(8,128)(2,1)S(1)}, u32[]{:S(2)}, u32[]{:S(2)}) %collective-permute-start.14) | collective-permute-done | bytes 393248 | tf_op jit(solution)/shard_map/ppermute | solution.py:559
  151.0 1.7 collective-permute-start.16
  152.7 2.1 %collective-permute-start.17 = (bf16[128,1536]{1,0:T(8,128)(2,1)}, bf16[128,1536]{1,0:T(8,128)(2,1)S(1)}, u32[]{:S(2)}, u32[]{:S(2)}) collective-permute-start(bf16[128,1536]{1,0:T(8,128)(2,1)} %get-tuple-element.71), channel_id=1, source_target_pairs={{0,128},{16,144},{32,160},{48,176},{64,192},{80,208},{96,224},{112... | collective-permute-start | bytes 1179656 | tf_op jit(solution)/shard_map/ppermute | solution.py:559
  154.8 2.0 %collective-permute-start.19 = (bf16[128,1536]{1,0:T(8,128)(2,1)S(1)}, bf16[128,1536]{1,0:T(8,128)(2,1)S(1)}, u32[]{:S(2)}, u32[]{:S(2)}) collective-permute-start(bf16[128,1536]{1,0:T(8,128)(2,1)S(1)} %get-tuple-element.73), channel_id=1, source_target_pairs={{0,192},{16,208},{32,224},{48,240},{64,0},{80,16},{96,32},{112,48}... | collective-permute-start | bytes 1179656 | tf_op jit(solution)/shard_map/ppermute | solution.py:559
  156.8 24.2 %all-to-all-done.1 = bf16[16,48,2048]{2,1,0:T(8,128)(2,1)} async-done(((bf16[16,48,2048]{2,1,0:T(8,128)(2,1)}), bf16[16,48,2048]{2,1,0:T(8,128)(2,1)}, u32[]{:S(2)}, u32[]{:S(2)}) %all-to-all-start.1) | async-done | bytes 3145760 | tf_op jit(solution)/shard_map/all_to_all | solution.py:551
  181.0 3.3 %convolution_convert_fusion = bf16[128,2048]{1,0:T(8,128)(2,1)} fusion(bf16[128,768]{1,0:T(8,128)(2,1)S(1)} %copy-done.2, bf16[768,2048]{1,0:T(8,128)(2,1)} %bitcast.6), kind=kOutput, calls=%fused_computation | convolution fusion | flops 402915328 | bytes 3866624 | tf_op jit(solution)/shard_map/dot_general | solution.py:567
  (51 shorter events, 11.1 us)
Async XLA Ops:
  2.7 1.0 copy-start.1
  5.6 52.1 %copy-start = (bf16[256,2816]{1,0:T(8,128)(2,1)}, bf16[256,2816]{1,0:T(8,128)(2,1)S(1)}, u32[]{:S(2)}) copy-start(bf16[256,2816]{1,0:T(8,128)(2,1)S(1)} %get-tuple-element.48) | copy-start | bytes 4325380
  5.6 13.5 %collective-permute-start.2 = (bf16[64,2816]{1,0:T(8,128)(2,1)S(1)}, bf16[64,2816]{1,0:T(8,128)(2,1)S(1)}, u32[]{:S(2)}, u32[]{:S(2)}) collective-permute-start(bf16[64,2816]{1,0:T(8,128)(2,1)S(1)} %get-tuple-element.41.refs_0_), channel_id=1, source_target_pairs={{0,14},{1,15},{2,0},{3,1},{4,2},{5,3},{6,4},{7,5},{8,6},{9,7},{10,... | collective-permute-start | bytes 1081352 | tf_op jit(solution)/shard_map/ppermute | solution.py:531
  11.5 11.1 %collective-permute-start = (bf16[64,2816]{1,0:T(8,128)(2,1)S(1)}, bf16[64,2816]{1,0:T(8,128)(2,1)S(1)}, u32[]{:S(2)}, u32[]{:S(2)}) collective-permute-start(bf16[64,2816]{1,0:T(8,128)(2,1)S(1)} %get-tuple-element.41.refs_0_), channel_id=1, source_target_pairs={{0,2},{1,3},{2,4},{3,5},{4,6},{5,7},{6,8},{7,9},{8,10},{9,11},{10,... | collective-permute-start | bytes 1081352 | tf_op jit(solution)/shard_map/ppermute | solution.py:530
  23.1 16.9 %collective-permute-start.7 = (bf16[96,2816]{1,0:T(8,128)(2,1)S(1)}, bf16[96,2816]{1,0:T(8,128)(2,1)S(1)}, u32[]{:S(2)}, u32[]{:S(2)}) collective-permute-start(bf16[96,2816]{1,0:T(8,128)(2,1)S(1)} %choose.2), channel_id=1, source_target_pairs={{0,1},{1,0},{2,3},{3,2},{4,5},{5,4},{6,7},{7,6},{8,9},{9,8},{10,11... | collective-permute-start | bytes 1622024 | tf_op jit(solution)/shard_map/ppermute | solution.py:539
  24.1 8.7 %collective-permute-start.3 = (bf16[64,2816]{1,0:T(8,128)(2,1)S(1)}, bf16[64,2816]{1,0:T(8,128)(2,1)S(1)}, u32[]{:S(2)}, u32[]{:S(2)}) collective-permute-start(bf16[64,2816]{1,0:T(8,128)(2,1)S(1)} %collective-permute-done.2.refs_2_), channel_id=1, source_target_pairs={{0,14},{1,15},{2,0},{3,1},{4,2},{5,3},{6,4},{7,5},{8,6},{9,7},{10,... | collective-permute-start | bytes 1081352 | tf_op jit(solution)/shard_map/ppermute | solution.py:531
  24.3 9.9 %collective-permute-start.1 = (bf16[64,2816]{1,0:T(8,128)(2,1)S(1)}, bf16[64,2816]{1,0:T(8,128)(2,1)S(1)}, u32[]{:S(2)}, u32[]{:S(2)}) collective-permute-start(bf16[64,2816]{1,0:T(8,128)(2,1)S(1)} %collective-permute-done.refs_1_), channel_id=1, source_target_pairs={{0,2},{1,3},{2,4},{3,5},{4,6},{5,7},{6,8},{7,9},{8,10},{9,11},{10,... | collective-permute-start | bytes 1081352 | tf_op jit(solution)/shard_map/ppermute | solution.py:530
  34.9 10.6 %collective-permute-start.4 = (bf16[32,2816]{1,0:T(8,128)(2,1)S(1)}, bf16[32,2816]{1,0:T(8,128)(2,1)S(1)}, u32[]{:S(2)}, u32[]{:S(2)}) collective-permute-start(bf16[32,2816]{1,0:T(8,128)(2,1)S(1)} %get-tuple-element.42), channel_id=1, source_target_pairs={{0,2},{1,3},{2,4},{3,5},{4,6},{5,7},{6,8},{7,9},{8,10},{9,11},{10,... | collective-permute-start | bytes 540680 | tf_op jit(solution)/shard_map/ppermute | solution.py:534
  35.2 10.4 %collective-permute-start.5 = (bf16[32,2816]{1,0:T(8,128)(2,1)S(1)}, bf16[32,2816]{1,0:T(8,128)(2,1)S(1)}, u32[]{:S(2)}, u32[]{:S(2)}) collective-permute-start(bf16[32,2816]{1,0:T(8,128)(2,1)S(1)} %get-tuple-element.43), channel_id=1, source_target_pairs={{0,14},{1,15},{2,0},{3,1},{4,2},{5,3},{6,4},{7,5},{8,6},{9,7},{10,... | collective-permute-start | bytes 540680 | tf_op jit(solution)/shard_map/ppermute | solution.py:534
  38.8 18.9 %collective-permute-start.8 = (bf16[64,2816]{1,0:T(8,128)(2,1)S(1)}, bf16[64,2816]{1,0:T(8,128)(2,1)S(1)}, u32[]{:S(2)}, u32[]{:S(2)}) collective-permute-start(bf16[64,2816]{1,0:T(8,128)(2,1)S(1)} %choose.3), channel_id=1, source_target_pairs={{0,1},{1,0},{2,3},{3,2},{4,5},{5,4},{6,7},{7,6},{8,9},{9,8},{10,11... | collective-permute-start | bytes 1081352 | tf_op jit(solution)/shard_map/ppermute | solution.py:539
  40.1 9.9 %collective-permute-start.6 = (bf16[32,2816]{1,0:T(8,128)(2,1)S(1)}, bf16[32,2816]{1,0:T(8,128)(2,1)S(1)}, u32[]{:S(2)}, u32[]{:S(2)}) collective-permute-start(bf16[32,2816]{1,0:T(8,128)(2,1)S(1)} %get-tuple-element.44), channel_id=1, source_target_pairs={{0,4},{1,5},{2,6},{3,7},{4,8},{5,9},{6,10},{7,11},{8,12},{9,13},{1... | collective-permute-start | bytes 540680 | tf_op jit(solution)/shard_map/ppermute | solution.py:534
  40.1 17.6 %copy-start.3 = (bf16[96,2816]{1,0:T(8,128)(2,1)}, bf16[96,2816]{1,0:T(8,128)(2,1)S(1)}, u32[]{:S(2)}) copy-start(bf16[96,2816]{1,0:T(8,128)(2,1)S(1)} %collective-permute-done.7.refs_8_) | copy-start | bytes 1622020
  40.1 14.5 %collective-permute-start.9 = (bf16[32,2816]{1,0:T(8,128)(2,1)S(1)}, bf16[32,2816]{1,0:T(8,128)(2,1)S(1)}, u32[]{:S(2)}, u32[]{:S(2)}) collective-permute-start(bf16[32,2816]{1,0:T(8,128)(2,1)S(1)} %get-tuple-element.45), channel_id=1, source_target_pairs={{0,3},{1,2},{2,5},{3,4},{4,7},{5,6},{6,9},{7,8},{8,11},{9,10},{10,... | collective-permute-start | bytes 540680 | tf_op jit(solution)/shard_map/ppermute | solution.py:534
  45.5 19.3 %copy-start.5 = (bf16[32,2816]{1,0:T(8,128)(2,1)}, bf16[32,2816]{1,0:T(8,128)(2,1)S(1)}, u32[]{:S(2)}) copy-start(bf16[32,2816]{1,0:T(8,128)(2,1)S(1)} %collective-permute-done.4.refs_5_) | copy-start | bytes 540676
  45.5 10.3 %collective-permute-start.10 = (bf16[32,2816]{1,0:T(8,128)(2,1)S(1)}, bf16[32,2816]{1,0:T(8,128)(2,1)S(1)}, u32[]{:S(2)}, u32[]{:S(2)}) collective-permute-start(bf16[32,2816]{1,0:T(8,128)(2,1)S(1)} %get-tuple-element.46), channel_id=1, source_target_pairs={{0,15},{1,14},{2,1},{3,0},{4,3},{5,2},{6,5},{7,4},{8,7},{9,6},{10,... | collective-permute-start | bytes 540680 | tf_op jit(solution)/shard_map/ppermute | solution.py:534
  45.6 12.1 %copy-start.6 = (bf16[32,2816]{1,0:T(8,128)(2,1)}, bf16[32,2816]{1,0:T(8,128)(2,1)S(1)}, u32[]{:S(2)}) copy-start(bf16[32,2816]{1,0:T(8,128)(2,1)S(1)} %collective-permute-done.5.refs_6_) | copy-start | bytes 540676
  45.6 10.2 %collective-permute-start.11 = (bf16[32,2816]{1,0:T(8,128)(2,1)S(1)}, bf16[32,2816]{1,0:T(8,128)(2,1)S(1)}, u32[]{:S(2)}, u32[]{:S(2)}) collective-permute-start(bf16[32,2816]{1,0:T(8,128)(2,1)S(1)} %get-tuple-element.47), channel_id=1, source_target_pairs={{0,13},{1,12},{2,15},{3,14},{4,1},{5,0},{6,3},{7,2},{8,5},{9,4},{1... | collective-permute-start | bytes 540680 | tf_op jit(solution)/shard_map/ppermute | solution.py:534
  50.0 7.7 %copy-start.7 = (bf16[32,2816]{1,0:T(8,128)(2,1)}, bf16[32,2816]{1,0:T(8,128)(2,1)S(1)}, u32[]{:S(2)}) copy-start(bf16[32,2816]{1,0:T(8,128)(2,1)S(1)} %collective-permute-done.6.refs_7_) | copy-start | bytes 540676
  54.6 3.1 %copy-start.8 = (bf16[32,2816]{1,0:T(8,128)(2,1)}, bf16[32,2816]{1,0:T(8,128)(2,1)S(1)}, u32[]{:S(2)}) copy-start(bf16[32,2816]{1,0:T(8,128)(2,1)S(1)} %collective-permute-done.9.refs_10_) | copy-start | bytes 540676
  55.8 1.9 %copy-start.9 = (bf16[32,2816]{1,0:T(8,128)(2,1)}, bf16[32,2816]{1,0:T(8,128)(2,1)S(1)}, u32[]{:S(2)}) copy-start(bf16[32,2816]{1,0:T(8,128)(2,1)S(1)} %collective-permute-done.10.refs_11_) | copy-start | bytes 540676
  55.8 1.9 %copy-start.10 = (bf16[32,2816]{1,0:T(8,128)(2,1)}, bf16[32,2816]{1,0:T(8,128)(2,1)S(1)}, u32[]{:S(2)}) copy-start(bf16[32,2816]{1,0:T(8,128)(2,1)S(1)} %collective-permute-done.11.refs_12_) | copy-start | bytes 540676
  58.4 37.4 %all-to-all-start = ((bf16[16,16,2816]{2,1,0:T(8,128)(2,1)}), bf16[16,16,2816]{2,1,0:T(8,128)(2,1)S(1)}, u32[]{:S(2)}, u32[]{:S(2)}) async-start(bf16[16,16,2816]{2,1,0:T(8,128)(2,1)} %bitcast.18), calls=%async_computation | async-start | bytes 2883584 | tf_op jit(solution)/shard_map/all_to_all | solution.py:542
  104.2 76.8 %all-to-all-start.1 = ((bf16[16,48,2048]{2,1,0:T(8,128)(2,1)}), bf16[16,48,2048]{2,1,0:T(8,128)(2,1)}, u32[]{:S(2)}, u32[]{:S(2)}) async-start(bf16[16,48,2048]{2,1,0:T(8,128)(2,1)} %bitcast.24), calls=%async_computation.1 | async-start | bytes 6291456 | tf_op jit(solution)/shard_map/all_to_all | solution.py:551
  116.7 64.3 %copy-start.2 = (bf16[128,768]{1,0:T(8,128)(2,1)S(1)}, bf16[128,768]{1,0:T(8,128)(2,1)}, u32[]{:S(2)}) copy-start(bf16[128,768]{1,0:T(8,128)(2,1)} %get-tuple-element.67) | copy-start | bytes 589828
  116.7 5.7 %collective-permute-start.12 = (bf16[1024,1536]{1,0:T(8,128)(2,1)S(1)}, bf16[1024,1536]{1,0:T(8,128)(2,1)S(1)}, u32[]{:S(2)}, u32[]{:S(2)}) collective-permute-start(bf16[1024,1536]{1,0:T(8,128)(2,1)S(1)} %weight_send.1), channel_id=1, source_target_pairs={{0,16},{16,0},{32,48},{48,32},{64,80},{80,64},{96,112},{112,96},{1... | collective-permute-start | bytes 9437192 | tf_op jit(solution)/shard_map/ppermute | solution.py:554
  129.5 13.5 %collective-permute-start.13 = (bf16[128,1536]{1,0:T(8,128)(2,1)S(1)}, bf16[128,1536]{1,0:T(8,128)(2,1)S(1)}, u32[]{:S(2)}, u32[]{:S(2)}) collective-permute-start(bf16[128,1536]{1,0:T(8,128)(2,1)S(1)} %get-tuple-element.64), channel_id=1, source_target_pairs={{0,128},{16,144},{32,160},{48,176},{64,192},{80,208},{96,224},{112... | collective-permute-start | bytes 1179656 | tf_op jit(solution)/shard_map/ppermute | solution.py:559
  131.9 18.9 %collective-permute-start.14 = (bf16[128,1536]{1,0:T(8,128)(2,1)S(1)}, bf16[128,1536]{1,0:T(8,128)(2,1)S(1)}, u32[]{:S(2)}, u32[]{:S(2)}) collective-permute-start(bf16[128,1536]{1,0:T(8,128)(2,1)S(1)} %get-tuple-element.65), channel_id=1, source_target_pairs={{0,64},{16,80},{32,96},{48,112},{64,128},{80,144},{96,160},{112,17... | collective-permute-start | bytes 1179656 | tf_op jit(solution)/shard_map/ppermute | solution.py:559
  131.9 18.9 %collective-permute-start.15 = (bf16[128,1536]{1,0:T(8,128)(2,1)S(1)}, bf16[128,1536]{1,0:T(8,128)(2,1)S(1)}, u32[]{:S(2)}, u32[]{:S(2)}) collective-permute-start(bf16[128,1536]{1,0:T(8,128)(2,1)S(1)} %get-tuple-element.66), channel_id=1, source_target_pairs={{0,192},{16,208},{32,224},{48,240},{64,0},{80,16},{96,32},{112,48}... | collective-permute-start | bytes 1179656 | tf_op jit(solution)/shard_map/ppermute | solution.py:559
  151.0 33.8 %collective-permute-start.16 = (bf16[128,1536]{1,0:T(8,128)(2,1)S(1)}, bf16[128,1536]{1,0:T(8,128)(2,1)S(1)}, u32[]{:S(2)}, u32[]{:S(2)}) collective-permute-start(bf16[128,1536]{1,0:T(8,128)(2,1)S(1)} %add_convert_fusion), channel_id=1, source_target_pairs={{0,32},{16,48},{32,0},{48,16},{64,96},{80,112},{96,64},{112,80},{1... | collective-permute-start | bytes 1179656 | tf_op jit(solution)/shard_map/ppermute | solution.py:564
  152.7 32.1 %collective-permute-start.17 = (bf16[128,1536]{1,0:T(8,128)(2,1)}, bf16[128,1536]{1,0:T(8,128)(2,1)S(1)}, u32[]{:S(2)}, u32[]{:S(2)}) collective-permute-start(bf16[128,1536]{1,0:T(8,128)(2,1)} %get-tuple-element.71), channel_id=1, source_target_pairs={{0,128},{16,144},{32,160},{48,176},{64,192},{80,208},{96,224},{112... | collective-permute-start | bytes 1179656 | tf_op jit(solution)/shard_map/ppermute | solution.py:559
  154.8 30.0 %collective-permute-start.18 = (bf16[128,1536]{1,0:T(8,128)(2,1)}, bf16[128,1536]{1,0:T(8,128)(2,1)S(1)}, u32[]{:S(2)}, u32[]{:S(2)}) collective-permute-start(bf16[128,1536]{1,0:T(8,128)(2,1)} %get-tuple-element.72), channel_id=1, source_target_pairs={{0,64},{16,80},{32,96},{48,112},{64,128},{80,144},{96,160},{112,17... | collective-permute-start | bytes 1179656 | tf_op jit(solution)/shard_map/ppermute | solution.py:559
  154.8 30.0 %collective-permute-start.19 = (bf16[128,1536]{1,0:T(8,128)(2,1)S(1)}, bf16[128,1536]{1,0:T(8,128)(2,1)S(1)}, u32[]{:S(2)}, u32[]{:S(2)}) collective-permute-start(bf16[128,1536]{1,0:T(8,128)(2,1)S(1)} %get-tuple-element.73), channel_id=1, source_target_pairs={{0,192},{16,208},{32,224},{48,240},{64,0},{80,16},{96,32},{112,48}... | collective-permute-start | bytes 1179656 | tf_op jit(solution)/shard_map/ppermute | solution.py:559
  (1 other events, 0.7 us)

commit v5 on v4

--- a/solution.py
+++ b/solution.py
@@ -18,10 +18,10 @@
 DIRECT = EXPERTS * COLD
 OVER = EXPERTS * SPILL
 WIDTH = D + FF
-OFFSETS = (0, -1, 1, -2, 2, -3, 3, 4)
+OFFSETS = (0, -1, 1, -2, 2, 4, -3, 3)
 PIECES = ((0, 3), (3, 5))
 SLOT_ME, HOT_ME, SLOT_BESIDE, ME = range(4)
-HOPS = ((0, 1, False), (1, -1, False), (0, 2, False), (0, 1, True), (1, -1, True), (1, -2, True))
+HOPS = ((0, 2, False), (1, -2, True), (0, 1, False), (1, -1, False), (0, 1, True), (1, -1, True))
 SLOT_HOP = 4
 BLOCK = 128
 FF_BLOCK = 256
@@ -38,24 +38,47 @@
 
 
 def pack_kernel(
-    me_ref, routes_ref, tokens_ref, grads_ref, choice_ref, sel_ref, out_ref, over_ref
+    me_ref,
+    routes_ref,
+    all_tokens_ref,
+    all_grads_ref,
+    choice_ref,
+    sel_ref,
+    out_ref,
+    over_ref,
+    tokens_ref,
+    grads_ref,
+    sems,
 ):
-    pairs = routes_ref.shape[1]
-    toks = tokens_ref.shape[0]
+    copies = [
+        pltpu.make_async_copy(all_tokens_ref, tokens_ref, sems.at[0]),
+        pltpu.make_async_copy(all_grads_ref, grads_ref, sems.at[1]),
+    ]
+    for copy in copies:
+        copy.start()
+    toks = routes_ref.shape[1]
     me = me_ref[0]
-    routes = routes_ref[...]
-    member = (routes == lax.broadcasted_iota(jnp.int32, (EXPERTS, pairs), 0)).astype(jnp.float32)
+    routes = [routes_ref[k : k + 1, :] for k in range(2)]
+    expert_ids = lax.broadcasted_iota(jnp.int32, (EXPERTS, toks), 0)
+    members = [(r == expert_ids).astype(jnp.float32) for r in routes]
+    member = members[0] + members[1]
     member_low = member.astype(jnp.bfloat16)
-    earlier = (
-        lax.broadcasted_iota(jnp.int32, (pairs, pairs), 0)
-        < lax.broadcasted_iota(jnp.int32, (pairs, pairs), 1)
-    ).astype(jnp.bfloat16)
-    before = jnp.dot(member_low, earlier, preferred_element_type=jnp.float32)
-    rank = jnp.sum(member * before, axis=0, keepdims=True).astype(jnp.int32)
+    token_down = lax.broadcasted_iota(jnp.int32, (toks, toks), 0)
+    token_across = lax.broadcasted_iota(jnp.int32, (toks, toks), 1)
+    before = jnp.dot(
+        member_low,
+        (token_down < token_across).astype(jnp.bfloat16),
+        preferred_element_type=jnp.float32,
+    )
+
+    def of_pair(table):
+        return [jnp.sum(m * table, axis=0, keepdims=True).astype(jnp.int32) for m in members]
+
+    ranks = of_pair(before)
 
     count_col = jnp.sum(member, axis=1, keepdims=True)
     count_row = lax.dot_general(
-        jnp.ones((8, pairs), jnp.bfloat16),
+        jnp.ones((8, toks), jnp.bfloat16),
         member_low,
         (((1,), (1,)), ((), ())),
         preferred_element_type=jnp.float32,
@@ -68,7 +91,7 @@
     hot_row = (above_row < 1.5).astype(jnp.float32)
     which_col = jnp.sum(hot_row * (across < down).astype(jnp.float32), axis=1, keepdims=True)
     which_row = jnp.sum(hot_col * (down < across).astype(jnp.float32), axis=0, keepdims=True)
-    which = jnp.sum(member * which_col, axis=0, keepdims=True).astype(jnp.int32)
+    whiches = of_pair(which_col)
 
     lane16 = lax.broadcasted_iota(jnp.int32, (1, EXPERTS), 1)
 
@@ -92,46 +115,49 @@
         choice = jnp.where(lane == at, value, choice)
     choice_ref[...] = choice
 
-    to_token = (
-        lax.broadcasted_iota(jnp.int32, (pairs, toks), 0) // 2
-        == lax.broadcasted_iota(jnp.int32, (pairs, toks), 1)
-    ).astype(jnp.bfloat16)
-
-    def picked(slot, rows):
-        pick = (slot == lax.broadcasted_iota(jnp.int32, (rows, pairs), 0)).astype(jnp.bfloat16)
-        tok = jnp.dot(pick, to_token, preferred_element_type=jnp.float32).astype(jnp.bfloat16)
-        return pick, tok
-
-    def fill(ref, slot):
-        pick, tok = picked(slot, ref.shape[0])
-        ref[:, :D] = jnp.dot(tok, tokens_ref[...], preferred_element_type=jnp.float32).astype(
-            jnp.bfloat16
-        )
-        ref[:, D:] = jnp.dot(pick, grads_ref[...], preferred_element_type=jnp.float32).astype(
-            jnp.bfloat16
-        )
-
-    fill(over_ref, jnp.where(rank >= COLD, which * SPILL + rank - COLD, -1))
-    fill(out_ref, jnp.where(rank < COLD, routes * COLD + rank, -1))
-    back = routes * CAP + rank == lax.broadcasted_iota(jnp.int32, (ROWS, pairs), 0)
-    of_token = (
-        lax.broadcasted_iota(jnp.int32, (toks, pairs), 1) // 2
-        == lax.broadcasted_iota(jnp.int32, (toks, pairs), 0)
-    ).astype(jnp.bfloat16)
+    def picked(slots, rows):
+        at = lax.broadcasted_iota(jnp.int32, (rows, toks), 0)
+        return [(slot == at).astype(jnp.bfloat16) for slot in slots]
+
+    def fill(ref, slots):
+        first, second = picked(slots, ref.shape[0])
+        ref[:, :D] = jnp.dot(
+            first + second, tokens_ref[...], preferred_element_type=jnp.float32
+        ).astype(jnp.bfloat16)
+        ref[:, D:] = (
+            jnp.dot(first, grads_ref[0], preferred_element_type=jnp.float32)
+            + jnp.dot(second, grads_ref[1], preferred_element_type=jnp.float32)
+        ).astype(jnp.bfloat16)
+
+    first, second = picked([r * CAP + rank for r, rank in zip(routes, ranks)], ROWS)
     sel_ref[...] = lax.dot_general(
-        of_token,
-        back.astype(jnp.bfloat16),
+        (token_down == token_across).astype(jnp.bfloat16),
+        first + second,
         (((1,), (1,)), ((), ())),
         preferred_element_type=jnp.float32,
     ).astype(jnp.bfloat16)
+    for copy in copies:
+        copy.wait()
+    fill(
+        over_ref,
+        [
+            jnp.where(rank >= COLD, which * SPILL + rank - COLD, -1)
+            for which, rank in zip(whiches, ranks)
+        ],
+    )
+    fill(
+        out_ref,
+        [jnp.where(rank < COLD, r * COLD + rank, -1) for r, rank in zip(routes, ranks)],
+    )
 
 
 def pack(me, routes, tokens, grads):
-    toks, pairs = tokens.shape[0], grads.shape[0]
+    toks = tokens.shape[0]
     vmem = pl.BlockSpec(memory_space=pltpu.VMEM)
+    hbm = pl.BlockSpec(memory_space=pltpu.HBM)
     return pl.pallas_call(
         pack_kernel,
-        in_specs=[pl.BlockSpec(memory_space=pltpu.SMEM), vmem, vmem, vmem],
+        in_specs=[pl.BlockSpec(memory_space=pltpu.SMEM), vmem, hbm, hbm],
         out_specs=[vmem] * 4,
         out_shape=[
             jax.ShapeDtypeStruct((1, 128), jnp.int32),
@@ -139,10 +165,15 @@
             jax.ShapeDtypeStruct((DIRECT, WIDTH), jnp.bfloat16),
             jax.ShapeDtypeStruct((2 * SPILL, WIDTH), jnp.bfloat16),
         ],
+        scratch_shapes=[
+            pltpu.VMEM(tokens.shape, tokens.dtype),
+            pltpu.VMEM(grads.shape, grads.dtype),
+            pltpu.SemaphoreType.DMA((2,)),
+        ],
         compiler_params=pltpu.CompilerParams(vmem_limit_bytes=12 * MIB),
         cost_estimate=pl.CostEstimate(flops=10**9, bytes_accessed=4 * MIB, transcendentals=0),
         name="pack",
-    )(me, routes, tokens, grads)
+    )(me, routes, in_hbm(tokens), in_hbm(grads))
 
 
 def choose_kernel(choice_ref, *refs):
@@ -307,72 +338,85 @@
 
 
 def direct_kernel(
-    x_ref, dh_ref, wg_ref, wu_ref, old_ref, delta_ref, back_ref, acc_ref, low_ref, sems
+    got_ref,
+    all_wg_ref,
+    all_wu_ref,
+    old_ref,
+    delta_ref,
+    back_ref,
+    wg_ref,
+    wu_ref,
+    low_ref,
+    high_ref,
+    in_sems,
+    out_sems,
 ):
-    j = pl.program_id(0)
-    delta_g, delta_u = deltas(x_ref[...], dh_ref[...], wg_ref[0], wu_ref[0])
-    part = back_rows(delta_g, delta_u, wg_ref[0], wu_ref[0])
-    put_deltas(delta_ref, j, delta_g, delta_u)
-    last = pl.num_programs(0) - 1
-
-    @pl.when(j == 0)
-    def _():
-        acc_ref[...] = part
-
-    @pl.when(jnp.logical_and(j > 0, j < last))
-    def _():
-        acc_ref[...] += part
-
-    @pl.when(j == last)
-    def _():
-        low_ref[...] = (acc_ref[...] + part).astype(jnp.bfloat16)
-        copies = [
-            pltpu.make_async_copy(
-                low_ref.at[pl.ds(e * COLD, COLD), :],
-                back_ref.at[pl.ds(e * CAP, COLD), :],
-                sems.at[e],
-            )
-            for e in range(EXPERTS)
+    parts = [slice(k * FF_BLOCK, (k + 1) * FF_BLOCK) for k in range(FF // FF_BLOCK)]
+    loads = [
+        [
+            pltpu.make_async_copy(all_ref.at[0, :, part], ref.at[:, part], in_sems.at[which, k])
+            for which, (all_ref, ref) in enumerate(((all_wg_ref, wg_ref), (all_wu_ref, wu_ref)))
         ]
-        for copy in copies:
-            copy.start()
-        for copy in copies:
-            copy.wait()
+        for k, part in enumerate(parts)
+    ]
+    for pair in loads:
+        for load in pair:
+            load.start()
+    x = got_ref[:, :D]
+    for k, part in enumerate(parts):
+        for load in loads[k]:
+            load.wait()
+        dh = got_ref[:, D + part.start : D + part.stop]
+        delta_g, delta_u = deltas(x, dh, wg_ref[:, part], wu_ref[:, part])
+        delta_ref[:, part] = delta_g
+        delta_ref[:, FF + part.start : FF + part.stop] = delta_u
+    width = D // 4
+    stores = []
+    for q in range(4):
+        rows = slice(q * width, (q + 1) * width)
+        back = back_rows(delta_ref[:, :FF], delta_ref[:, FF:], wg_ref[rows, :], wu_ref[rows, :])
+        half_ref = low_ref if q < 2 else high_ref
+        half_ref[:, q % 2 * width : (q % 2 + 1) * width] = back.astype(jnp.bfloat16)
+        if q % 2 == 1:
+            columns = slice((q - 1) * width, (q + 1) * width)
+            for e in range(EXPERTS):
+                store = pltpu.make_async_copy(
+                    half_ref.at[e * COLD : (e + 1) * COLD, :],
+                    back_ref.at[e * CAP : e * CAP + COLD, columns],
+                    out_sems.at[q // 2, e],
+                )
+                store.start()
+                stores.append(store)
+    for store in stores:
+        store.wait()
 
 
 def direct(got, w_gate, w_up, back):
-    steps = FF // FF_BLOCK
-    off = D // FF_BLOCK
+    vmem = pl.BlockSpec(memory_space=pltpu.VMEM)
+    hbm = pl.BlockSpec(memory_space=pltpu.HBM)
     return pl.pallas_call(
         direct_kernel,
-        grid=(steps,),
-        in_specs=[
-            pl.BlockSpec((DIRECT, D), lambda j: (0, 0)),
-            pl.BlockSpec((DIRECT, FF_BLOCK), lambda j: (0, off + j)),
-            pl.BlockSpec((1, D, FF_BLOCK), lambda j: (0, 0, j)),
-            pl.BlockSpec((1, D, FF_BLOCK), lambda j: (0, 0, j)),
-            pl.BlockSpec(memory_space=pltpu.HBM),
-        ],
-        out_specs=[
-            pl.BlockSpec((DIRECT, 2 * FF), lambda j: (0, 0)),
-            pl.BlockSpec(memory_space=pltpu.HBM),
-        ],
+        in_specs=[vmem, hbm, hbm, hbm],
+        out_specs=[vmem, hbm],
         out_shape=[
             pltpu.HBM((DIRECT, 2 * FF), jnp.bfloat16),
             pltpu.HBM((ROWS, D), jnp.bfloat16),
         ],
         scratch_shapes=[
-            pltpu.VMEM((DIRECT, D), jnp.float32),
-            pltpu.VMEM((DIRECT, D), jnp.bfloat16),
-            pltpu.SemaphoreType.DMA((EXPERTS,)),
+            pltpu.VMEM((D, FF), jnp.bfloat16),
+            pltpu.VMEM((D, FF), jnp.bfloat16),
+            pltpu.VMEM((DIRECT, D // 2), jnp.bfloat16),
+            pltpu.VMEM((DIRECT, D // 2), jnp.bfloat16),
+            pltpu.SemaphoreType.DMA((2, FF // FF_BLOCK)),
+            pltpu.SemaphoreType.DMA((2, EXPERTS)),
         ],
-        input_output_aliases={4: 1},
-        compiler_params=pltpu.CompilerParams(vmem_limit_bytes=20 * MIB),
+        input_output_aliases={3: 1},
+        compiler_params=pltpu.CompilerParams(vmem_limit_bytes=24 * MIB),
         cost_estimate=pl.CostEstimate(
             flops=8 * DIRECT * D * FF, bytes_accessed=10 * MIB, transcendentals=DIRECT * FF
         ),
         name="direct",
-    )(got, got, w_gate, w_up, pltpu.with_memory_space_constraint(back, pltpu.HBM))
+    )(got, w_gate, w_up, pltpu.with_memory_space_constraint(back, pltpu.HBM))
 
 
 def turned(x_ref, turned_ref, block_ref, first):
@@ -507,16 +551,14 @@
 
 
 def per_device(tokens, routes, grad_hidden, w_gate, w_up):
-    toks, per_token = routes.shape
-    pairs = toks * per_token
     groups = lax.axis_size("dp")
     steps = groups // 2
     expert_at = lax.axis_index("expert")
     choice, sel, send, spill = pack(
         expert_at.reshape(1).astype(jnp.int32),
-        routes.reshape(1, pairs),
+        routes.T,
         tokens,
-        grad_hidden.reshape(pairs, grad_hidden.shape[2]),
+        grad_hidden.transpose(1, 0, 2),
     )
     choice = choice.reshape(128)
     w_gate, w_up = in_hbm(w_gate), in_hbm(w_up)
@@ -537,7 +579,8 @@
         for block, (_, step, crosses) in zip(hop_rows(choice, (right, left)), HOPS)
     ]
     pieces = [lax.ppermute(choose(choice, column[a:b]), "expert", beside) for a, b in PIECES]
-    rest = [*hops[:3], *pieces, *hops[3:]]
+    crossing = [hop for hop, (_, _, crosses) in zip(hops, HOPS) if crosses]
+    rest = [hop for hop, (_, _, crosses) in zip(hops, HOPS) if not crosses] + pieces + crossing
     send, *rest = lax.optimization_barrier((send, *rest))
     got = lax.all_to_all(send, "expert", split_axis=0, concat_axis=0, tiled=True)
     rest = [in_hbm(a) for a in rest]

time: 187 us -> 186 us (level)
  waiting for transfers between devices: 97.1 us -> 90.6 us
  starting transfers between devices: 37.7 us -> 43.6 us
    ppermute x6, starting transfers between devices: 5.32 us -> 11 us  [per_device(): lax.ppermute(block, 'expert', [(e, target(e, step, crosses)) for e in ran...]
    ppermute x6, waiting for transfers between devices: 13.7 us -> 8.96 us  [per_device(): lax.ppermute(block, 'expert', [(e, target(e, step, crosses)) for e in ran...]
    ppermute x2, waiting for transfers between devices: 1.89 us -> 0.01 us  [per_device(): lax.ppermute(choose(choice, column[a:b]), 'expert', beside)]
  transfers between devices with their start and end apart: 22 -> 22, of which waited for: 15 -> 14; matrix products, arithmetic and copies ran while one was open for 2% -> 2% of each run, Pallas kernels for 16% -> 17%
where the time goes in v5:
time: 186 us; the launch traced here: 184 us
  waiting for transfers between devices  90.6 us (49%)
  starting transfers between devices  43.6 us (23%)
  Pallas kernels  40.4 us (22%)
  local copies, waits for them, and re-layouts  4.84 us (3%)
  matrix products  3.3 us (2%)
    all_to_all x1, waiting for transfers between devices, per_device(): lax.all_to_all(back, 'expert', split_axis=0, concat_axis=0, tiled=True)  24.7 us
    ppermute x6, waiting for transfers between devices, per_device(): lax.ppermute(halves[s + half], 'dp', [(i, partner(i, s)) for i in range(g...  16.9 us
    all_to_all x1, waiting for transfers between devices, per_device(): lax.all_to_all(send, 'expert', split_axis=0, concat_axis=0, tiled=True)  15.1 us
    ppermute x2, waiting for transfers between devices, per_device(): left = lax.ppermute(left, 'expert', downs)  14.3 us
    ppermute x6, starting transfers between devices, per_device(): lax.ppermute(block, 'expert', [(e, target(e, step, crosses)) for e in ran...  11 us
    ppermute x6, waiting for transfers between devices, per_device(): lax.ppermute(block, 'expert', [(e, target(e, step, crosses)) for e in ran...  8.96 us
    ppermute x6, starting transfers between devices, per_device(): lax.ppermute(halves[s + half], 'dp', [(i, partner(i, s)) for i in range(g...  8.48 us
    pallas_call x1, Pallas kernels, weight_over(): pl.pallas_call(weight_over_kernel, grid_spec=pltpu.PrefetchScalarGridSpec...  8.24 us
  transfers between devices with their start and end apart: 22, of which 14 were waited for; matrix products, arithmetic and copies ran while one was open for 2% of the time, Pallas kernels for 17%

profile of v5, /device:TPU:14, one launch (start us, length us, event | category | flops | bytes accessed | tf_op | source)
XLA Modules:
  0.0 184.0 jit_solution(10590003179169747137)
XLA Ops:
  0.6 1.8 copy.12
  3.1 2.0 %pack.1 = (s32[1,128]{1,0:T(1,128)S(1)}, bf16[128,768]{1,0:T(8,128)(2,1)}, bf16[256,2816]{1,0:T(8,128)(2,1)S(1)}, bf16[64,2816]{1,0:T(8,128)(2,1)S(1)}) custom-call(s32[1]{0:T(128)} %bitcast.1.me_ref, s32[2,128]{1,0:T(2,128)S(1)} %bitcast.27, bf16[128,2048]{1,0:T(8,128)(2,1)} %all_tokens_ref.1, bf16[2,128,768]{2,1,0:T(8,128)(2,1)} %bitcast.29), custom_call_target="tpu_custom_call" | custom-call | flops 1000000000 | bytes 4194304 | tf_op jit(solution)/shard_map/pack/pallas_call | solution.py:158
  5.1 5.9 %collective-permute-start.2 = (bf16[64,2816]{1,0:T(8,128)(2,1)S(1)}, bf16[64,2816]{1,0:T(8,128)(2,1)S(1)}, u32[]{:S(2)}, u32[]{:S(2)}) collective-permute-start(bf16[64,2816]{1,0:T(8,128)(2,1)S(1)} %get-tuple-element.41.refs_0_), channel_id=1, source_target_pairs={{0,14},{1,15},{2,0},{3,1},{4,2},{5,3},{6,4},{7,5},{8,6},{9,7},{10,... | collective-permute-start | bytes 1081352 | tf_op jit(solution)/shard_map/ppermute | solution.py:573
  11.0 7.7 %collective-permute-done.2.refs_2_ = bf16[64,2816]{1,0:T(8,128)(2,1)S(1)} collective-permute-done((bf16[64,2816]{1,0:T(8,128)(2,1)S(1)}, bf16[64,2816]{1,0:T(8,128)(2,1)S(1)}, u32[]{:S(2)}, u32[]{:S(2)}) %collective-permute-start.2) | collective-permute-done | bytes 360480 | tf_op jit(solution)/shard_map/ppermute | solution.py:573
  18.7 3.4 %collective-permute-done.refs_1_ = bf16[64,2816]{1,0:T(8,128)(2,1)S(1)} collective-permute-done((bf16[64,2816]{1,0:T(8,128)(2,1)S(1)}, bf16[64,2816]{1,0:T(8,128)(2,1)S(1)}, u32[]{:S(2)}, u32[]{:S(2)}) %collective-permute-start) | collective-permute-done | bytes 360480 | tf_op jit(solution)/shard_map/ppermute | solution.py:572
  23.9 1.7 collective-permute-start.1
  25.6 6.7 %collective-permute-done.3.refs_1_.refs_3_.refs_5_.refs_4_ = bf16[64,2816]{1,0:T(8,128)(2,1)S(1)} collective-permute-done((bf16[64,2816]{1,0:T(8,128)(2,1)S(1)}, bf16[64,2816]{1,0:T(8,128)(2,1)S(1)}, u32[]{:S(2)}, u32[]{:S(2)}) %collective-permute-start.3) | collective-permute-done | bytes 360480 | tf_op jit(solution)/shard_map/ppermute | solution.py:573
  32.3 1.5 collective-permute-done.1.refs_0_.refs_2_.refs_4_.refs_3_
  36.7 3.0 %collective-permute-start.6 = (bf16[32,2816]{1,0:T(8,128)(2,1)S(1)}, bf16[32,2816]{1,0:T(8,128)(2,1)S(1)}, u32[]{:S(2)}, u32[]{:S(2)}) collective-permute-start(bf16[32,2816]{1,0:T(8,128)(2,1)S(1)} %get-tuple-element.44), channel_id=1, source_target_pairs={{0,14},{1,15},{2,0},{3,1},{4,2},{5,3},{6,4},{7,5},{8,6},{9,7},{10,... | collective-permute-start | bytes 540680 | tf_op jit(solution)/shard_map/ppermute | solution.py:576
  39.7 3.1 %collective-permute-start.9 = (bf16[32,2816]{1,0:T(8,128)(2,1)S(1)}, bf16[32,2816]{1,0:T(8,128)(2,1)S(1)}, u32[]{:S(2)}, u32[]{:S(2)}) collective-permute-start(bf16[32,2816]{1,0:T(8,128)(2,1)S(1)} %get-tuple-element.45), channel_id=1, source_target_pairs={{0,13},{1,12},{2,15},{3,14},{4,1},{5,0},{6,3},{7,2},{8,5},{9,4},{1... | collective-permute-start | bytes 540680 | tf_op jit(solution)/shard_map/ppermute | solution.py:576
  42.8 2.9 %collective-permute-done.4.refs_5_ = bf16[32,2816]{1,0:T(8,128)(2,1)S(1)} collective-permute-done((bf16[32,2816]{1,0:T(8,128)(2,1)S(1)}, bf16[32,2816]{1,0:T(8,128)(2,1)S(1)}, u32[]{:S(2)}, u32[]{:S(2)}) %collective-permute-start.4) | collective-permute-done | bytes 180256 | tf_op jit(solution)/shard_map/ppermute | solution.py:576
  46.8 4.0 %collective-permute-start.11 = (bf16[32,2816]{1,0:T(8,128)(2,1)S(1)}, bf16[32,2816]{1,0:T(8,128)(2,1)S(1)}, u32[]{:S(2)}, u32[]{:S(2)}) collective-permute-start(bf16[32,2816]{1,0:T(8,128)(2,1)S(1)} %get-tuple-element.47), channel_id=1, source_target_pairs={{0,15},{1,14},{2,1},{3,0},{4,3},{5,2},{6,5},{7,4},{8,7},{9,6},{10,... | collective-permute-start | bytes 540680 | tf_op jit(solution)/shard_map/ppermute | solution.py:576
  50.8 1.8 collective-permute-done.9.refs_10_
  52.6 2.0 %collective-permute-done.10.refs_11_ = bf16[32,2816]{1,0:T(8,128)(2,1)S(1)} collective-permute-done((bf16[32,2816]{1,0:T(8,128)(2,1)S(1)}, bf16[32,2816]{1,0:T(8,128)(2,1)S(1)}, u32[]{:S(2)}, u32[]{:S(2)}) %collective-permute-start.10) | collective-permute-done | bytes 180256 | tf_op jit(solution)/shard_map/ppermute | solution.py:576
  54.6 1.6 collective-permute-done.11.refs_12_
  57.1 6.0 %all-to-all-start = ((bf16[16,16,2816]{2,1,0:T(8,128)(2,1)}), bf16[16,16,2816]{2,1,0:T(8,128)(2,1)S(1)}, u32[]{:S(2)}, u32[]{:S(2)}) async-start(bf16[16,16,2816]{2,1,0:T(8,128)(2,1)} %bitcast.21), calls=%async_computation | async-start | bytes 2883584 | tf_op jit(solution)/shard_map/all_to_all | solution.py:585
  63.8 7.7 %over.1 = (bf16[512,2048]{1,0:T(8,128)(2,1)}, bf16[512,1536]{1,0:T(8,128)(2,1)}, bf16[768,2048]{1,0:T(8,128)(2,1)}) custom-call(s32[128]{0:T(128)S(1)} %bitcast.25, bf16[64,2816]{1,0:T(8,128)(2,1)S(1)} %get-tuple-element.41.refs_0_, bf16[64,2816]{1,0:T(8,128)(2,1)S(1)} %collective-permute-done.refs_1_, bf16[64,2816]{1,0:T(8,128)(2,1)S(1)} %collective-permute-done.2.refs_2_, ...), custom_call_target="tpu_custom_call" | custom-call | flops 6442450944 | bytes 17825792 | tf_op jit(solution)/shard_map/over/pallas_call | solution.py:309
  71.5 8.2 %weight_over.1.part_ref = f32[2048,1536]{1,0:T(8,128)} custom-call(s32[16]{0:T(128)S(1)} %dynamic-slice_bitcast_fusion.block_ref, s32[128]{0:T(128)S(1)} %bitcast.26, bf16[512,2048]{1,0:T(8,128)(2,1)} %get-tuple-element.57.x_ref, bf16[512,1536]{1,0:T(8,128)(2,1)} %get-tuple-element.58.delta_ref), custom_call_target="tpu_custom_call" | custom-call | flops 3221225472 | bytes 17825792 | tf_op jit(solution)/shard_map/weight_over/pallas_call | solution.py:448
  79.7 15.1 %all-to-all-done = bf16[16,16,2816]{2,1,0:T(8,128)(2,1)S(1)} async-done(((bf16[16,16,2816]{2,1,0:T(8,128)(2,1)}), bf16[16,16,2816]{2,1,0:T(8,128)(2,1)S(1)}, u32[]{:S(2)}, u32[]{:S(2)}) %all-to-all-start) | async-done | bytes 1441824 | tf_op jit(solution)/shard_map/all_to_all | solution.py:585
  94.9 7.5 %direct.1 = (bf16[256,1536]{1,0:T(8,128)(2,1)}, bf16[768,2048]{1,0:T(8,128)(2,1)}) custom-call(bf16[256,2816]{1,0:T(8,128)(2,1)S(1)} %bitcast.18, bf16[1,2048,768]{2,1,0:T(8,128)(2,1)} %all_wg_ref.1, bf16[1,2048,768]{2,1,0:T(8,128)(2,1)} %all_wu_ref.1, bf16[768,2048]{1,0:T(8,128)(2,1)} %get-tuple-element.60.old_ref), custom_call_target="tpu_custom_call", output_to_operand_aliasing={{1}: (3, {})} | custom-call | flops 3221225472 | bytes 10485760 | tf_op jit(solution)/shard_map/direct/pallas_call | solution.py:397
  102.4 6.4 %all-to-all-start.1 = ((bf16[16,48,2048]{2,1,0:T(8,128)(2,1)}), bf16[16,48,2048]{2,1,0:T(8,128)(2,1)}, u32[]{:S(2)}, u32[]{:S(2)}) async-start(bf16[16,48,2048]{2,1,0:T(8,128)(2,1)} %bitcast.28), calls=%async_computation.1 | async-start | bytes 6291456 | tf_op jit(solution)/shard_map/all_to_all | solution.py:594
  108.8 6.2 %weight_send.1 = bf16[1024,1536]{1,0:T(8,128)(2,1)S(1)} custom-call(s32[16]{0:T(128)S(1)} %dynamic-slice_bitcast_fusion.block_ref, bf16[256,2816]{1,0:T(8,128)(2,1)S(1)} %bitcast.19, bf16[256,1536]{1,0:T(8,128)(2,1)} %get-tuple-element.61.delta_ref, f32[2048,1536]{1,0:T(8,128)} %weight_over.1.part_ref), custom_call_target="tpu_custom_call" | custom-call | flops 805306368 | bytes 11534336 | tf_op jit(solution)/shard_map/weight_send/pallas_call | solution.py:490
  115.1 5.6 %collective-permute-done.12.came_ref = bf16[1024,1536]{1,0:T(8,128)(2,1)S(1)} collective-permute-done((bf16[1024,1536]{1,0:T(8,128)(2,1)S(1)}, bf16[1024,1536]{1,0:T(8,128)(2,1)S(1)}, u32[]{:S(2)}, u32[]{:S(2)}) %collective-permute-start.12) | collective-permute-done | bytes 3145760 | tf_op jit(solution)/shard_map/ppermute | solution.py:597
  120.8 7.1 %weight_keep.1 = (f32[128,1536]{1,0:T(8,128)S(1)}, f32[128,1536]{1,0:T(8,128)S(1)}, bf16[128,1536]{1,0:T(8,128)(2,1)}, bf16[128,1536]{1,0:T(8,128)(2,1)S(1)}, bf...) custom-call(s32[16]{0:T(128)S(1)} %dynamic-slice_bitcast_fusion.bloc, ...), custom_call_target="tpu_custom_call" | custom-call | flops 805306368 | bytes 14680064 | tf_op jit(solution)/shard_map/weight_keep/pallas_call | solution.py:525
  127.8 2.3 %collective-permute-start.13 = (bf16[128,1536]{1,0:T(8,128)(2,1)S(1)}, bf16[128,1536]{1,0:T(8,128)(2,1)S(1)}, u32[]{:S(2)}, u32[]{:S(2)}) collective-permute-start(bf16[128,1536]{1,0:T(8,128)(2,1)S(1)} %get-tuple-element.64), channel_id=1, source_target_pairs={{0,128},{16,144},{32,160},{48,176},{64,192},{80,208},{96,224},{112... | collective-permute-start | bytes 1179656 | tf_op jit(solution)/shard_map/ppermute | solution.py:602
  130.1 2.0 %collective-permute-start.15 = (bf16[128,1536]{1,0:T(8,128)(2,1)S(1)}, bf16[128,1536]{1,0:T(8,128)(2,1)S(1)}, u32[]{:S(2)}, u32[]{:S(2)}) collective-permute-start(bf16[128,1536]{1,0:T(8,128)(2,1)S(1)} %get-tuple-element.66), channel_id=1, source_target_pairs={{0,192},{16,208},{32,224},{48,240},{64,0},{80,16},{96,32},{112,48}... | collective-permute-start | bytes 1179656 | tf_op jit(solution)/shard_map/ppermute | solution.py:602
  132.2 9.2 %collective-permute-done.13 = bf16[128,1536]{1,0:T(8,128)(2,1)S(1)} collective-permute-done((bf16[128,1536]{1,0:T(8,128)(2,1)S(1)}, bf16[128,1536]{1,0:T(8,128)(2,1)S(1)}, u32[]{:S(2)}, u32[]{:S(2)}) %collective-permute-start.13) | collective-permute-done | bytes 393248 | tf_op jit(solution)/shard_map/ppermute | solution.py:602
  141.4 7.7 %collective-permute-done.14 = bf16[128,1536]{1,0:T(8,128)(2,1)S(1)} collective-permute-done((bf16[128,1536]{1,0:T(8,128)(2,1)S(1)}, bf16[128,1536]{1,0:T(8,128)(2,1)S(1)}, u32[]{:S(2)}, u32[]{:S(2)}) %collective-permute-start.14) | collective-permute-done | bytes 393248 | tf_op jit(solution)/shard_map/ppermute | solution.py:602
  150.7 2.1 %collective-permute-start.17 = (bf16[128,1536]{1,0:T(8,128)(2,1)}, bf16[128,1536]{1,0:T(8,128)(2,1)S(1)}, u32[]{:S(2)}, u32[]{:S(2)}) collective-permute-start(bf16[128,1536]{1,0:T(8,128)(2,1)} %get-tuple-element.71), channel_id=1, source_target_pairs={{0,128},{16,144},{32,160},{48,176},{64,192},{80,208},{96,224},{112... | collective-permute-start | bytes 1179656 | tf_op jit(solution)/shard_map/ppermute | solution.py:602
  152.8 2.0 %collective-permute-start.19 = (bf16[128,1536]{1,0:T(8,128)(2,1)S(1)}, bf16[128,1536]{1,0:T(8,128)(2,1)S(1)}, u32[]{:S(2)}, u32[]{:S(2)}) collective-permute-start(bf16[128,1536]{1,0:T(8,128)(2,1)S(1)} %get-tuple-element.73), channel_id=1, source_target_pairs={{0,192},{16,208},{32,224},{48,240},{64,0},{80,16},{96,32},{112,48}... | collective-permute-start | bytes 1179656 | tf_op jit(solution)/shard_map/ppermute | solution.py:602
  154.8 24.7 %all-to-all-done.1 = bf16[16,48,2048]{2,1,0:T(8,128)(2,1)} async-done(((bf16[16,48,2048]{2,1,0:T(8,128)(2,1)}), bf16[16,48,2048]{2,1,0:T(8,128)(2,1)}, u32[]{:S(2)}, u32[]{:S(2)}) %all-to-all-start.1) | async-done | bytes 3145760 | tf_op jit(solution)/shard_map/all_to_all | solution.py:594
  179.5 3.3 %convolution_convert_fusion = bf16[128,2048]{1,0:T(8,128)(2,1)} fusion(bf16[128,768]{1,0:T(8,128)(2,1)S(1)} %copy-done.2, bf16[768,2048]{1,0:T(8,128)(2,1)} %bitcast.8), kind=kOutput, calls=%fused_computation | convolution fusion | flops 402915328 | bytes 3866624 | tf_op jit(solution)/shard_map/dot_general | solution.py:610
  (49 shorter events, 10.6 us)
Async XLA Ops:
  2.4 0.7 copy-start.1
  5.1 51.2 %copy-start = (bf16[256,2816]{1,0:T(8,128)(2,1)}, bf16[256,2816]{1,0:T(8,128)(2,1)S(1)}, u32[]{:S(2)}) copy-start(bf16[256,2816]{1,0:T(8,128)(2,1)S(1)} %get-tuple-element.48) | copy-start | bytes 4325380
  5.1 13.6 %collective-permute-start.2 = (bf16[64,2816]{1,0:T(8,128)(2,1)S(1)}, bf16[64,2816]{1,0:T(8,128)(2,1)S(1)}, u32[]{:S(2)}, u32[]{:S(2)}) collective-permute-start(bf16[64,2816]{1,0:T(8,128)(2,1)S(1)} %get-tuple-element.41.refs_0_), channel_id=1, source_target_pairs={{0,14},{1,15},{2,0},{3,1},{4,2},{5,3},{6,4},{7,5},{8,6},{9,7},{10,... | collective-permute-start | bytes 1081352 | tf_op jit(solution)/shard_map/ppermute | solution.py:573
  11.0 11.1 %collective-permute-start = (bf16[64,2816]{1,0:T(8,128)(2,1)S(1)}, bf16[64,2816]{1,0:T(8,128)(2,1)S(1)}, u32[]{:S(2)}, u32[]{:S(2)}) collective-permute-start(bf16[64,2816]{1,0:T(8,128)(2,1)S(1)} %get-tuple-element.41.refs_0_), channel_id=1, source_target_pairs={{0,2},{1,3},{2,4},{3,5},{4,6},{5,7},{6,8},{7,9},{8,10},{9,11},{10,... | collective-permute-start | bytes 1081352 | tf_op jit(solution)/shard_map/ppermute | solution.py:572
  22.7 17.0 %collective-permute-start.7 = (bf16[96,2816]{1,0:T(8,128)(2,1)S(1)}, bf16[96,2816]{1,0:T(8,128)(2,1)S(1)}, u32[]{:S(2)}, u32[]{:S(2)}) collective-permute-start(bf16[96,2816]{1,0:T(8,128)(2,1)S(1)} %choose.2), channel_id=1, source_target_pairs={{0,1},{1,0},{2,3},{3,2},{4,5},{5,4},{6,7},{7,6},{8,9},{9,8},{10,11... | collective-permute-start | bytes 1622024 | tf_op jit(solution)/shard_map/ppermute | solution.py:581
  23.6 8.7 %collective-permute-start.3 = (bf16[64,2816]{1,0:T(8,128)(2,1)S(1)}, bf16[64,2816]{1,0:T(8,128)(2,1)S(1)}, u32[]{:S(2)}, u32[]{:S(2)}) collective-permute-start(bf16[64,2816]{1,0:T(8,128)(2,1)S(1)} %collective-permute-done.2.refs_2_), channel_id=1, source_target_pairs={{0,14},{1,15},{2,0},{3,1},{4,2},{5,3},{6,4},{7,5},{8,6},{9,7},{10,... | collective-permute-start | bytes 1081352 | tf_op jit(solution)/shard_map/ppermute | solution.py:573
  23.9 9.9 %collective-permute-start.1 = (bf16[64,2816]{1,0:T(8,128)(2,1)S(1)}, bf16[64,2816]{1,0:T(8,128)(2,1)S(1)}, u32[]{:S(2)}, u32[]{:S(2)}) collective-permute-start(bf16[64,2816]{1,0:T(8,128)(2,1)S(1)} %collective-permute-done.refs_1_), channel_id=1, source_target_pairs={{0,2},{1,3},{2,4},{3,5},{4,6},{5,7},{6,8},{7,9},{8,10},{9,11},{10,... | collective-permute-start | bytes 1081352 | tf_op jit(solution)/shard_map/ppermute | solution.py:572
  34.4 11.3 %collective-permute-start.4 = (bf16[32,2816]{1,0:T(8,128)(2,1)S(1)}, bf16[32,2816]{1,0:T(8,128)(2,1)S(1)}, u32[]{:S(2)}, u32[]{:S(2)}) collective-permute-start(bf16[32,2816]{1,0:T(8,128)(2,1)S(1)} %get-tuple-element.42), channel_id=1, source_target_pairs={{0,4},{1,5},{2,6},{3,7},{4,8},{5,9},{6,10},{7,11},{8,12},{9,13},{1... | collective-permute-start | bytes 540680 | tf_op jit(solution)/shard_map/ppermute | solution.py:576
  34.5 12.2 %collective-permute-start.5 = (bf16[32,2816]{1,0:T(8,128)(2,1)S(1)}, bf16[32,2816]{1,0:T(8,128)(2,1)S(1)}, u32[]{:S(2)}, u32[]{:S(2)}) collective-permute-start(bf16[32,2816]{1,0:T(8,128)(2,1)S(1)} %get-tuple-element.43), channel_id=1, source_target_pairs={{0,2},{1,3},{2,4},{3,5},{4,6},{5,7},{6,8},{7,9},{8,10},{9,11},{10,... | collective-permute-start | bytes 540680 | tf_op jit(solution)/shard_map/ppermute | solution.py:576
  35.4 20.9 %collective-permute-start.8 = (bf16[64,2816]{1,0:T(8,128)(2,1)S(1)}, bf16[64,2816]{1,0:T(8,128)(2,1)S(1)}, u32[]{:S(2)}, u32[]{:S(2)}) collective-permute-start(bf16[64,2816]{1,0:T(8,128)(2,1)S(1)} %choose.3), channel_id=1, source_target_pairs={{0,1},{1,0},{2,3},{3,2},{4,5},{5,4},{6,7},{7,6},{8,9},{9,8},{10,11... | collective-permute-start | bytes 1081352 | tf_op jit(solution)/shard_map/ppermute | solution.py:581
  36.7 14.1 %collective-permute-start.6 = (bf16[32,2816]{1,0:T(8,128)(2,1)S(1)}, bf16[32,2816]{1,0:T(8,128)(2,1)S(1)}, u32[]{:S(2)}, u32[]{:S(2)}) collective-permute-start(bf16[32,2816]{1,0:T(8,128)(2,1)S(1)} %get-tuple-element.44), channel_id=1, source_target_pairs={{0,14},{1,15},{2,0},{3,1},{4,2},{5,3},{6,4},{7,5},{8,6},{9,7},{10,... | collective-permute-start | bytes 540680 | tf_op jit(solution)/shard_map/ppermute | solution.py:576
  39.7 16.6 %copy-start.3 = (bf16[96,2816]{1,0:T(8,128)(2,1)}, bf16[96,2816]{1,0:T(8,128)(2,1)S(1)}, u32[]{:S(2)}) copy-start(bf16[96,2816]{1,0:T(8,128)(2,1)S(1)} %collective-permute-done.7.refs_8_) | copy-start | bytes 1622020
  39.7 12.9 %collective-permute-start.9 = (bf16[32,2816]{1,0:T(8,128)(2,1)S(1)}, bf16[32,2816]{1,0:T(8,128)(2,1)S(1)}, u32[]{:S(2)}, u32[]{:S(2)}) collective-permute-start(bf16[32,2816]{1,0:T(8,128)(2,1)S(1)} %get-tuple-element.45), channel_id=1, source_target_pairs={{0,13},{1,12},{2,15},{3,14},{4,1},{5,0},{6,3},{7,2},{8,5},{9,4},{1... | collective-permute-start | bytes 540680 | tf_op jit(solution)/shard_map/ppermute | solution.py:576
  45.7 18.1 %copy-start.5 = (bf16[32,2816]{1,0:T(8,128)(2,1)}, bf16[32,2816]{1,0:T(8,128)(2,1)S(1)}, u32[]{:S(2)}) copy-start(bf16[32,2816]{1,0:T(8,128)(2,1)S(1)} %collective-permute-done.4.refs_5_) | copy-start | bytes 540676
  45.7 8.9 %collective-permute-start.10 = (bf16[32,2816]{1,0:T(8,128)(2,1)S(1)}, bf16[32,2816]{1,0:T(8,128)(2,1)S(1)}, u32[]{:S(2)}, u32[]{:S(2)}) collective-permute-start(bf16[32,2816]{1,0:T(8,128)(2,1)S(1)} %get-tuple-element.46), channel_id=1, source_target_pairs={{0,3},{1,2},{2,5},{3,4},{4,7},{5,6},{6,9},{7,8},{8,11},{9,10},{10,... | collective-permute-start | bytes 540680 | tf_op jit(solution)/shard_map/ppermute | solution.py:576
  46.8 9.5 %copy-start.6 = (bf16[32,2816]{1,0:T(8,128)(2,1)}, bf16[32,2816]{1,0:T(8,128)(2,1)S(1)}, u32[]{:S(2)}) copy-start(bf16[32,2816]{1,0:T(8,128)(2,1)S(1)} %collective-permute-done.5.refs_6_) | copy-start | bytes 540676
  46.8 9.5 %collective-permute-start.11 = (bf16[32,2816]{1,0:T(8,128)(2,1)S(1)}, bf16[32,2816]{1,0:T(8,128)(2,1)S(1)}, u32[]{:S(2)}, u32[]{:S(2)}) collective-permute-start(bf16[32,2816]{1,0:T(8,128)(2,1)S(1)} %get-tuple-element.47), channel_id=1, source_target_pairs={{0,15},{1,14},{2,1},{3,0},{4,3},{5,2},{6,5},{7,4},{8,7},{9,6},{10,... | collective-permute-start | bytes 540680 | tf_op jit(solution)/shard_map/ppermute | solution.py:576
  50.8 5.5 %copy-start.7 = (bf16[32,2816]{1,0:T(8,128)(2,1)}, bf16[32,2816]{1,0:T(8,128)(2,1)S(1)}, u32[]{:S(2)}) copy-start(bf16[32,2816]{1,0:T(8,128)(2,1)S(1)} %collective-permute-done.6.refs_7_) | copy-start | bytes 540676
  52.6 3.7 %copy-start.8 = (bf16[32,2816]{1,0:T(8,128)(2,1)}, bf16[32,2816]{1,0:T(8,128)(2,1)S(1)}, u32[]{:S(2)}) copy-start(bf16[32,2816]{1,0:T(8,128)(2,1)S(1)} %collective-permute-done.9.refs_10_) | copy-start | bytes 540676
  54.6 1.7 copy-start.9
  56.3 0.8 copy-start.4
  57.1 37.8 %all-to-all-start = ((bf16[16,16,2816]{2,1,0:T(8,128)(2,1)}), bf16[16,16,2816]{2,1,0:T(8,128)(2,1)S(1)}, u32[]{:S(2)}, u32[]{:S(2)}) async-start(bf16[16,16,2816]{2,1,0:T(8,128)(2,1)} %bitcast.21), calls=%async_computation | async-start | bytes 2883584 | tf_op jit(solution)/shard_map/all_to_all | solution.py:585
  102.4 77.1 %all-to-all-start.1 = ((bf16[16,48,2048]{2,1,0:T(8,128)(2,1)}), bf16[16,48,2048]{2,1,0:T(8,128)(2,1)}, u32[]{:S(2)}, u32[]{:S(2)}) async-start(bf16[16,48,2048]{2,1,0:T(8,128)(2,1)} %bitcast.28), calls=%async_computation.1 | async-start | bytes 6291456 | tf_op jit(solution)/shard_map/all_to_all | solution.py:594
  115.0 64.5 %copy-start.2 = (bf16[128,768]{1,0:T(8,128)(2,1)S(1)}, bf16[128,768]{1,0:T(8,128)(2,1)}, u32[]{:S(2)}) copy-start(bf16[128,768]{1,0:T(8,128)(2,1)} %get-tuple-element.67) | copy-start | bytes 589828
  115.0 5.7 %collective-permute-start.12 = (bf16[1024,1536]{1,0:T(8,128)(2,1)S(1)}, bf16[1024,1536]{1,0:T(8,128)(2,1)S(1)}, u32[]{:S(2)}, u32[]{:S(2)}) collective-permute-start(bf16[1024,1536]{1,0:T(8,128)(2,1)S(1)} %weight_send.1), channel_id=1, source_target_pairs={{0,16},{16,0},{32,48},{48,32},{64,80},{80,64},{96,112},{112,96},{1... | collective-permute-start | bytes 9437192 | tf_op jit(solution)/shard_map/ppermute | solution.py:597
  127.8 13.5 %collective-permute-start.13 = (bf16[128,1536]{1,0:T(8,128)(2,1)S(1)}, bf16[128,1536]{1,0:T(8,128)(2,1)S(1)}, u32[]{:S(2)}, u32[]{:S(2)}) collective-permute-start(bf16[128,1536]{1,0:T(8,128)(2,1)S(1)} %get-tuple-element.64), channel_id=1, source_target_pairs={{0,128},{16,144},{32,160},{48,176},{64,192},{80,208},{96,224},{112... | collective-permute-start | bytes 1179656 | tf_op jit(solution)/shard_map/ppermute | solution.py:602
  130.1 18.9 %collective-permute-start.14 = (bf16[128,1536]{1,0:T(8,128)(2,1)S(1)}, bf16[128,1536]{1,0:T(8,128)(2,1)S(1)}, u32[]{:S(2)}, u32[]{:S(2)}) collective-permute-start(bf16[128,1536]{1,0:T(8,128)(2,1)S(1)} %get-tuple-element.65), channel_id=1, source_target_pairs={{0,64},{16,80},{32,96},{48,112},{64,128},{80,144},{96,160},{112,17... | collective-permute-start | bytes 1179656 | tf_op jit(solution)/shard_map/ppermute | solution.py:602
  130.1 18.9 %collective-permute-start.15 = (bf16[128,1536]{1,0:T(8,128)(2,1)S(1)}, bf16[128,1536]{1,0:T(8,128)(2,1)S(1)}, u32[]{:S(2)}, u32[]{:S(2)}) collective-permute-start(bf16[128,1536]{1,0:T(8,128)(2,1)S(1)} %get-tuple-element.66), channel_id=1, source_target_pairs={{0,192},{16,208},{32,224},{48,240},{64,0},{80,16},{96,32},{112,48}... | collective-permute-start | bytes 1179656 | tf_op jit(solution)/shard_map/ppermute | solution.py:602
  149.2 33.5 %collective-permute-start.16 = (bf16[128,1536]{1,0:T(8,128)(2,1)S(1)}, bf16[128,1536]{1,0:T(8,128)(2,1)S(1)}, u32[]{:S(2)}, u32[]{:S(2)}) collective-permute-start(bf16[128,1536]{1,0:T(8,128)(2,1)S(1)} %add_convert_fusion), channel_id=1, source_target_pairs={{0,32},{16,48},{32,0},{48,16},{64,96},{80,112},{96,64},{112,80},{1... | collective-permute-start | bytes 1179656 | tf_op jit(solution)/shard_map/ppermute | solution.py:607
  150.7 32.1 %collective-permute-start.17 = (bf16[128,1536]{1,0:T(8,128)(2,1)}, bf16[128,1536]{1,0:T(8,128)(2,1)S(1)}, u32[]{:S(2)}, u32[]{:S(2)}) collective-permute-start(bf16[128,1536]{1,0:T(8,128)(2,1)} %get-tuple-element.71), channel_id=1, source_target_pairs={{0,128},{16,144},{32,160},{48,176},{64,192},{80,208},{96,224},{112... | collective-permute-start | bytes 1179656 | tf_op jit(solution)/shard_map/ppermute | solution.py:602
  152.8 30.0 %collective-permute-start.18 = (bf16[128,1536]{1,0:T(8,128)(2,1)}, bf16[128,1536]{1,0:T(8,128)(2,1)S(1)}, u32[]{:S(2)}, u32[]{:S(2)}) collective-permute-start(bf16[128,1536]{1,0:T(8,128)(2,1)} %get-tuple-element.72), channel_id=1, source_target_pairs={{0,64},{16,80},{32,96},{48,112},{64,128},{80,144},{96,160},{112,17... | collective-permute-start | bytes 1179656 | tf_op jit(solution)/shard_map/ppermute | solution.py:602
  152.8 30.0 %collective-permute-start.19 = (bf16[128,1536]{1,0:T(8,128)(2,1)S(1)}, bf16[128,1536]{1,0:T(8,128)(2,1)S(1)}, u32[]{:S(2)}, u32[]{:S(2)}) collective-permute-start(bf16[128,1536]{1,0:T(8,128)(2,1)S(1)} %get-tuple-element.73), channel_id=1, source_target_pairs={{0,192},{16,208},{32,224},{48,240},{64,0},{80,16},{96,32},{112,48}... | collective-permute-start | bytes 1179656 | tf_op jit(solution)/shard_map/ppermute | solution.py:602
  (1 other events, 0.7 us)

commit v6 on v5

--- a/solution.py
+++ b/solution.py
@@ -19,7 +19,7 @@
 OVER = EXPERTS * SPILL
 WIDTH = D + FF
 OFFSETS = (0, -1, 1, -2, 2, 4, -3, 3)
-PIECES = ((0, 3), (3, 5))
+PIECES = ((0, 5),)
 SLOT_ME, HOT_ME, SLOT_BESIDE, ME = range(4)
 HOPS = ((0, 2, False), (1, -2, True), (0, 1, False), (1, -1, False), (0, 1, True), (1, -1, True))
 SLOT_HOP = 4
@@ -192,7 +192,7 @@
             out_specs=pl.BlockSpec((count * SPILL, WIDTH), lambda i, c: (0, 0)),
         ),
         out_shape=jax.ShapeDtypeStruct((count * SPILL, WIDTH), jnp.bfloat16),
-        compiler_params=pltpu.CompilerParams(vmem_limit_bytes=4 * MIB),
+        compiler_params=pltpu.CompilerParams(vmem_limit_bytes=8 * MIB),
         cost_estimate=pl.CostEstimate(
             flops=0, bytes_accessed=4 * count * SPILL * WIDTH, transcendentals=0
         ),

time: 186 us -> 193 us (1.038)
  waiting for transfers between devices: 90.6 us -> 99.9 us
    ppermute x2 -> x1, waiting for transfers between devices: 0.01 us -> 8.56 us  [per_device(): lax.ppermute(choose(choice, column[a:b]), 'expert', beside)]
    ppermute x2, starting transfers between devices: 6.22 us -> 9.63 us  [per_device(): left = lax.ppermute(left, 'expert', downs)]
    ppermute x6, waiting for transfers between devices: 8.96 us -> 11.4 us  [per_device(): lax.ppermute(block, 'expert', [(e, target(e, step, crosses)) for e in ran...]
  transfers between devices with their start and end apart: 22 -> 21, of which waited for: 14 -> 14; matrix products, arithmetic and copies ran while one was open for 2% -> 2% of each run, Pallas kernels for 17% -> 16%
where the time goes in v6:
time: 193 us; the launch traced here: 192 us
  waiting for transfers between devices  99.9 us (52%)
  starting transfers between devices  42.4 us (22%)
  Pallas kernels  39.8 us (21%)
  local copies, waits for them, and re-layouts  5.05 us (3%)
  matrix products  3.3 us (2%)
    all_to_all x1, waiting for transfers between devices, per_device(): lax.all_to_all(back, 'expert', split_axis=0, concat_axis=0, tiled=True)  23.5 us
    ppermute x6, waiting for transfers between devices, per_device(): lax.ppermute(halves[s + half], 'dp', [(i, partner(i, s)) for i in range(g...  16.9 us
    all_to_all x1, waiting for transfers between devices, per_device(): lax.all_to_all(send, 'expert', split_axis=0, concat_axis=0, tiled=True)  14.7 us
    ppermute x2, waiting for transfers between devices, per_device(): left = lax.ppermute(left, 'expert', downs)  14.5 us
    ppermute x6, waiting for transfers between devices, per_device(): lax.ppermute(block, 'expert', [(e, target(e, step, crosses)) for e in ran...  11.4 us
    ppermute x6, starting transfers between devices, per_device(): lax.ppermute(block, 'expert', [(e, target(e, step, crosses)) for e in ran...  9.77 us
    ppermute x2, starting transfers between devices, per_device(): left = lax.ppermute(left, 'expert', downs)  9.63 us
    ppermute x1, waiting for transfers between devices, per_device(): lax.ppermute(choose(choice, column[a:b]), 'expert', beside)  8.56 us
  transfers between devices with their start and end apart: 21, of which 14 were waited for; matrix products, arithmetic and copies ran while one was open for 2% of the time, Pallas kernels for 16%

profile of v6, /device:TPU:14, one launch (start us, length us, event | category | flops | bytes accessed | tf_op | source)
XLA Modules:
  0.0 191.7 jit_solution(18314997435465093005)
XLA Ops:
  0.6 1.8 copy.12
  3.1 2.0 %pack.1 = (s32[1,128]{1,0:T(1,128)S(1)}, bf16[128,768]{1,0:T(8,128)(2,1)}, bf16[256,2816]{1,0:T(8,128)(2,1)S(1)}, bf16[64,2816]{1,0:T(8,128)(2,1)S(1)}) custom-call(s32[1]{0:T(128)} %bitcast.1.me_ref, s32[2,128]{1,0:T(2,128)S(1)} %bitcast.26, bf16[128,2048]{1,0:T(8,128)(2,1)} %all_tokens_ref.1, bf16[2,128,768]{2,1,0:T(8,128)(2,1)} %bitcast.28), custom_call_target="tpu_custom_call" | custom-call | flops 1000000000 | bytes 4194304 | tf_op jit(solution)/shard_map/pack/pallas_call | solution.py:158
  5.1 5.9 %collective-permute-start.2 = (bf16[64,2816]{1,0:T(8,128)(2,1)S(1)}, bf16[64,2816]{1,0:T(8,128)(2,1)S(1)}, u32[]{:S(2)}, u32[]{:S(2)}) collective-permute-start(bf16[64,2816]{1,0:T(8,128)(2,1)S(1)} %get-tuple-element.40.refs_0_), channel_id=1, source_target_pairs={{0,14},{1,15},{2,0},{3,1},{4,2},{5,3},{6,4},{7,5},{8,6},{9,7},{10,... | collective-permute-start | bytes 1081352 | tf_op jit(solution)/shard_map/ppermute | solution.py:573
  11.0 7.7 %collective-permute-done.2.refs_2_ = bf16[64,2816]{1,0:T(8,128)(2,1)S(1)} collective-permute-done((bf16[64,2816]{1,0:T(8,128)(2,1)S(1)}, bf16[64,2816]{1,0:T(8,128)(2,1)S(1)}, u32[]{:S(2)}, u32[]{:S(2)}) %collective-permute-start.2) | collective-permute-done | bytes 360480 | tf_op jit(solution)/shard_map/ppermute | solution.py:573
  18.7 3.7 %collective-permute-start.3 = (bf16[64,2816]{1,0:T(8,128)(2,1)S(1)}, bf16[64,2816]{1,0:T(8,128)(2,1)S(1)}, u32[]{:S(2)}, u32[]{:S(2)}) collective-permute-start(bf16[64,2816]{1,0:T(8,128)(2,1)S(1)} %collective-permute-done.2.refs_2_), channel_id=1, source_target_pairs={{0,14},{1,15},{2,0},{3,1},{4,2},{5,3},{6,4},{7,5},{8,6},{9,7},{10,... | collective-permute-start | bytes 1081352 | tf_op jit(solution)/shard_map/ppermute | solution.py:573
  22.4 6.8 %collective-permute-done.3.refs_1_.refs_3_.refs_5_.refs_4_ = bf16[64,2816]{1,0:T(8,128)(2,1)S(1)} collective-permute-done((bf16[64,2816]{1,0:T(8,128)(2,1)S(1)}, bf16[64,2816]{1,0:T(8,128)(2,1)S(1)}, u32[]{:S(2)}, u32[]{:S(2)}) %collective-permute-start.3) | collective-permute-done | bytes 360480 | tf_op jit(solution)/shard_map/ppermute | solution.py:573
  29.2 3.4 %collective-permute-done.1.refs_0_.refs_2_.refs_4_.refs_3_ = bf16[64,2816]{1,0:T(8,128)(2,1)S(1)} collective-permute-done((bf16[64,2816]{1,0:T(8,128)(2,1)S(1)}, bf16[64,2816]{1,0:T(8,128)(2,1)S(1)}, u32[]{:S(2)}, u32[]{:S(2)}) %collective-permute-start.1) | collective-permute-done | bytes 360480 | tf_op jit(solution)/shard_map/ppermute | solution.py:572
  34.9 3.2 %collective-permute-start.6 = (bf16[32,2816]{1,0:T(8,128)(2,1)S(1)}, bf16[32,2816]{1,0:T(8,128)(2,1)S(1)}, u32[]{:S(2)}, u32[]{:S(2)}) collective-permute-start(bf16[32,2816]{1,0:T(8,128)(2,1)S(1)} %get-tuple-element.43), channel_id=1, source_target_pairs={{0,14},{1,15},{2,0},{3,1},{4,2},{5,3},{6,4},{7,5},{8,6},{9,7},{10,... | collective-permute-start | bytes 540680 | tf_op jit(solution)/shard_map/ppermute | solution.py:576
  38.2 3.5 %collective-permute-start.8 = (bf16[32,2816]{1,0:T(8,128)(2,1)S(1)}, bf16[32,2816]{1,0:T(8,128)(2,1)S(1)}, u32[]{:S(2)}, u32[]{:S(2)}) collective-permute-start(bf16[32,2816]{1,0:T(8,128)(2,1)S(1)} %get-tuple-element.44), channel_id=1, source_target_pairs={{0,13},{1,12},{2,15},{3,14},{4,1},{5,0},{6,3},{7,2},{8,5},{9,4},{1... | collective-permute-start | bytes 540680 | tf_op jit(solution)/shard_map/ppermute | solution.py:576
  41.6 4.6 %collective-permute-done.4.refs_5_ = bf16[32,2816]{1,0:T(8,128)(2,1)S(1)} collective-permute-done((bf16[32,2816]{1,0:T(8,128)(2,1)S(1)}, bf16[32,2816]{1,0:T(8,128)(2,1)S(1)}, u32[]{:S(2)}, u32[]{:S(2)}) %collective-permute-start.4) | collective-permute-done | bytes 180256 | tf_op jit(solution)/shard_map/ppermute | solution.py:576
  46.2 1.7 collective-permute-done.5.refs_6_
  47.9 2.9 %collective-permute-start.10 = (bf16[32,2816]{1,0:T(8,128)(2,1)S(1)}, bf16[32,2816]{1,0:T(8,128)(2,1)S(1)}, u32[]{:S(2)}, u32[]{:S(2)}) collective-permute-start(bf16[32,2816]{1,0:T(8,128)(2,1)S(1)} %get-tuple-element.46), channel_id=1, source_target_pairs={{0,15},{1,14},{2,1},{3,0},{4,3},{5,2},{6,5},{7,4},{8,7},{9,6},{10,... | collective-permute-start | bytes 540680 | tf_op jit(solution)/shard_map/ppermute | solution.py:576
  50.8 4.3 %collective-permute-done.9.refs_10_ = bf16[32,2816]{1,0:T(8,128)(2,1)S(1)} collective-permute-done((bf16[32,2816]{1,0:T(8,128)(2,1)S(1)}, bf16[32,2816]{1,0:T(8,128)(2,1)S(1)}, u32[]{:S(2)}, u32[]{:S(2)}) %collective-permute-start.9) | collective-permute-done | bytes 180256 | tf_op jit(solution)/shard_map/ppermute | solution.py:576
  56.0 8.6 %collective-permute-done.7.refs_8_ = bf16[160,2816]{1,0:T(8,128)(2,1)S(1)} collective-permute-done((bf16[160,2816]{1,0:T(8,128)(2,1)S(1)}, bf16[160,2816]{1,0:T(8,128)(2,1)S(1)}, u32[]{:S(2)}, u32[]{:S(2)}) %collective-permute-start.7) | collective-permute-done | bytes 901152 | tf_op jit(solution)/shard_map/ppermute | solution.py:581
  65.5 4.8 %all-to-all-start = ((bf16[16,16,2816]{2,1,0:T(8,128)(2,1)}), bf16[16,16,2816]{2,1,0:T(8,128)(2,1)S(1)}, u32[]{:S(2)}, u32[]{:S(2)}) async-start(bf16[16,16,2816]{2,1,0:T(8,128)(2,1)} %bitcast.21), calls=%async_computation | async-start | bytes 2883584 | tf_op jit(solution)/shard_map/all_to_all | solution.py:585
  71.0 7.7 %over.1 = (bf16[512,2048]{1,0:T(8,128)(2,1)}, bf16[512,1536]{1,0:T(8,128)(2,1)}, bf16[768,2048]{1,0:T(8,128)(2,1)}) custom-call(s32[128]{0:T(128)S(1)} %bitcast.24, bf16[64,2816]{1,0:T(8,128)(2,1)S(1)} %get-tuple-element.40.refs_0_, bf16[64,2816]{1,0:T(8,128)(2,1)S(1)} %collective-permute-done.refs_1_, bf16[64,2816]{1,0:T(8,128)(2,1)S(1)} %collective-permute-done.2.refs_2_, ...), custom_call_target="tpu_custom_call" | custom-call | flops 6442450944 | bytes 17825792 | tf_op jit(solution)/shard_map/over/pallas_call | solution.py:309
  78.7 8.2 %weight_over.1.part_ref = f32[2048,1536]{1,0:T(8,128)} custom-call(s32[16]{0:T(128)S(1)} %dynamic-slice_bitcast_fusion.block_ref, s32[128]{0:T(128)S(1)} %bitcast.25, bf16[512,2048]{1,0:T(8,128)(2,1)} %get-tuple-element.55.x_ref, bf16[512,1536]{1,0:T(8,128)(2,1)} %get-tuple-element.56.delta_ref), custom_call_target="tpu_custom_call" | custom-call | flops 3221225472 | bytes 17825792 | tf_op jit(solution)/shard_map/weight_over/pallas_call | solution.py:448
  86.9 14.7 %all-to-all-done = bf16[16,16,2816]{2,1,0:T(8,128)(2,1)S(1)} async-done(((bf16[16,16,2816]{2,1,0:T(8,128)(2,1)}), bf16[16,16,2816]{2,1,0:T(8,128)(2,1)S(1)}, u32[]{:S(2)}, u32[]{:S(2)}) %all-to-all-start) | async-done | bytes 1441824 | tf_op jit(solution)/shard_map/all_to_all | solution.py:585
  101.6 7.5 %direct.1 = (bf16[256,1536]{1,0:T(8,128)(2,1)}, bf16[768,2048]{1,0:T(8,128)(2,1)}) custom-call(bf16[256,2816]{1,0:T(8,128)(2,1)S(1)} %bitcast.18, bf16[1,2048,768]{2,1,0:T(8,128)(2,1)} %all_wg_ref.1, bf16[1,2048,768]{2,1,0:T(8,128)(2,1)} %all_wu_ref.1, bf16[768,2048]{1,0:T(8,128)(2,1)} %get-tuple-element.58.old_ref), custom_call_target="tpu_custom_call", output_to_operand_aliasing={{1}: (3, {})} | custom-call | flops 3221225472 | bytes 10485760 | tf_op jit(solution)/shard_map/direct/pallas_call | solution.py:397
  109.1 7.3 %all-to-all-start.1 = ((bf16[16,48,2048]{2,1,0:T(8,128)(2,1)}), bf16[16,48,2048]{2,1,0:T(8,128)(2,1)}, u32[]{:S(2)}, u32[]{:S(2)}) async-start(bf16[16,48,2048]{2,1,0:T(8,128)(2,1)} %bitcast.27), calls=%async_computation.1 | async-start | bytes 6291456 | tf_op jit(solution)/shard_map/all_to_all | solution.py:594
  116.4 6.2 %weight_send.1 = bf16[1024,1536]{1,0:T(8,128)(2,1)S(1)} custom-call(s32[16]{0:T(128)S(1)} %dynamic-slice_bitcast_fusion.block_ref, bf16[256,2816]{1,0:T(8,128)(2,1)S(1)} %bitcast.19, bf16[256,1536]{1,0:T(8,128)(2,1)} %get-tuple-element.59.delta_ref, f32[2048,1536]{1,0:T(8,128)} %weight_over.1.part_ref), custom_call_target="tpu_custom_call" | custom-call | flops 805306368 | bytes 11534336 | tf_op jit(solution)/shard_map/weight_send/pallas_call | solution.py:490
  122.7 5.6 %collective-permute-done.11.came_ref = bf16[1024,1536]{1,0:T(8,128)(2,1)S(1)} collective-permute-done((bf16[1024,1536]{1,0:T(8,128)(2,1)S(1)}, bf16[1024,1536]{1,0:T(8,128)(2,1)S(1)}, u32[]{:S(2)}, u32[]{:S(2)}) %collective-permute-start.11) | collective-permute-done | bytes 3145760 | tf_op jit(solution)/shard_map/ppermute | solution.py:597
  128.3 7.1 %weight_keep.1 = (f32[128,1536]{1,0:T(8,128)S(1)}, f32[128,1536]{1,0:T(8,128)S(1)}, bf16[128,1536]{1,0:T(8,128)(2,1)}, bf16[128,1536]{1,0:T(8,128)(2,1)S(1)}, bf...) custom-call(s32[16]{0:T(128)S(1)} %dynamic-slice_bitcast_fusion.bloc, ...), custom_call_target="tpu_custom_call" | custom-call | flops 805306368 | bytes 14680064 | tf_op jit(solution)/shard_map/weight_keep/pallas_call | solution.py:525
  135.4 2.3 %collective-permute-start.12 = (bf16[128,1536]{1,0:T(8,128)(2,1)S(1)}, bf16[128,1536]{1,0:T(8,128)(2,1)S(1)}, u32[]{:S(2)}, u32[]{:S(2)}) collective-permute-start(bf16[128,1536]{1,0:T(8,128)(2,1)S(1)} %get-tuple-element.62), channel_id=1, source_target_pairs={{0,128},{16,144},{32,160},{48,176},{64,192},{80,208},{96,224},{112... | collective-permute-start | bytes 1179656 | tf_op jit(solution)/shard_map/ppermute | solution.py:602
  137.7 2.0 %collective-permute-start.14 = (bf16[128,1536]{1,0:T(8,128)(2,1)S(1)}, bf16[128,1536]{1,0:T(8,128)(2,1)S(1)}, u32[]{:S(2)}, u32[]{:S(2)}) collective-permute-start(bf16[128,1536]{1,0:T(8,128)(2,1)S(1)} %get-tuple-element.64), channel_id=1, source_target_pairs={{0,192},{16,208},{32,224},{48,240},{64,0},{80,16},{96,32},{112,48}... | collective-permute-start | bytes 1179656 | tf_op jit(solution)/shard_map/ppermute | solution.py:602
  139.7 9.2 %collective-permute-done.12 = bf16[128,1536]{1,0:T(8,128)(2,1)S(1)} collective-permute-done((bf16[128,1536]{1,0:T(8,128)(2,1)S(1)}, bf16[128,1536]{1,0:T(8,128)(2,1)S(1)}, u32[]{:S(2)}, u32[]{:S(2)}) %collective-permute-start.12) | collective-permute-done | bytes 393248 | tf_op jit(solution)/shard_map/ppermute | solution.py:602
  148.9 7.7 %collective-permute-done.13 = bf16[128,1536]{1,0:T(8,128)(2,1)S(1)} collective-permute-done((bf16[128,1536]{1,0:T(8,128)(2,1)S(1)}, bf16[128,1536]{1,0:T(8,128)(2,1)S(1)}, u32[]{:S(2)}, u32[]{:S(2)}) %collective-permute-start.13) | collective-permute-done | bytes 393248 | tf_op jit(solution)/shard_map/ppermute | solution.py:602
  156.8 1.5 collective-permute-start.15
  158.3 2.1 %collective-permute-start.16 = (bf16[128,1536]{1,0:T(8,128)(2,1)}, bf16[128,1536]{1,0:T(8,128)(2,1)S(1)}, u32[]{:S(2)}, u32[]{:S(2)}) collective-permute-start(bf16[128,1536]{1,0:T(8,128)(2,1)} %get-tuple-element.69), channel_id=1, source_target_pairs={{0,128},{16,144},{32,160},{48,176},{64,192},{80,208},{96,224},{112... | collective-permute-start | bytes 1179656 | tf_op jit(solution)/shard_map/ppermute | solution.py:602
  160.4 2.0 %collective-permute-start.18 = (bf16[128,1536]{1,0:T(8,128)(2,1)S(1)}, bf16[128,1536]{1,0:T(8,128)(2,1)S(1)}, u32[]{:S(2)}, u32[]{:S(2)}) collective-permute-start(bf16[128,1536]{1,0:T(8,128)(2,1)S(1)} %get-tuple-element.71), channel_id=1, source_target_pairs={{0,192},{16,208},{32,224},{48,240},{64,0},{80,16},{96,32},{112,48}... | collective-permute-start | bytes 1179656 | tf_op jit(solution)/shard_map/ppermute | solution.py:602
  162.4 23.5 %all-to-all-done.1 = bf16[16,48,2048]{2,1,0:T(8,128)(2,1)} async-done(((bf16[16,48,2048]{2,1,0:T(8,128)(2,1)}), bf16[16,48,2048]{2,1,0:T(8,128)(2,1)}, u32[]{:S(2)}, u32[]{:S(2)}) %all-to-all-start.1) | async-done | bytes 3145760 | tf_op jit(solution)/shard_map/all_to_all | solution.py:594
  186.0 3.3 %convolution_convert_fusion = bf16[128,2048]{1,0:T(8,128)(2,1)} fusion(bf16[128,768]{1,0:T(8,128)(2,1)S(1)} %copy-done.2, bf16[768,2048]{1,0:T(8,128)(2,1)} %bitcast.8), kind=kOutput, calls=%fused_computation | convolution fusion | flops 402915328 | bytes 3866624 | tf_op jit(solution)/shard_map/dot_general | solution.py:610
  (44 shorter events, 8.1 us)
Async XLA Ops:
  2.4 0.7 copy-start.1
  5.1 60.4 %copy-start = (bf16[256,2816]{1,0:T(8,128)(2,1)}, bf16[256,2816]{1,0:T(8,128)(2,1)S(1)}, u32[]{:S(2)}) copy-start(bf16[256,2816]{1,0:T(8,128)(2,1)S(1)} %get-tuple-element.47) | copy-start | bytes 4325380
  5.1 13.6 %collective-permute-start.2 = (bf16[64,2816]{1,0:T(8,128)(2,1)S(1)}, bf16[64,2816]{1,0:T(8,128)(2,1)S(1)}, u32[]{:S(2)}, u32[]{:S(2)}) collective-permute-start(bf16[64,2816]{1,0:T(8,128)(2,1)S(1)} %get-tuple-element.40.refs_0_), channel_id=1, source_target_pairs={{0,14},{1,15},{2,0},{3,1},{4,2},{5,3},{6,4},{7,5},{8,6},{9,7},{10,... | collective-permute-start | bytes 1081352 | tf_op jit(solution)/shard_map/ppermute | solution.py:573
  11.0 11.4 %collective-permute-start = (bf16[64,2816]{1,0:T(8,128)(2,1)S(1)}, bf16[64,2816]{1,0:T(8,128)(2,1)S(1)}, u32[]{:S(2)}, u32[]{:S(2)}) collective-permute-start(bf16[64,2816]{1,0:T(8,128)(2,1)S(1)} %get-tuple-element.40.refs_0_), channel_id=1, source_target_pairs={{0,2},{1,3},{2,4},{3,5},{4,6},{5,7},{6,8},{7,9},{8,10},{9,11},{10,... | collective-permute-start | bytes 1081352 | tf_op jit(solution)/shard_map/ppermute | solution.py:572
  18.7 10.5 %collective-permute-start.3 = (bf16[64,2816]{1,0:T(8,128)(2,1)S(1)}, bf16[64,2816]{1,0:T(8,128)(2,1)S(1)}, u32[]{:S(2)}, u32[]{:S(2)}) collective-permute-start(bf16[64,2816]{1,0:T(8,128)(2,1)S(1)} %collective-permute-done.2.refs_2_), channel_id=1, source_target_pairs={{0,14},{1,15},{2,0},{3,1},{4,2},{5,3},{6,4},{7,5},{8,6},{9,7},{10,... | collective-permute-start | bytes 1081352 | tf_op jit(solution)/shard_map/ppermute | solution.py:573
  22.4 10.2 %collective-permute-start.1 = (bf16[64,2816]{1,0:T(8,128)(2,1)S(1)}, bf16[64,2816]{1,0:T(8,128)(2,1)S(1)}, u32[]{:S(2)}, u32[]{:S(2)}) collective-permute-start(bf16[64,2816]{1,0:T(8,128)(2,1)S(1)} %collective-permute-done.refs_1_), channel_id=1, source_target_pairs={{0,2},{1,3},{2,4},{3,5},{4,6},{5,7},{6,8},{7,9},{8,10},{9,11},{10,... | collective-permute-start | bytes 1081352 | tf_op jit(solution)/shard_map/ppermute | solution.py:572
  33.2 31.3 %collective-permute-start.7 = (bf16[160,2816]{1,0:T(8,128)(2,1)S(1)}, bf16[160,2816]{1,0:T(8,128)(2,1)S(1)}, u32[]{:S(2)}, u32[]{:S(2)}) collective-permute-start(bf16[160,2816]{1,0:T(8,128)(2,1)S(1)} %choose.1), channel_id=1, source_target_pairs={{0,1},{1,0},{2,3},{3,2},{4,5},{5,4},{6,7},{7,6},{8,9},{9,8},{10,11... | collective-permute-start | bytes 2703368 | tf_op jit(solution)/shard_map/ppermute | solution.py:581
  34.7 11.4 %collective-permute-start.4 = (bf16[32,2816]{1,0:T(8,128)(2,1)S(1)}, bf16[32,2816]{1,0:T(8,128)(2,1)S(1)}, u32[]{:S(2)}, u32[]{:S(2)}) collective-permute-start(bf16[32,2816]{1,0:T(8,128)(2,1)S(1)} %get-tuple-element.41), channel_id=1, source_target_pairs={{0,4},{1,5},{2,6},{3,7},{4,8},{5,9},{6,10},{7,11},{8,12},{9,13},{1... | collective-permute-start | bytes 540680 | tf_op jit(solution)/shard_map/ppermute | solution.py:576
  34.8 13.0 %collective-permute-start.5 = (bf16[32,2816]{1,0:T(8,128)(2,1)S(1)}, bf16[32,2816]{1,0:T(8,128)(2,1)S(1)}, u32[]{:S(2)}, u32[]{:S(2)}) collective-permute-start(bf16[32,2816]{1,0:T(8,128)(2,1)S(1)} %get-tuple-element.42), channel_id=1, source_target_pairs={{0,2},{1,3},{2,4},{3,5},{4,6},{5,7},{6,8},{7,9},{8,10},{9,11},{10,... | collective-permute-start | bytes 540680 | tf_op jit(solution)/shard_map/ppermute | solution.py:576
  34.9 15.9 %collective-permute-start.6 = (bf16[32,2816]{1,0:T(8,128)(2,1)S(1)}, bf16[32,2816]{1,0:T(8,128)(2,1)S(1)}, u32[]{:S(2)}, u32[]{:S(2)}) collective-permute-start(bf16[32,2816]{1,0:T(8,128)(2,1)S(1)} %get-tuple-element.43), channel_id=1, source_target_pairs={{0,14},{1,15},{2,0},{3,1},{4,2},{5,3},{6,4},{7,5},{8,6},{9,7},{10,... | collective-permute-start | bytes 540680 | tf_op jit(solution)/shard_map/ppermute | solution.py:576
  38.2 12.6 %collective-permute-start.8 = (bf16[32,2816]{1,0:T(8,128)(2,1)S(1)}, bf16[32,2816]{1,0:T(8,128)(2,1)S(1)}, u32[]{:S(2)}, u32[]{:S(2)}) collective-permute-start(bf16[32,2816]{1,0:T(8,128)(2,1)S(1)} %get-tuple-element.44), channel_id=1, source_target_pairs={{0,13},{1,12},{2,15},{3,14},{4,1},{5,0},{6,3},{7,2},{8,5},{9,4},{1... | collective-permute-start | bytes 540680 | tf_op jit(solution)/shard_map/ppermute | solution.py:576
  46.2 24.8 %copy-start.4 = (bf16[32,2816]{1,0:T(8,128)(2,1)}, bf16[32,2816]{1,0:T(8,128)(2,1)S(1)}, u32[]{:S(2)}) copy-start(bf16[32,2816]{1,0:T(8,128)(2,1)S(1)} %collective-permute-done.4.refs_5_) | copy-start | bytes 540676
  46.2 9.0 %collective-permute-start.9 = (bf16[32,2816]{1,0:T(8,128)(2,1)S(1)}, bf16[32,2816]{1,0:T(8,128)(2,1)S(1)}, u32[]{:S(2)}, u32[]{:S(2)}) collective-permute-start(bf16[32,2816]{1,0:T(8,128)(2,1)S(1)} %get-tuple-element.45), channel_id=1, source_target_pairs={{0,3},{1,2},{2,5},{3,4},{4,7},{5,6},{6,9},{7,8},{8,11},{9,10},{10,... | collective-permute-start | bytes 540680 | tf_op jit(solution)/shard_map/ppermute | solution.py:576
  47.9 17.6 %copy-start.5 = (bf16[32,2816]{1,0:T(8,128)(2,1)}, bf16[32,2816]{1,0:T(8,128)(2,1)S(1)}, u32[]{:S(2)}) copy-start(bf16[32,2816]{1,0:T(8,128)(2,1)S(1)} %collective-permute-done.5.refs_6_) | copy-start | bytes 540676
  47.9 8.1 %collective-permute-start.10 = (bf16[32,2816]{1,0:T(8,128)(2,1)S(1)}, bf16[32,2816]{1,0:T(8,128)(2,1)S(1)}, u32[]{:S(2)}, u32[]{:S(2)}) collective-permute-start(bf16[32,2816]{1,0:T(8,128)(2,1)S(1)} %get-tuple-element.46), channel_id=1, source_target_pairs={{0,15},{1,14},{2,1},{3,0},{4,3},{5,2},{6,5},{7,4},{8,7},{9,6},{10,... | collective-permute-start | bytes 540680 | tf_op jit(solution)/shard_map/ppermute | solution.py:576
  50.8 14.7 %copy-start.6 = (bf16[32,2816]{1,0:T(8,128)(2,1)}, bf16[32,2816]{1,0:T(8,128)(2,1)S(1)}, u32[]{:S(2)}) copy-start(bf16[32,2816]{1,0:T(8,128)(2,1)S(1)} %collective-permute-done.6.refs_7_) | copy-start | bytes 540676
  50.8 14.7 %copy-start.7 = (bf16[32,2816]{1,0:T(8,128)(2,1)}, bf16[32,2816]{1,0:T(8,128)(2,1)S(1)}, u32[]{:S(2)}) copy-start(bf16[32,2816]{1,0:T(8,128)(2,1)S(1)} %collective-permute-done.8.refs_9_) | copy-start | bytes 540676
  55.1 10.3 %copy-start.8 = (bf16[32,2816]{1,0:T(8,128)(2,1)}, bf16[32,2816]{1,0:T(8,128)(2,1)S(1)}, u32[]{:S(2)}) copy-start(bf16[32,2816]{1,0:T(8,128)(2,1)S(1)} %collective-permute-done.9.refs_10_) | copy-start | bytes 540676
  56.0 9.5 %copy-start.9 = (bf16[32,2816]{1,0:T(8,128)(2,1)}, bf16[32,2816]{1,0:T(8,128)(2,1)S(1)}, u32[]{:S(2)}) copy-start(bf16[32,2816]{1,0:T(8,128)(2,1)S(1)} %collective-permute-done.10.refs_11_) | copy-start | bytes 540676
  64.5 0.9 copy-start.3
  65.5 36.1 %all-to-all-start = ((bf16[16,16,2816]{2,1,0:T(8,128)(2,1)}), bf16[16,16,2816]{2,1,0:T(8,128)(2,1)S(1)}, u32[]{:S(2)}, u32[]{:S(2)}) async-start(bf16[16,16,2816]{2,1,0:T(8,128)(2,1)} %bitcast.21), calls=%async_computation | async-start | bytes 2883584 | tf_op jit(solution)/shard_map/all_to_all | solution.py:585
  109.1 76.9 %all-to-all-start.1 = ((bf16[16,48,2048]{2,1,0:T(8,128)(2,1)}), bf16[16,48,2048]{2,1,0:T(8,128)(2,1)}, u32[]{:S(2)}, u32[]{:S(2)}) async-start(bf16[16,48,2048]{2,1,0:T(8,128)(2,1)} %bitcast.27), calls=%async_computation.1 | async-start | bytes 6291456 | tf_op jit(solution)/shard_map/all_to_all | solution.py:594
  122.5 63.4 %copy-start.2 = (bf16[128,768]{1,0:T(8,128)(2,1)S(1)}, bf16[128,768]{1,0:T(8,128)(2,1)}, u32[]{:S(2)}) copy-start(bf16[128,768]{1,0:T(8,128)(2,1)} %get-tuple-element.65) | copy-start | bytes 589828
  122.6 5.7 %collective-permute-start.11 = (bf16[1024,1536]{1,0:T(8,128)(2,1)S(1)}, bf16[1024,1536]{1,0:T(8,128)(2,1)S(1)}, u32[]{:S(2)}, u32[]{:S(2)}) collective-permute-start(bf16[1024,1536]{1,0:T(8,128)(2,1)S(1)} %weight_send.1), channel_id=1, source_target_pairs={{0,16},{16,0},{32,48},{48,32},{64,80},{80,64},{96,112},{112,96},{1... | collective-permute-start | bytes 9437192 | tf_op jit(solution)/shard_map/ppermute | solution.py:597
  135.4 13.5 %collective-permute-start.12 = (bf16[128,1536]{1,0:T(8,128)(2,1)S(1)}, bf16[128,1536]{1,0:T(8,128)(2,1)S(1)}, u32[]{:S(2)}, u32[]{:S(2)}) collective-permute-start(bf16[128,1536]{1,0:T(8,128)(2,1)S(1)} %get-tuple-element.62), channel_id=1, source_target_pairs={{0,128},{16,144},{32,160},{48,176},{64,192},{80,208},{96,224},{112... | collective-permute-start | bytes 1179656 | tf_op jit(solution)/shard_map/ppermute | solution.py:602
  137.7 18.9 %collective-permute-start.13 = (bf16[128,1536]{1,0:T(8,128)(2,1)S(1)}, bf16[128,1536]{1,0:T(8,128)(2,1)S(1)}, u32[]{:S(2)}, u32[]{:S(2)}) collective-permute-start(bf16[128,1536]{1,0:T(8,128)(2,1)S(1)} %get-tuple-element.63), channel_id=1, source_target_pairs={{0,64},{16,80},{32,96},{48,112},{64,128},{80,144},{96,160},{112,17... | collective-permute-start | bytes 1179656 | tf_op jit(solution)/shard_map/ppermute | solution.py:602
  137.7 18.9 %collective-permute-start.14 = (bf16[128,1536]{1,0:T(8,128)(2,1)S(1)}, bf16[128,1536]{1,0:T(8,128)(2,1)S(1)}, u32[]{:S(2)}, u32[]{:S(2)}) collective-permute-start(bf16[128,1536]{1,0:T(8,128)(2,1)S(1)} %get-tuple-element.64), channel_id=1, source_target_pairs={{0,192},{16,208},{32,224},{48,240},{64,0},{80,16},{96,32},{112,48}... | collective-permute-start | bytes 1179656 | tf_op jit(solution)/shard_map/ppermute | solution.py:602
  156.8 33.7 %collective-permute-start.15 = (bf16[128,1536]{1,0:T(8,128)(2,1)S(1)}, bf16[128,1536]{1,0:T(8,128)(2,1)S(1)}, u32[]{:S(2)}, u32[]{:S(2)}) collective-permute-start(bf16[128,1536]{1,0:T(8,128)(2,1)S(1)} %add_convert_fusion), channel_id=1, source_target_pairs={{0,32},{16,48},{32,0},{48,16},{64,96},{80,112},{96,64},{112,80},{1... | collective-permute-start | bytes 1179656 | tf_op jit(solution)/shard_map/ppermute | solution.py:607
  158.3 32.2 %collective-permute-start.16 = (bf16[128,1536]{1,0:T(8,128)(2,1)}, bf16[128,1536]{1,0:T(8,128)(2,1)S(1)}, u32[]{:S(2)}, u32[]{:S(2)}) collective-permute-start(bf16[128,1536]{1,0:T(8,128)(2,1)} %get-tuple-element.69), channel_id=1, source_target_pairs={{0,128},{16,144},{32,160},{48,176},{64,192},{80,208},{96,224},{112... | collective-permute-start | bytes 1179656 | tf_op jit(solution)/shard_map/ppermute | solution.py:602
  160.4 30.1 %collective-permute-start.17 = (bf16[128,1536]{1,0:T(8,128)(2,1)}, bf16[128,1536]{1,0:T(8,128)(2,1)S(1)}, u32[]{:S(2)}, u32[]{:S(2)}) collective-permute-start(bf16[128,1536]{1,0:T(8,128)(2,1)} %get-tuple-element.70), channel_id=1, source_target_pairs={{0,64},{16,80},{32,96},{48,112},{64,128},{80,144},{96,160},{112,17... | collective-permute-start | bytes 1179656 | tf_op jit(solution)/shard_map/ppermute | solution.py:602
  160.4 30.1 %collective-permute-start.18 = (bf16[128,1536]{1,0:T(8,128)(2,1)S(1)}, bf16[128,1536]{1,0:T(8,128)(2,1)S(1)}, u32[]{:S(2)}, u32[]{:S(2)}) collective-permute-start(bf16[128,1536]{1,0:T(8,128)(2,1)S(1)} %get-tuple-element.71), channel_id=1, source_target_pairs={{0,192},{16,208},{32,224},{48,240},{64,0},{80,16},{96,32},{112,48}... | collective-permute-start | bytes 1179656 | tf_op jit(solution)/shard_map/ppermute | solution.py:602
